TPU v7x, 32 devices: a whole 2x2x4 slice. The times are simulated.
32 devices in a mesh: dp: 8 (over z, y), ctx: 4 (over x, core).
Axes of the slice: x: 2, y: 2, z: 4, core: 2. Of those that a mesh axis runs over, the one named last changes fastest.
Arguments:
- student_queries: bfloat16 [8, 512, 2048], P('dp', 'ctx'), may hold values from -8 to 8
- student_keys: bfloat16 [8, 512, 512], P('dp', 'ctx'), may hold values from -8 to 8
- teacher_maps: bfloat16 [8, 16, 512, 512], P('dp', 'ctx'), may hold values from 0.049804688 to 5
- lengths: int32 [8], P('dp'), may hold values from 256 to 512
- hidden_in: bfloat16 [8, 512, 4096], P('dp', 'ctx'), may hold values from -6 to 6
- adapter_in: bfloat16 [8, 512, 128], P('dp', 'ctx'), may hold values from -6 to 6
- adapter_up: bfloat16 [2560, 64], replicated, may hold values from -0.75 to 0.75
Outputs:
- grad_down: float32 [4096, 128], P(('dp', 'ctx'))
- grad_up: float32 [2560, 64], P(('dp', 'ctx'))
All inputs are finite; a program needn't handle non-finite values.
Results may differ from a plain program's by a relative error of at most 0.0049.
Values may be sent and summed in bfloat16 or wider, within the bound.
No kernel may reach another device: no remote copies, remote signals or barrier semaphores. Data moves between devices by JAX's collectives and lax.ppermute only.
A program may use at most 64 MiB of HBM per device.

v0:
```python
import math

import jax
import jax.numpy as jnp
from jax import lax
from jax.sharding import PartitionSpec as P

DH = 128
H = 16
KV = 4
R = 64


def attend_backward(queries, keys_here, teacher, length):
    seq_len = queries.shape[0]
    heads_here = queries.shape[1]
    block_rows = min(512, seq_len)
    score_scale = 1.0 / math.sqrt(DH)
    key_pos = jnp.arange(seq_len, dtype=jnp.int32)

    def one_block(dk_accum, block_idx):
        row_start = block_idx * block_rows
        query_blk = lax.dynamic_slice_in_dim(queries, row_start, block_rows, 0)
        teach_blk = lax.dynamic_slice_in_dim(teacher, row_start, block_rows, 1).astype(jnp.float32)
        row_pos = row_start + jnp.arange(block_rows, dtype=jnp.int32)
        visible = (key_pos[None, :] <= row_pos[:, None]) & (key_pos[None, :] < length)
        scores = (
            jnp.einsum("ihd,jhd->hij", query_blk, keys_here, preferred_element_type=jnp.float32)
            * score_scale
        )
        scores = jnp.where(visible[None], scores, -jnp.inf)
        row_peak = jnp.max(scores, axis=2, keepdims=True)
        exp_scores = jnp.exp(scores - row_peak)
        student = exp_scores / jnp.sum(exp_scores, axis=2, keepdims=True)
        masked_teacher = jnp.where(visible[None], teach_blk, 0.0)
        target = masked_teacher / jnp.sum(masked_teacher, axis=2, keepdims=True)
        weight_row = jnp.where(row_pos < length, 1.0 / H, 0.0)
        grad_scores = ((student - target) * weight_row[None, :, None]).astype(jnp.bfloat16)
        dq_blk = jnp.einsum(
            "hij,jhd->ihd", grad_scores, keys_here, preferred_element_type=jnp.float32
        )
        dq_blk = (dq_blk * score_scale).astype(jnp.bfloat16)
        dk_accum = dk_accum + jnp.einsum(
            "hij,ihd->jhd", grad_scores, query_blk, preferred_element_type=jnp.float32
        )
        return (dk_accum, dq_blk)

    dk_total, dq_blocks = lax.scan(
        one_block,
        jnp.zeros((seq_len, heads_here, DH), jnp.float32),
        jnp.arange(seq_len // block_rows, dtype=jnp.int32),
    )
    return (
        dq_blocks.reshape(seq_len, heads_here, DH),
        (dk_total * score_scale).astype(jnp.bfloat16),
    )


def down_terms(hidden_cols, lowered):
    return lax.dot_general(
        hidden_cols, lowered, (((0,), (0,)), ((), ())), preferred_element_type=jnp.float32
    )


def up_terms(grad_cols, anchor_index, adapter_loc, q_width):
    both_halves = lax.dot_general(
        grad_cols, adapter_loc, (((0,), (0,)), ((), ())), preferred_element_type=jnp.float32
    )
    return jnp.where((anchor_index < q_width)[:, None], both_halves[:, :R], both_halves[:, R:])


def body(student_queries, student_keys, teacher_maps, lengths, hidden_in, adapter_in, adapter_up):
    tok_rows = student_queries.shape[1]
    group_size = H // KV
    length = lengths[0]
    queries = student_queries[0].reshape(tok_rows, H, DH)
    keys_loc = student_keys[0].reshape(tok_rows, KV, DH)
    teacher = teacher_maps[0]
    keys_wide = jnp.repeat(keys_loc, group_size, axis=1)
    q_heads, k_heads = (
        lax.all_to_all(queries, "ctx", split_axis=1, concat_axis=0, tiled=True),
        lax.all_to_all(keys_wide, "ctx", split_axis=1, concat_axis=0, tiled=True),
    )
    dq_heads, dk_heads = attend_backward(q_heads, k_heads, teacher, length)
    grad_q, grad_kwide = (
        lax.all_to_all(dq_heads, "ctx", split_axis=0, concat_axis=1, tiled=True),
        lax.all_to_all(dk_heads, "ctx", split_axis=0, concat_axis=1, tiled=True),
    )
    grad_k = jnp.sum(grad_kwide.astype(jnp.float32).reshape(tok_rows, KV, group_size, DH), axis=2)
    grad_k = grad_k.astype(jnp.bfloat16)
    q_width = H * DH
    grad_qflat = grad_q.reshape(tok_rows, q_width)
    grad_kflat = grad_k.reshape(tok_rows, KV * DH)
    low_q = jnp.dot(grad_qflat, adapter_up[:q_width], preferred_element_type=jnp.float32)
    low_k = jnp.dot(grad_kflat, adapter_up[q_width:], preferred_element_type=jnp.float32)
    lowered = jnp.concatenate([low_q, low_k], axis=1).astype(jnp.bfloat16)
    grad_both = jnp.concatenate([grad_qflat, grad_kflat], axis=1)
    hidden = hidden_in[0]
    adapter_loc = adapter_in[0]
    anchor_index = jnp.arange(grad_both.shape[1], dtype=jnp.int32)
    grad_down = lax.psum_scatter(
        down_terms(hidden, lowered), ("dp", "ctx"), scatter_dimension=0, tiled=True
    )
    grad_up = lax.psum_scatter(
        up_terms(grad_both, anchor_index, adapter_loc, q_width),
        ("dp", "ctx"),
        scatter_dimension=0,
        tiled=True,
    )
    return (grad_down, grad_up)


def solution(mesh):
    placed = (
        P("dp", "ctx", None),
        P("dp", "ctx", None),
        P("dp", "ctx", None, None),
        P("dp"),
        P("dp", "ctx", None),
        P("dp", "ctx", None),
        P(),
    )
    return jax.shard_map(
        body,
        mesh=mesh,
        in_specs=placed,
        out_specs=(P(("dp", "ctx"), None), P(("dp", "ctx"), None)),
        check_vma=False,
    )
```

profile of v0, /device:TPU:0, one launch (start us, length us, event | category | flops | bytes accessed | tf_op | source)
XLA Modules:
  0.0 364.9 jit_solution(8015521657462655842)
XLA Ops:
  7.2 1.1 reshape_squeeze.7
  9.2 4.2 %all-to-all-start.1 = ((bf16[128,16,128]{2,0,1:T(8,128)(2,1)}), bf16[128,16,128]{2,0,1:T(8,128)(2,1)}, u32[]{:S(2)}, u32[]{:S(2)}) async-start(bf16[128,16,128]{2,0,1:T(8,128)(2,1)} %bitcast.6), calls=%async_computation.1 | async-start | bytes 1048576 | tf_op jit(solution)/shard_map/all_to_all | solution.py:82
  14.1 2.1 copy.41
  16.2 6.7 %all-to-all-done.1 = bf16[128,16,128]{2,0,1:T(8,128)(2,1)} async-done(((bf16[128,16,128]{2,0,1:T(8,128)(2,1)}), bf16[128,16,128]{2,0,1:T(8,128)(2,1)}, u32[]{:S(2)}, u32[]{:S(2)}) %all-to-all-start.1) | async-done | bytes 524320 | tf_op jit(solution)/shard_map/all_to_all | solution.py:82
  22.9 4.1 %all-to-all-start = ((bf16[128,16,128]{0,2,1:T(8,128)(2,1)}), bf16[128,16,128]{0,2,1:T(8,128)(2,1)}, u32[]{:S(2)}, u32[]{:S(2)}) async-start(bf16[128,16,128]{0,2,1:T(8,128)(2,1)} %bitcast.60), calls=%async_computation | async-start | bytes 1048576 | tf_op jit(solution)/shard_map/all_to_all | solution.py:81
  27.1 2.4 copy.46
  30.7 5.2 %all-to-all-done = bf16[128,16,128]{0,2,1:T(8,128)(2,1)} async-done(((bf16[128,16,128]{0,2,1:T(8,128)(2,1)}), bf16[128,16,128]{0,2,1:T(8,128)(2,1)}, u32[]{:S(2)}, u32[]{:S(2)}) %all-to-all-start) | async-done | bytes 524320 | tf_op jit(solution)/shard_map/all_to_all | solution.py:81
  35.9 1.3 copy.43
  37.3 4.0 %fusion.1 = f32[4,512,512]{1,2,0:T(8,128)} fusion(pred[512,512]{0,1:T(8,128)(4,1)S(1)} %fusion.20, bf16[512,4,128]{2,0,1:T(8,128)(2,1)S(1)} %bitcast.62, bf16[512,4,128]{2,0,1:T(8,128)(2,1)S(1)} %bitcast.57), kind=kOutput, calls=%fused_computation.1 | convolution fusion | flops 271586304 | bytes 5505024 | tf_op jit(solution)/shard_map/while/body/eval_jaxpr/div | solution.py:34
  41.3 3.5 subtract_exponential_fusion
  44.8 7.0 %fusion.7 = bf16[4,512,512]{1,2,0:T(8,128)(2,1)S(1)} fusion(f32[4,512,512]{1,2,0:T(8,128)} %subtract_exponential_fusion, f32[4,512,512]{1,2,0:T(8,128)} %fusion.1, bf16[1,4,512,512]{2,3,1,0:T(8,128)(2,1)} %copy.46, f32[512]{0:T(512)S(1)} %broadcast_select_fusion, pred[512,512]{0,1:T(8,128)(4,1)S(1)} %fusion.20), kind=kOutput, calls=%fused_computation.11 | output fusion | flops 9439743 | bytes 12847104 | tf_op jit(solution)/shard_map/while/body/eval_jaxpr/div | solution.py:36
  53.1 1.2 copy.48
  54.3 3.5 all-to-all-start.2
  57.8 2.3 fusion.17
  60.1 1.2 copy.51
  61.3 5.3 %all-to-all-done.2 = bf16[512,4,128]{2,1,0:T(4,128)(2,1)S(1)} async-done(((bf16[512,4,128]{2,1,0:T(4,128)(2,1)}), bf16[512,4,128]{2,1,0:T(4,128)(2,1)S(1)}, u32[]{:S(2)}, u32[]{:S(2)}) %all-to-all-start.2) | async-done | bytes 524320 | tf_op jit(solution)/shard_map/all_to_all | solution.py:86
  66.6 3.5 all-to-all-start.3
  70.5 8.3 %all-to-all-done.3 = bf16[512,4,128]{2,1,0:T(4,128)(2,1)S(1)} async-done(((bf16[512,4,128]{2,1,0:T(4,128)(2,1)}), bf16[512,4,128]{2,1,0:T(4,128)(2,1)S(1)}, u32[]{:S(2)}, u32[]{:S(2)}) %all-to-all-start.3) | async-done | bytes 524320 | tf_op jit(solution)/shard_map/all_to_all | solution.py:87
  80.1 1.5 copy.56
  82.0 1.8 convolution_bitcast_fusion
  83.8 136.3 %reduce-scatter.7.cloned.1.call-done = f32[80,64]{1,0:T(8,128)} async-done(((f32[2560,64]{1,0:T(8,128)}), f32[80,64]{1,0:T(8,128)}) %reduce-scatter.7.cloned.1.call-update) | async-done | bytes 20496
  220.1 1.5 copy.57
  221.6 134.9 %reduce-scatter.5.cloned.1.call-done = f32[128,128]{0,1:T(8,128)} async-done(((f32[4096,128]{0,1:T(8,128)}), f32[128,128]{0,1:T(8,128)}) %reduce-scatter.5.cloned.1.call-update) | async-done | bytes 65552 | tf_op jit(solution)/shard_map/reduce_scatter | solution.py:101
  356.5 1.6 copy.53
  (30 shorter events, 5.6 us)
Async XLA Ops:
  7.2 74.9 %copy-start = (bf16[1,128,4096]{2,1,0:T(8,128)(2,1)S(1)}, bf16[1,128,4096]{2,1,0:T(8,128)(2,1)}, u32[]{:S(2)}) copy-start(bf16[1,128,4096]{2,1,0:T(8,128)(2,1)} %param.11) | copy-start | bytes 3145732
  7.2 19.9 %copy-start.2 = (bf16[1,4,512,512]{3,2,1,0:T(8,128)(2,1)S(1)}, bf16[1,4,512,512]{3,2,1,0:T(8,128)(2,1)}, u32[]{:S(2)}) copy-start(bf16[1,4,512,512]{3,2,1,0:T(8,128)(2,1)} %param.9) | copy-start | bytes 6291460
  9.2 13.7 %all-to-all-start.1 = ((bf16[128,16,128]{2,0,1:T(8,128)(2,1)}), bf16[128,16,128]{2,0,1:T(8,128)(2,1)}, u32[]{:S(2)}, u32[]{:S(2)}) async-start(bf16[128,16,128]{2,0,1:T(8,128)(2,1)} %bitcast.6), calls=%async_computation.1 | async-start | bytes 1048576 | tf_op jit(solution)/shard_map/all_to_all | solution.py:82
  22.9 13.0 %all-to-all-start = ((bf16[128,16,128]{0,2,1:T(8,128)(2,1)}), bf16[128,16,128]{0,2,1:T(8,128)(2,1)}, u32[]{:S(2)}, u32[]{:S(2)}) async-start(bf16[128,16,128]{0,2,1:T(8,128)(2,1)} %bitcast.60), calls=%async_computation | async-start | bytes 1048576 | tf_op jit(solution)/shard_map/all_to_all | solution.py:81
  51.7 1.4 copy-start.1
  54.3 12.3 %all-to-all-start.2 = ((bf16[512,4,128]{2,1,0:T(4,128)(2,1)}), bf16[512,4,128]{2,1,0:T(4,128)(2,1)S(1)}, u32[]{:S(2)}, u32[]{:S(2)}) async-start(bf16[512,4,128]{2,1,0:T(4,128)(2,1)} %copy.48), calls=%async_computation.2 | async-start | bytes 1048576 | tf_op jit(solution)/shard_map/all_to_all | solution.py:86
  57.8 21.8 %copy-start.4 = (bf16[1,128,128]{2,1,0:T(8,128)(2,1)S(1)}, bf16[1,128,128]{2,1,0:T(8,128)(2,1)}, u32[]{:S(2)}) copy-start(bf16[1,128,128]{2,1,0:T(8,128)(2,1)} %param.12) | copy-start | bytes 98308
  66.6 12.3 %all-to-all-start.3 = ((bf16[512,4,128]{2,1,0:T(4,128)(2,1)}), bf16[512,4,128]{2,1,0:T(4,128)(2,1)S(1)}, u32[]{:S(2)}, u32[]{:S(2)}) async-start(bf16[512,4,128]{2,1,0:T(4,128)(2,1)} %copy.51), calls=%async_computation.3 | async-start | bytes 1048576 | tf_op jit(solution)/shard_map/all_to_all | solution.py:87
  70.0 150.1 %reduce-scatter.7.cloned.1.call-start = ((), (), s32[]{:S(2)}) async-start(), calls=%async_computation.7 | async-start | bytes 1351680
  70.5 11.2 %copy-start.3 = (bf16[2560,64]{0,1:T(8,128)(2,1)S(1)}, bf16[2560,64]{0,1:T(8,128)(2,1)}, u32[]{:S(2)}) copy-start(bf16[2560,64]{0,1:T(8,128)(2,1)} %param.13) | copy-start | bytes 983044
  81.6 274.9 %reduce-scatter.5.cloned.1.call-start = ((), (), s32[]{:S(2)}) async-start(), calls=%async_computation.6 | async-start | bytes 2162688 | tf_op jit(solution)/shard_map/reduce_scatter | solution.py:101
Sparse Core Ops, SparseCore 0:
  81.7 138.3 reduce-scatter.6
  222.4 134.0 reduce-scatter.4
where the time goes:
time: 366 us; the launch traced here: 365 us
  waiting for transfers between devices  297 us (81%)
  local copies, waits for them, and re-layouts  16.8 us (5%)
  starting transfers between devices  15.4 us (4%)
  between operations  14.9 us (4%)
  matrix products  13.3 us (4%)
  other arithmetic  7.86 us (2%)
    unnamed x3, waiting for transfers between devices  136 us
    reduce_scatter x1, waiting for transfers between devices, body(): lax.psum_scatter(down_terms(hidden, lowered), ('dp', 'ctx'), scatter_dime...  135 us
    unnamed x15, local copies, waits for them, and re-layouts  9.45 us
    all_to_all x1, waiting for transfers between devices, body(): lax.all_to_all(dk_heads, 'ctx', split_axis=0, concat_axis=1, tiled=True)  8.34 us
  transfers between devices with their start and end apart: 6, of which 6 were waited for; matrix products, arithmetic and copies ran while one was open for 4% of the time, Pallas kernels for 0%

commit v1 on v0

v1 whole, which is shorter than its diff:
```python
import functools
import math

import jax
import jax.numpy as jnp
import numpy as np
from jax import lax
from jax.experimental import pallas as pl
from jax.experimental.pallas import tpu as pltpu
from jax.sharding import PartitionSpec as P

NT = (((1,), (1,)), ((), ()))
TN = (((0,), (0,)), ((), ()))


def dot32(a, b, dims=(((1,), (0,)), ((), ()))):
    return lax.dot_general(a, b, dims, preferred_element_type=jnp.float32)


def owner_tables(C, Dp, W, Wk, DH, q_width, group_cols, rows_total, lane_block):
    rows_each = rows_total // (C * Dp)
    local = []
    for c in range(C):
        k_start = q_width + (c * W // group_cols) * DH
        local.append(np.concatenate([c * W + np.arange(W), k_start + np.arange(Wk)]))
    owner = [rows // rows_each for rows in local]
    most = max(int(np.sum(o % C == dst)) for o in owner for dst in range(C))
    slot = -(-most // 128) * 128
    pack = np.full((C, C, slot), -1, np.int32)
    land = np.full((C, C, slot), -1, np.int32)
    rows_of = {}
    for c in range(C):
        for dst in range(C):
            mine = np.nonzero(owner[c] % C == dst)[0]
            rows_of[c, dst] = mine
    for me in range(C):
        for s in range(C):
            mine = rows_of[me, me ^ s]
            pack[me, s, : len(mine)] = mine
            src = me ^ s
            sent = local[src][rows_of[src, me]]
            blk = sent // rows_each
            land[me, s, : len(sent)] = blk // C * lane_block + sent % rows_each
    return pack, land, slot, rows_each


def attend_kernel(C, tok, hq, kh, DH, H, R, scalars, *refs):
    q_in, k_in, a_in = refs[:C], refs[C : 2 * C], refs[2 * C : 3 * C]
    teacher, up_q, up_k, pack = refs[3 * C : 3 * C + 4]
    low_out, grad_out = refs[3 * C + 4 : 3 * C + 6]
    q_buf, k_buf, a_buf, dq_buf, dk_buf = refs[3 * C + 6 :]
    me, length = scalars[0], scalars[1]
    per_key = hq // kh
    scale = 1.0 / math.sqrt(DH)
    exp_scale = scale * math.log2(math.e)
    for s in range(C):
        row = pl.multiple_of(jnp.bitwise_xor(me, s) * tok, tok)
        for h in range(hq):
            q_buf[h, pl.ds(row, tok), :] = q_in[s][:, h * DH : (h + 1) * DH]
        k_buf[pl.ds(row, tok), :] = k_in[s][...]
        a_buf[pl.ds(row, tok), :] = a_in[s][...]
    dk_buf[...] = jnp.zeros_like(dk_buf)
    row_in = lax.broadcasted_iota(jnp.int32, (tok, 1), 0)
    col_in = lax.broadcasted_iota(jnp.int32, (tok, tok), 1)
    for p in range(C):
        start, ext = p * tok, (p + 1) * tok
        row_pos = row_in + start
        visible = (col_in + start) <= jnp.minimum(row_pos, length - 1)
        weight = jnp.where(row_pos < length, 1.0 / H, 0.0)
        for g in range(kh):
            keys = k_buf[:ext, g * DH : (g + 1) * DH]
            heads = range(g * per_key, (g + 1) * per_key)
            q_all = q_buf[g * per_key : (g + 1) * per_key, start:ext, :].reshape(per_key * tok, DH)
            scores = dot32(q_all, keys, NT)
            grads = []
            for n, h in enumerate(heads):
                sc = scores[n * tok : (n + 1) * tok]
                diag = jnp.where(visible, sc[:, start:], -1e30)
                sc = diag if p == 0 else jnp.concatenate([sc[:, :start], diag], axis=1)
                te_d = jnp.where(visible, teacher[h, start:ext, start:ext].astype(jnp.float32), 0.0)
                te = te_d if p == 0 else jnp.concatenate(
                    [teacher[h, start:ext, :start].astype(jnp.float32), te_d], axis=1
                )
                ex = jnp.exp2((sc - jnp.max(sc, axis=1, keepdims=True)) * exp_scale)
                w_s = weight / jnp.sum(ex, axis=1, keepdims=True)
                w_t = weight / jnp.sum(te, axis=1, keepdims=True)
                grads.append((ex * w_s - te * w_t).astype(jnp.bfloat16))
            grad = grads[0] if per_key == 1 else jnp.concatenate(grads, axis=0)
            dq = (dot32(grad, keys) * scale).astype(jnp.bfloat16)
            for n, h in enumerate(heads):
                dq_buf[start:ext, h * DH : (h + 1) * DH] = dq[n * tok : (n + 1) * tok]
            dk_buf[g * DH : (g + 1) * DH, :ext] += dot32(q_all, grad, TN)
    dq = dq_buf[...]
    dk = (dk_buf[...] * scale).astype(jnp.bfloat16)
    low_out[:R, :] = dot32(up_q[...], dq, NT).astype(low_out.dtype)
    low_out[R:, :] = dot32(up_k[...], dk).astype(low_out.dtype)
    a_q, a_k = a_buf[:, :R], a_buf[:, R:]
    grad_up = jnp.concatenate(
        [dot32(a_q, dq, TN).astype(jnp.bfloat16), dot32(a_k.T, dk, NT).astype(jnp.bfloat16)], axis=1
    )
    pick = lax.broadcasted_iota(jnp.int32, (grad_up.shape[1], pack.shape[1]), 0) == pack[...]
    pick = jnp.where(pick, 1.0, 0.0).astype(jnp.bfloat16)
    grad_out[...] = dot32(grad_up, pick).astype(grad_out.dtype)


def down_kernel(C, Dp, tok, R, rblk, scalars, *refs):
    low_a, low_b = refs[:2]
    hid = refs[2 : 2 + C]
    got = refs[2 + C : 2 + 2 * C]
    land, out = refs[2 + 2 * C :]
    me = scalars[0]
    acc = None
    low = (low_a[...].astype(jnp.float32) + low_b[...].astype(jnp.float32)).astype(jnp.bfloat16)
    blocks = [low[:, p * tok : (p + 1) * tok] for p in range(C)]
    for s in range(C):
        pos = jnp.bitwise_xor(me, s)
        part = blocks[0]
        for p in range(1, C):
            part = jnp.where(pos == p, blocks[p], part)
        term = dot32(part, hid[s][...])
        acc = term if acc is None else acc + term
    rows = jnp.concatenate([g[...] for g in got], axis=1)
    place = lax.broadcasted_iota(jnp.int32, (Dp * rblk, rows.shape[1]), 0) == land[...]
    place = jnp.where(place, 1.0, 0.0).astype(jnp.bfloat16)
    ups = dot32(rows, place, NT)
    for d in range(Dp):
        out[d, : 2 * R, :] = acc[:, d * rblk : (d + 1) * rblk].astype(out.dtype)
        out[d, 2 * R :, :] = ups[:, d * rblk : (d + 1) * rblk].astype(out.dtype)


def final_kernel(R, rows_each, got, down, up):
    total = jnp.sum(got[...].astype(jnp.float32), axis=0)
    down[...] = total[: 2 * R].T
    up[...] = total[2 * R :, :rows_each]


def solution(mesh):
    C, Dp = mesh.shape["ctx"], mesh.shape["dp"]

    def swap(x, s):
        return lax.ppermute(x, "ctx", [(i, i ^ s) for i in range(C)])

    def body(queries, keys, teacher, lengths, hidden, adapter, adapter_up):
        tok = queries.shape[1]
        hq = teacher.shape[1]
        S = teacher.shape[2]
        H = hq * C
        DH = queries.shape[2] // H
        KV = keys.shape[2] // DH
        R = adapter.shape[2] // 2
        D = hidden.shape[2]
        q_width = H * DH
        rows_total = adapter_up.shape[0]
        kh = max(1, KV // C)
        W, Wk = hq * DH, kh * DH
        rblk = D // (C * Dp)
        group_cols = (H // KV) * DH
        me = lax.axis_index("ctx")
        queries, keys, hidden, adapter = queries[0], keys[0], hidden[0], adapter[0]

        def key_col(dst):
            return (dst * W // group_cols) * DH

        q_blk, k_blk, a_blk, h_blk = [], [], [], []
        for s in range(C):
            dst = me ^ s
            q_blk.append(lax.dynamic_slice_in_dim(queries, dst * W, W, 1))
            k_blk.append(lax.dynamic_slice_in_dim(keys, key_col(dst), Wk, 1))
            if rblk % 128 == 0:
                cols = [lax.dynamic_slice_in_dim(hidden, (d * C + dst) * rblk, rblk, 1) for d in range(Dp)]
                h_blk.append(jnp.concatenate(cols, axis=1))
            else:
                cols = lax.dynamic_index_in_dim(hidden.reshape(tok, Dp, C, rblk), dst, 2, keepdims=False)
                h_blk.append(cols.reshape(tok, Dp * rblk))
        for s in range(1, C):
            q_blk[s] = swap(q_blk[s], s)
            k_blk[s] = swap(k_blk[s], s)
        a_blk = [adapter] + [swap(adapter, s) for s in range(1, C)]
        for s in range(1, C):
            h_blk[s] = swap(h_blk[s], s)

        pack, land, slot, rows_each = owner_tables(C, Dp, W, Wk, DH, q_width, group_cols, rows_total, rblk)
        pack_me = lax.dynamic_index_in_dim(jnp.asarray(pack.reshape(C, 1, C * slot)), me, 0, keepdims=False)
        land_me = lax.dynamic_index_in_dim(jnp.asarray(land.reshape(C, 1, C * slot)), me, 0, keepdims=False)
        up_t = adapter_up.T
        up_q = lax.dynamic_slice_in_dim(up_t, me * W, W, 1)
        up_k = lax.dynamic_slice_in_dim(up_t, q_width + key_col(me), Wk, 1)
        scalars = jnp.stack([me.astype(jnp.int32), lengths[0]])

        smem = pl.BlockSpec(memory_space=pltpu.SMEM)
        vmem = pl.BlockSpec(memory_space=pltpu.VMEM)
        bf = jnp.bfloat16
        low, packed = pl.pallas_call(
            functools.partial(attend_kernel, C, tok, hq, kh, DH, H, R),
            out_shape=(jax.ShapeDtypeStruct((2 * R, S), bf), jax.ShapeDtypeStruct((R, C * slot), bf)),
            in_specs=[smem] + [vmem] * (3 * C + 4),
            out_specs=(vmem, vmem),
            scratch_shapes=[
                pltpu.VMEM((hq, S, DH), bf),
                pltpu.VMEM((S, Wk), bf),
                pltpu.VMEM((S, 2 * R), bf),
                pltpu.VMEM((S, W), bf),
                pltpu.VMEM((Wk, S), jnp.float32),
            ],
            name="attend",
        )(scalars, *q_blk, *k_blk, *a_blk, teacher[0], up_q, up_k, pack_me)

        got = [packed[:, :slot]]
        for s in range(1, C):
            got.append(swap(packed[:, s * slot : (s + 1) * slot], s))
        bit = 1
        other = swap(low, bit)
        while bit * 2 < C:
            low = (low.astype(jnp.float32) + other.astype(jnp.float32)).astype(bf)
            bit *= 2
            other = swap(low, bit)

        msg = pl.pallas_call(
            functools.partial(down_kernel, C, Dp, tok, R, rblk),
            out_shape=jax.ShapeDtypeStruct((Dp, 3 * R, rblk), bf),
            in_specs=[smem] + [vmem] * (2 * C + 3),
            out_specs=vmem,
            name="down",
        )(scalars, low, other, *h_blk, *got, land_me)
        msg = lax.all_to_all(msg, "dp", split_axis=0, concat_axis=0, tiled=True)
        down, up = pl.pallas_call(
            functools.partial(final_kernel, R, rows_each),
            out_shape=(
                jax.ShapeDtypeStruct((rblk, 2 * R), jnp.float32),
                jax.ShapeDtypeStruct((R, rows_each), jnp.float32),
            ),
            in_specs=[vmem],
            out_specs=(vmem, vmem),
            name="final",
        )(msg)
        return down, up.T

    placed = (
        P("dp", "ctx", None),
        P("dp", "ctx", None),
        P("dp", "ctx", None, None),
        P("dp"),
        P("dp", "ctx", None),
        P("dp", "ctx", None),
        P(),
    )
    return jax.shard_map(
        body,
        mesh=mesh,
        in_specs=placed,
        out_specs=(P(("dp", "ctx"), None), P(("dp", "ctx"), None)),
        check_vma=False,
    )
```

time: 366 us -> 62.3 us (0.17)
  waiting for transfers between devices: 297 us -> 7.13 us
  blocking collectives: 0 us -> 17.7 us
  matrix products: 13.3 us -> 0 us
  between operations: 14.9 us -> 1.73 us
  Pallas kernels: 0 us -> 10.4 us
  other arithmetic: 7.86 us -> 1.53 us
  local copies, waits for them, and re-layouts: 16.8 us -> 11.5 us
  starting transfers between devices: 15.4 us -> 11.7 us
    unnamed x3 -> x0, waiting for transfers between devices: 136 us -> none
    reduce_scatter x1 -> x0, waiting for transfers between devices: 135 us -> none  [body(): lax.psum_scatter(down_terms(hidden, lowered), ('dp', 'ctx'), scatter_dime...]
    all_to_all x4 -> x0, waiting for transfers between devices: 25.5 us -> none  [the longest x1 8.34 us: body(): lax.all_to_all(dk_heads, 'ctx', split_axis=0, concat_axis=1, tiled=True)]
    all_to_all x0 -> x1, blocking collectives: none -> 17.7 us  [body(): msg = lax.all_to_all(msg, 'dp', split_axis=0, concat_axis=0, tiled=True)]
    all_to_all x4 -> x0, starting transfers between devices: 15.3 us -> none  [the longest x1 4.24 us: body(): lax.all_to_all(keys_wide, 'ctx', split_axis=1, concat_axis=0, tiled=True)]
    ppermute x0 -> x17, starting transfers between devices: none -> 11.7 us  [swap(): return lax.ppermute(x, 'ctx', [(i, i ^ s) for i in range(C)])]
    pallas_call x0 -> x3, Pallas kernels: none -> 10.4 us  [the longest x1 5.57 us: body(): pl.pallas_call(functools.partial(attend_kernel, C, tok, hq, kh, DH, H, R)...]
    ppermute x0 -> x17, waiting for transfers between devices: none -> 7.13 us  [swap(): return lax.ppermute(x, 'ctx', [(i, i ^ s) for i in range(C)])]
  transfers between devices with their start and end apart: 6 -> 17, of which waited for: 6 -> 4; matrix products, arithmetic and copies ran while one was open for 4% -> 16% of each run, Pallas kernels for 0% -> 9%
where the time goes in v1:
time: 62.3 us; the launch traced here: 61.6 us
  blocking collectives  17.7 us (28%)
  starting transfers between devices  11.7 us (19%)
  local copies, waits for them, and re-layouts  11.5 us (18%)
  Pallas kernels  10.4 us (17%)
  waiting for transfers between devices  7.13 us (11%)
  between operations  1.73 us (3%)
  other arithmetic  1.53 us (2%)
    all_to_all x1, blocking collectives, body(): msg = lax.all_to_all(msg, 'dp', split_axis=0, concat_axis=0, tiled=True)  17.7 us
    ppermute x17, starting transfers between devices, swap(): return lax.ppermute(x, 'ctx', [(i, i ^ s) for i in range(C)])  11.7 us
    ppermute x17, waiting for transfers between devices, swap(): return lax.ppermute(x, 'ctx', [(i, i ^ s) for i in range(C)])  7.13 us
    pallas_call x1, Pallas kernels, body(): pl.pallas_call(functools.partial(attend_kernel, C, tok, hq, kh, DH, H, R)...  5.57 us
    pallas_call x1, Pallas kernels, body(): pl.pallas_call(functools.partial(down_kernel, C, Dp, tok, R, rblk), out_s...  3.11 us
    unnamed x49, local copies, waits for them, and re-layouts  2.8 us
    dynamic_slice x1, local copies, waits for them, and re-layouts, body(): q_blk.append(lax.dynamic_slice_in_dim(queries, dst * W, W, 1))  1.78 us
    pallas_call x1, Pallas kernels, body(): pl.pallas_call(functools.partial(final_kernel, R, rows_each), out_shape=(...  1.74 us
  transfers between devices with their start and end apart: 17, of which 4 were waited for; matrix products, arithmetic and copies ran while one was open for 16% of the time, Pallas kernels for 9%

profile of v1, /device:TPU:0, one launch (start us, length us, event | category | flops | bytes accessed | tf_op | source)
XLA Modules:
  0.0 61.6 jit_solution(7059117138333209397)
XLA Ops:
  0.8 1.5 %dynamic-slice_bitcast_fusion.5 = (bf16[128,128]{1,0:T(8,128)(2,1)S(1)}, bf16[128,128]{1,0:T(8,128)(2,1)S(1)}, bf16[128,128]{1,0:T(8,128)(2,1)}, bf16[128,128]{1,0:T(8,128)(2,1)S(1)}) fusion(bf16[1,128,512]{2,1,0:T(8,128)(2,1)} %param.10, s32[]{:T(128)S(6)} %select_n.157, s32[]{:T(128)S(6)} %select_n.153, s32[]{:T(128)S(6)} %select_n.151, s32[]{:T(128)S(6)} %select_n.155), kind=kLoop, calls=%fused_computation.38 | loop fusion | bytes 262160 | tf_op jit(solution)/shard_map/dynamic_slice | solution.py:168
  2.8 2.5 %collective-permute-start.4 = (bf16[128,128]{1,0:T(8,128)(2,1)S(1)}, bf16[128,128]{1,0:T(8,128)(2,1)S(1)}, u32[]{:S(2)}, u32[]{:S(2)}) collective-permute-start(bf16[128,128]{1,0:T(8,128)(2,1)S(1)} %get-tuple-element.53), channel_id=1, source_target_pairs={{0,2},{1,3},{2,0},{3,1},{4,6},{5,7},{6,4},{7,5},{8,10},{9,11},{10,... | collective-permute-start | bytes 98312 | tf_op jit(solution)/shard_map/ppermute | solution.py:141
  5.4 1.8 %dynamic-slice_bitcast_fusion = (bf16[128,512]{1,0:T(8,128)(2,1)S(1)}, bf16[128,512]{1,0:T(8,128)(2,1)S(1)}, bf16[128,512]{1,0:T(8,128)(2,1)}, bf16[128,512]{1,0:T(8,128)(2,1)S(1)}) fusion(bf16[1,128,2048]{2,1,0:T(8,128)(2,1)} %param.9, s32[]{:T(128)S(6)} %select_n.149, s32[]{:T(128)S(6)} %select_n.147, s32[]{:T(128)S(6)} %select_n.146, s32[]{:T(128)S(6)} %select_n.148), kind=kLoop, calls=%fused_computation.1 | loop fusion | bytes 1048592 | tf_op jit(solution)/shard_map/dynamic_slice | solution.py:167
  7.3 1.9 %collective-permute-start.1 = (bf16[128,512]{1,0:T(8,128)(2,1)S(1)}, bf16[128,512]{1,0:T(8,128)(2,1)S(1)}, u32[]{:S(2)}, u32[]{:S(2)}) collective-permute-start(bf16[128,512]{1,0:T(8,128)(2,1)S(1)} %get-tuple-element.45), channel_id=1, source_target_pairs={{0,2},{1,3},{2,0},{3,1},{4,6},{5,7},{6,4},{7,5},{8,10},{9,11},{10,... | collective-permute-start | bytes 393224 | tf_op jit(solution)/shard_map/ppermute | solution.py:141
  9.2 0.6 %dynamic-slice_bitcast_fusion.4.refs_13_ = bf16[64,512]{1,0:T(8,128)(2,1)} fusion(bf16[2560,64]{0,1:T(8,128)(2,1)S(1)} %copy-done, s32[]{:T(128)S(6)} %select_n.158), kind=kLoop, calls=%fused_computation.37 | loop fusion | bytes 131076 | tf_op jit(solution)/shard_map/dynamic_slice | solution.py:186
  9.9 0.8 %constant_dynamic-update-slice_fusion.31 = (bf16[128,1024]{1,0:T(8,128)(2,1)S(1)}, bf16[128,1024]{1,0:T(8,128)(2,1)S(1)}, bf16[128,1024]{1,0:T(8,128)(2,1)S(1)}, bf16[128,1024]{1,0:T(8,128)(2,1)S(1)}) fusion(bf16[1,128,4096]{2,1,0:T(8,128)(2,1)} %param.13, s32[]{:T(128)S(6)} %select_n.185, s32[]{:T(128)S(6)} %select_n.177, s32[]{:T(128)S(6)} %select_n.169, ...), kind=kLoop, calls=%fused_computation.36 | loop fusion | bytes 262160
  11.3 0.7 %dynamic-slice_bitcast_fusion.9.refs_14_ = bf16[64,128]{1,0:T(8,128)(2,1)} fusion(bf16[2560,64]{0,1:T(8,128)(2,1)S(1)} %copy-done, s32[]{:T(128)S(6)} %select_n.159), kind=kLoop, calls=%fused_computation.42 | loop fusion | bytes 32772 | tf_op jit(solution)/shard_map/dynamic_slice | solution.py:187
  12.3 1.3 %fusion.refs_15_ = s32[1,1024]{1,0:T(1,128)} fusion(s32[4,1,1024]{2,1,0:T(1,128)} %constant.124.clone, s32[]{:T(128)S(6)} %select_n.160), kind=kLoop, calls=%fused_computation.45 | loop fusion | bytes 8196 | tf_op jit(solution)/shard_map/jit(dynamic_index_in_dim)/squeeze | solution.py:183
  14.2 2.0 %collective-permute-start.7 = (bf16[128,128]{1,0:T(8,128)(2,1)S(1)}, bf16[128,128]{1,0:T(8,128)(2,1)S(1)}, u32[]{:S(2)}, u32[]{:S(2)}) collective-permute-start(bf16[128,128]{1,0:T(8,128)(2,1)S(1)} %bitcast.95), channel_id=1, source_target_pairs={{0,2},{1,3},{2,0},{3,1},{4,6},{5,7},{6,4},{7,5},{8,10},{9,11},{10,... | collective-permute-start | bytes 98312 | tf_op jit(solution)/shard_map/ppermute | solution.py:141
  16.2 0.6 pad_add_fusion.scalars
  16.8 1.7 %collective-permute-done.7.refs_10_ = bf16[128,128]{1,0:T(8,128)(2,1)S(1)} collective-permute-done((bf16[128,128]{1,0:T(8,128)(2,1)S(1)}, bf16[128,128]{1,0:T(8,128)(2,1)S(1)}, u32[]{:S(2)}, u32[]{:S(2)}) %collective-permute-start.7) | collective-permute-done | bytes 32800 | tf_op jit(solution)/shard_map/ppermute | solution.py:141
  18.5 1.3 %collective-permute-done.8.refs_11_ = bf16[128,128]{1,0:T(8,128)(2,1)S(1)} collective-permute-done((bf16[128,128]{1,0:T(8,128)(2,1)S(1)}, bf16[128,128]{1,0:T(8,128)(2,1)S(1)}, u32[]{:S(2)}, u32[]{:S(2)}) %collective-permute-start.8) | collective-permute-done | bytes 32800 | tf_op jit(solution)/shard_map/ppermute | solution.py:141
  20.2 1.0 %collective-permute-start.13 = (bf16[128,1024]{1,0:T(8,128)(2,1)S(1)}, bf16[128,1024]{1,0:T(8,128)(2,1)S(1)}, u32[]{:S(2)}, u32[]{:S(2)}) collective-permute-start(bf16[128,1024]{1,0:T(8,128)(2,1)S(1)} %get-tuple-element.10), channel_id=1, source_target_pairs={{0,3},{1,2},{2,1},{3,0},{4,7},{5,6},{6,5},{7,4},{8,11},{9,10},{10,... | collective-permute-start | bytes 786440 | tf_op jit(solution)/shard_map/ppermute | solution.py:141
  21.9 5.6 %attend.1 = (bf16[128,512]{1,0:T(8,128)(2,1)}, bf16[64,1024]{1,0:T(8,128)(2,1)}) custom-call(s32[2]{0:T(128)} %pad_add_fusion.scalars, bf16[128,512]{1,0:T(8,128)(2,1)} %get-tuple-element.44.refs_0_, bf16[128,512]{1,0:T(8,128)(2,1)} %copy-done.7, bf16[128,512]{1,0:T(8,128)(2,1)} %copy-done.8, bf16[128,512]{1,0:T(8,128)(2,1)} %copy-done.9, ...), custom_call_target="tpu_custom_call" | custom-call | tf_op jit(solution)/shard_map/attend/pallas_call | solution.py:193
  27.5 0.8 %collective-permute-start.9 = (bf16[128,512]{1,0:T(8,128)(2,1)}, bf16[128,512]{1,0:T(8,128)(2,1)S(1)}, u32[]{:S(2)}, u32[]{:S(2)}) collective-permute-start(bf16[128,512]{1,0:T(8,128)(2,1)} %get-tuple-element.6), channel_id=1, source_target_pairs={{0,1},{1,0},{2,3},{3,2},{4,5},{5,4},{6,7},{7,6},{8,9},{9,8},{10,11... | collective-permute-start | bytes 393224 | tf_op jit(solution)/shard_map/ppermute | solution.py:141
  28.2 1.4 %fusion.2 = (bf16[64,256]{1,0:T(8,128)(2,1)S(1)}, bf16[64,256]{1,0:T(8,128)(2,1)S(1)}, bf16[64,256]{1,0:T(8,128)(2,1)S(1)}, bf16[64,256]{1,0:T(8,128)(2,1)}) fusion(bf16[64,1024]{1,0:T(8,128)(2,1)} %get-tuple-element.7), kind=kLoop, calls=%fused_computation.48 | loop fusion | bytes 262144 | tf_op jit(solution)/shard_map/slice | solution.py:210
  30.2 0.9 %add_convert_fusion.refs_0_ = bf16[128,512]{1,0:T(8,128)(2,1)S(1)} fusion(bf16[128,512]{1,0:T(8,128)(2,1)S(1)} %collective-permute-done.9, bf16[128,512]{1,0:T(8,128)(2,1)} %get-tuple-element.6), kind=kLoop, calls=%fused_computation | loop fusion | flops 262144 | bytes 393216 | tf_op jit(solution)/shard_map/convert_element_type | solution.py:214
  31.2 1.6 %collective-permute-start.10 = (bf16[128,512]{1,0:T(8,128)(2,1)S(1)}, bf16[128,512]{1,0:T(8,128)(2,1)S(1)}, u32[]{:S(2)}, u32[]{:S(2)}) collective-permute-start(bf16[128,512]{1,0:T(8,128)(2,1)S(1)} %add_convert_fusion.refs_0_), channel_id=1, source_target_pairs={{0,2},{1,3},{2,0},{3,1},{4,6},{5,7},{6,4},{7,5},{8,10},{9,11},{10,... | collective-permute-start | bytes 393224 | tf_op jit(solution)/shard_map/ppermute | solution.py:141
  32.8 2.0 %collective-permute-done.15.refs_8_ = bf16[64,256]{1,0:T(8,128)(2,1)S(1)} collective-permute-done((bf16[64,256]{1,0:T(8,128)(2,1)S(1)}, bf16[64,256]{1,0:T(8,128)(2,1)S(1)}, u32[]{:S(2)}, u32[]{:S(2)}) %collective-permute-start.15) | collective-permute-done | bytes 32800 | tf_op jit(solution)/shard_map/ppermute | solution.py:141
  34.8 1.3 %fusion.1.refs_10_ = s32[1,1024]{1,0:T(1,128)} fusion(s32[4,1,1024]{2,1,0:T(1,128)} %constant.125.clone, s32[]{:T(128)S(6)} %select_n.160), kind=kLoop, calls=%fused_computation.46 | loop fusion | bytes 8196 | tf_op jit(solution)/shard_map/jit(dynamic_index_in_dim)/squeeze | solution.py:184
  36.1 2.0 %collective-permute-done.16.refs_9_ = bf16[64,256]{1,0:T(8,128)(2,1)S(1)} collective-permute-done((bf16[64,256]{1,0:T(8,128)(2,1)S(1)}, bf16[64,256]{1,0:T(8,128)(2,1)S(1)}, u32[]{:S(2)}, u32[]{:S(2)}) %collective-permute-start.16) | collective-permute-done | bytes 32800 | tf_op jit(solution)/shard_map/ppermute | solution.py:141
  39.1 3.1 %down.1 = bf16[8,192,128]{2,1,0:T(8,128)(2,1)} custom-call(s32[2]{0:T(128)} %pad_add_fusion.scalars, bf16[128,512]{1,0:T(8,128)(2,1)} %copy-done.2, bf16[128,512]{1,0:T(8,128)(2,1)} %copy-done.10, bf16[128,1024]{1,0:T(8,128)(2,1)} %copy-done.3, bf16[128,1024]{1,0:T(8,128)(2,1)} %copy-done.4, bf16[128,1024]{1,0:T(8,128)(2,1)} %copy-done.5, ...), custom_call_target="tpu_custom_call" | custom-call | tf_op jit(solution)/shard_map/down/pallas_call | solution.py:218
  42.2 17.7 %all_to_all.5.got = bf16[8,192,128]{2,1,0:T(8,128)(2,1)} all-to-all(bf16[8,192,128]{2,1,0:T(8,128)(2,1)} %down.1), channel_id=1, replica_groups=mesh['dp'=8,'ctx'=4] {'dp'}, dimensions={0} | all-to-all | bytes 786432 | tf_op jit(solution)/shard_map/all_to_all | solution.py:225
  59.9 1.7 %final.1 = (f32[128,128]{1,0:T(8,128)}, f32[64,80]{1,0:T(8,128)}) custom-call(bf16[8,192,128]{2,1,0:T(8,128)(2,1)} %all_to_all.5.got), custom_call_target="tpu_custom_call" | custom-call | tf_op jit(solution)/shard_map/final/pallas_call | solution.py:226
  (73 shorter events, 4.0 us)
Async XLA Ops:
  0.6 8.6 %copy-start = (bf16[2560,64]{0,1:T(8,128)(2,1)S(1)}, bf16[2560,64]{0,1:T(8,128)(2,1)}, u32[]{:S(2)}) copy-start(bf16[2560,64]{0,1:T(8,128)(2,1)} %param.15) | copy-start | bytes 983044
  0.6 10.1 %copy-start.1 = (bf16[1,128,4096]{2,1,0:T(8,128)(2,1)S(1)}, bf16[1,128,4096]{2,1,0:T(8,128)(2,1)}, u32[]{:S(2)}) copy-start(bf16[1,128,4096]{2,1,0:T(8,128)(2,1)} %param.13) | copy-start | bytes 3145732
  0.7 11.3 %copy-start.11 = (bf16[1,128,128]{2,1,0:T(8,128)(2,1)S(1)}, bf16[1,128,128]{2,1,0:T(8,128)(2,1)}, u32[]{:S(2)}) copy-start(bf16[1,128,128]{2,1,0:T(8,128)(2,1)} %param.14) | copy-start | bytes 98308
  2.3 9.6 %collective-permute-start.3 = (bf16[128,128]{1,0:T(8,128)(2,1)S(1)}, bf16[128,128]{1,0:T(8,128)(2,1)S(1)}, u32[]{:S(2)}, u32[]{:S(2)}) collective-permute-start(bf16[128,128]{1,0:T(8,128)(2,1)S(1)} %get-tuple-element.51), channel_id=1, source_target_pairs={{0,1},{1,0},{2,3},{3,2},{4,5},{5,4},{6,7},{7,6},{8,9},{9,8},{10,11... | collective-permute-start | bytes 98312 | tf_op jit(solution)/shard_map/ppermute | solution.py:141
  2.8 9.2 %collective-permute-start.4 = (bf16[128,128]{1,0:T(8,128)(2,1)S(1)}, bf16[128,128]{1,0:T(8,128)(2,1)S(1)}, u32[]{:S(2)}, u32[]{:S(2)}) collective-permute-start(bf16[128,128]{1,0:T(8,128)(2,1)S(1)} %get-tuple-element.53), channel_id=1, source_target_pairs={{0,2},{1,3},{2,0},{3,1},{4,6},{5,7},{6,4},{7,5},{8,10},{9,11},{10,... | collective-permute-start | bytes 98312 | tf_op jit(solution)/shard_map/ppermute | solution.py:141
  5.3 8.9 %collective-permute-start.5 = (bf16[128,128]{1,0:T(8,128)(2,1)S(1)}, bf16[128,128]{1,0:T(8,128)(2,1)S(1)}, u32[]{:S(2)}, u32[]{:S(2)}) collective-permute-start(bf16[128,128]{1,0:T(8,128)(2,1)S(1)} %get-tuple-element.50), channel_id=1, source_target_pairs={{0,3},{1,2},{2,1},{3,0},{4,7},{5,6},{6,5},{7,4},{8,11},{9,10},{10,... | collective-permute-start | bytes 98312 | tf_op jit(solution)/shard_map/ppermute | solution.py:141
  7.2 13.0 %collective-permute-start = (bf16[128,512]{1,0:T(8,128)(2,1)S(1)}, bf16[128,512]{1,0:T(8,128)(2,1)S(1)}, u32[]{:S(2)}, u32[]{:S(2)}) collective-permute-start(bf16[128,512]{1,0:T(8,128)(2,1)S(1)} %get-tuple-element.43), channel_id=1, source_target_pairs={{0,1},{1,0},{2,3},{3,2},{4,5},{5,4},{6,7},{7,6},{8,9},{9,8},{10,11... | collective-permute-start | bytes 393224 | tf_op jit(solution)/shard_map/ppermute | solution.py:141
  7.3 13.9 %collective-permute-start.1 = (bf16[128,512]{1,0:T(8,128)(2,1)S(1)}, bf16[128,512]{1,0:T(8,128)(2,1)S(1)}, u32[]{:S(2)}, u32[]{:S(2)}) collective-permute-start(bf16[128,512]{1,0:T(8,128)(2,1)S(1)} %get-tuple-element.45), channel_id=1, source_target_pairs={{0,2},{1,3},{2,0},{3,1},{4,6},{5,7},{6,4},{7,5},{8,10},{9,11},{10,... | collective-permute-start | bytes 393224 | tf_op jit(solution)/shard_map/ppermute | solution.py:141
  11.3 27.0 %copy-start.3 = (bf16[128,1024]{1,0:T(8,128)(2,1)}, bf16[128,1024]{1,0:T(8,128)(2,1)S(1)}, u32[]{:S(2)}) copy-start(bf16[128,1024]{1,0:T(8,128)(2,1)S(1)} %get-tuple-element.13.refs_2_) | copy-start | bytes 786436
  12.0 9.3 %copy-start.12 = (bf16[128,128]{1,0:T(8,128)(2,1)}, bf16[128,128]{1,0:T(8,128)(2,1)S(1)}, u32[]{:S(2)}) copy-start(bf16[128,128]{1,0:T(8,128)(2,1)S(1)} %collective-permute-done.3.refs_5_) | copy-start | bytes 98308
  12.0 9.2 %collective-permute-start.2 = (bf16[128,512]{1,0:T(8,128)(2,1)S(1)}, bf16[128,512]{1,0:T(8,128)(2,1)S(1)}, u32[]{:S(2)}, u32[]{:S(2)}) collective-permute-start(bf16[128,512]{1,0:T(8,128)(2,1)S(1)} %get-tuple-element.42), channel_id=1, source_target_pairs={{0,3},{1,2},{2,1},{3,0},{4,7},{5,6},{6,5},{7,4},{8,11},{9,10},{10,... | collective-permute-start | bytes 393224 | tf_op jit(solution)/shard_map/ppermute | solution.py:141
  12.0 9.3 %copy-start.13 = (bf16[128,128]{1,0:T(8,128)(2,1)}, bf16[128,128]{1,0:T(8,128)(2,1)S(1)}, u32[]{:S(2)}) copy-start(bf16[128,128]{1,0:T(8,128)(2,1)S(1)} %collective-permute-done.4.refs_6_) | copy-start | bytes 98308
  12.0 4.2 %collective-permute-start.6 = (bf16[128,128]{1,0:T(8,128)(2,1)S(1)}, bf16[128,128]{1,0:T(8,128)(2,1)S(1)}, u32[]{:S(2)}, u32[]{:S(2)}) collective-permute-start(bf16[128,128]{1,0:T(8,128)(2,1)S(1)} %bitcast.94), channel_id=1, source_target_pairs={{0,1},{1,0},{2,3},{3,2},{4,5},{5,4},{6,7},{7,6},{8,9},{9,8},{10,11... | collective-permute-start | bytes 98312 | tf_op jit(solution)/shard_map/ppermute | solution.py:141
  14.2 4.2 %collective-permute-start.7 = (bf16[128,128]{1,0:T(8,128)(2,1)S(1)}, bf16[128,128]{1,0:T(8,128)(2,1)S(1)}, u32[]{:S(2)}, u32[]{:S(2)}) collective-permute-start(bf16[128,128]{1,0:T(8,128)(2,1)S(1)} %bitcast.95), channel_id=1, source_target_pairs={{0,2},{1,3},{2,0},{3,1},{4,6},{5,7},{6,4},{7,5},{8,10},{9,11},{10,... | collective-permute-start | bytes 98312 | tf_op jit(solution)/shard_map/ppermute | solution.py:141
  16.2 3.6 %collective-permute-start.8 = (bf16[128,128]{1,0:T(8,128)(2,1)S(1)}, bf16[128,128]{1,0:T(8,128)(2,1)S(1)}, u32[]{:S(2)}, u32[]{:S(2)}) collective-permute-start(bf16[128,128]{1,0:T(8,128)(2,1)S(1)} %bitcast.96), channel_id=1, source_target_pairs={{0,3},{1,2},{2,1},{3,0},{4,7},{5,6},{6,5},{7,4},{8,11},{9,10},{10,... | collective-permute-start | bytes 98312 | tf_op jit(solution)/shard_map/ppermute | solution.py:141
  18.5 19.7 %collective-permute-start.11 = (bf16[128,1024]{1,0:T(8,128)(2,1)S(1)}, bf16[128,1024]{1,0:T(8,128)(2,1)S(1)}, u32[]{:S(2)}, u32[]{:S(2)}) collective-permute-start(bf16[128,1024]{1,0:T(8,128)(2,1)S(1)} %get-tuple-element.12), channel_id=1, source_target_pairs={{0,1},{1,0},{2,3},{3,2},{4,5},{5,4},{6,7},{7,6},{8,9},{9,8},{10,11... | collective-permute-start | bytes 786440 | tf_op jit(solution)/shard_map/ppermute | solution.py:141
  19.8 18.4 %collective-permute-start.12 = (bf16[128,1024]{1,0:T(8,128)(2,1)S(1)}, bf16[128,1024]{1,0:T(8,128)(2,1)S(1)}, u32[]{:S(2)}, u32[]{:S(2)}) collective-permute-start(bf16[128,1024]{1,0:T(8,128)(2,1)S(1)} %get-tuple-element.11), channel_id=1, source_target_pairs={{0,2},{1,3},{2,0},{3,1},{4,6},{5,7},{6,4},{7,5},{8,10},{9,11},{10,... | collective-permute-start | bytes 786440 | tf_op jit(solution)/shard_map/ppermute | solution.py:141
  20.2 18.0 %collective-permute-start.13 = (bf16[128,1024]{1,0:T(8,128)(2,1)S(1)}, bf16[128,1024]{1,0:T(8,128)(2,1)S(1)}, u32[]{:S(2)}, u32[]{:S(2)}) collective-permute-start(bf16[128,1024]{1,0:T(8,128)(2,1)S(1)} %get-tuple-element.10), channel_id=1, source_target_pairs={{0,3},{1,2},{2,1},{3,0},{4,7},{5,6},{6,5},{7,4},{8,11},{9,10},{10,... | collective-permute-start | bytes 786440 | tf_op jit(solution)/shard_map/ppermute | solution.py:141
  27.5 2.2 %collective-permute-start.9 = (bf16[128,512]{1,0:T(8,128)(2,1)}, bf16[128,512]{1,0:T(8,128)(2,1)S(1)}, u32[]{:S(2)}, u32[]{:S(2)}) collective-permute-start(bf16[128,512]{1,0:T(8,128)(2,1)} %get-tuple-element.6), channel_id=1, source_target_pairs={{0,1},{1,0},{2,3},{3,2},{4,5},{5,4},{6,7},{7,6},{8,9},{9,8},{10,11... | collective-permute-start | bytes 393224 | tf_op jit(solution)/shard_map/ppermute | solution.py:141
  29.7 1.5 %collective-permute-start.14 = (bf16[64,256]{1,0:T(8,128)(2,1)S(1)}, bf16[64,256]{1,0:T(8,128)(2,1)S(1)}, u32[]{:S(2)}, u32[]{:S(2)}) collective-permute-start(bf16[64,256]{1,0:T(8,128)(2,1)S(1)} %get-tuple-element.48), channel_id=1, source_target_pairs={{0,1},{1,0},{2,3},{3,2},{4,5},{5,4},{6,7},{7,6},{8,9},{9,8},{10,11... | collective-permute-start | bytes 98312 | tf_op jit(solution)/shard_map/ppermute | solution.py:141
  29.7 5.2 %collective-permute-start.15 = (bf16[64,256]{1,0:T(8,128)(2,1)S(1)}, bf16[64,256]{1,0:T(8,128)(2,1)S(1)}, u32[]{:S(2)}, u32[]{:S(2)}) collective-permute-start(bf16[64,256]{1,0:T(8,128)(2,1)S(1)} %get-tuple-element.47), channel_id=1, source_target_pairs={{0,2},{1,3},{2,0},{3,1},{4,6},{5,7},{6,4},{7,5},{8,10},{9,11},{10,... | collective-permute-start | bytes 98312 | tf_op jit(solution)/shard_map/ppermute | solution.py:141
  31.1 7.1 %copy-start.2 = (bf16[128,512]{1,0:T(8,128)(2,1)}, bf16[128,512]{1,0:T(8,128)(2,1)S(1)}, u32[]{:S(2)}) copy-start(bf16[128,512]{1,0:T(8,128)(2,1)S(1)} %add_convert_fusion.refs_0_) | copy-start | bytes 393220
  31.2 7.1 %collective-permute-start.10 = (bf16[128,512]{1,0:T(8,128)(2,1)S(1)}, bf16[128,512]{1,0:T(8,128)(2,1)S(1)}, u32[]{:S(2)}, u32[]{:S(2)}) collective-permute-start(bf16[128,512]{1,0:T(8,128)(2,1)S(1)} %add_convert_fusion.refs_0_), channel_id=1, source_target_pairs={{0,2},{1,3},{2,0},{3,1},{4,6},{5,7},{6,4},{7,5},{8,10},{9,11},{10,... | collective-permute-start | bytes 393224 | tf_op jit(solution)/shard_map/ppermute | solution.py:141
  34.8 3.3 %collective-permute-start.16 = (bf16[64,256]{1,0:T(8,128)(2,1)S(1)}, bf16[64,256]{1,0:T(8,128)(2,1)S(1)}, u32[]{:S(2)}, u32[]{:S(2)}) collective-permute-start(bf16[64,256]{1,0:T(8,128)(2,1)S(1)} %get-tuple-element.46), channel_id=1, source_target_pairs={{0,3},{1,2},{2,1},{3,0},{4,7},{5,6},{6,5},{7,4},{8,11},{9,10},{10,... | collective-permute-start | bytes 98312 | tf_op jit(solution)/shard_map/ppermute | solution.py:141
  (14 other events, 33.2 us)

commit v2 on v1

v2 whole, which is shorter than its diff:
```python
import functools
import math

import jax
import jax.numpy as jnp
import numpy as np
from jax import lax
from jax.experimental import pallas as pl
from jax.experimental.pallas import tpu as pltpu
from jax.sharding import PartitionSpec as P

NT = (((1,), (1,)), ((), ()))
TN = (((0,), (0,)), ((), ()))


def dot32(a, b, dims=(((1,), (0,)), ((), ()))):
    return lax.dot_general(a, b, dims, preferred_element_type=jnp.float32)


def owner_tables(C, Dp, W, Wk, DH, q_width, group_cols, rows_total, lane_block, lanes):
    rows_each = rows_total // (C * Dp)
    local = []
    for c in range(C):
        k_start = q_width + (c * W // group_cols) * DH
        local.append(np.concatenate([c * W + np.arange(W), k_start + np.arange(Wk)]))

    def chosen(c, core, y):
        owner = local[c] // rows_each
        return np.nonzero((owner % C % 2 == core) & (owner // C % 2 == y))[0]

    most = max(len(chosen(c, core, y)) for c in range(C) for core in (0, 1) for y in (0, 1))
    slot = -(-most // lanes) * lanes
    pack = np.full((C, 2, 4, slot), -1, np.int32)
    land = np.full((C, 2, 4, slot), -1, np.int32)
    for c in range(C):
        for y in (0, 1):
            for n in range(4):
                there, across = n % 2, n // 2
                rows = chosen(c, c % 2 ^ there, y ^ across)
                pack[c, y, n, : len(rows)] = rows
                src = c ^ there
                rows = local[src][chosen(src, c % 2, y)]
                owner = rows // rows_each
                block = (owner // C // 2) * (C // 2) + owner % C // 2
                land[c, y, n, : len(rows)] = block * lane_block + rows % rows_each
    return pack.reshape(C * 2, 4 * slot), land.reshape(C * 2, 4 * slot), slot, rows_each


def slice_kernel(plan, n_in, *refs):
    ins, (*outs, sems) = refs[:n_in], refs[n_in:]
    copies = []
    for n, (i, src, o, dst, width) in enumerate(plan(lax.axis_index("ctx"), lax.axis_index("dp"))):
        source = ins[i] if src is None else ins[i].at[..., pl.ds(src, width)]
        target = outs[o] if dst is None else outs[o].at[..., pl.ds(dst, width)]
        copies.append(pltpu.make_async_copy(source, target, sems.at[n]))
    for c in copies:
        c.start()
    for c in copies:
        c.wait()


def slices(plan, count, ins, out_shapes):
    spec = pl.BlockSpec(memory_space=pltpu.HBM)
    vmem = pl.BlockSpec(memory_space=pltpu.VMEM)
    ins = [pltpu.with_memory_space_constraint(x, pltpu.HBM) for x in ins]
    return pl.pallas_call(
        functools.partial(slice_kernel, plan, len(ins)),
        out_shape=tuple(out_shapes),
        in_specs=[spec] * len(ins),
        out_specs=tuple([vmem] * len(out_shapes)),
        scratch_shapes=[pltpu.SemaphoreType.DMA((count,))],
        compiler_params=pltpu.CompilerParams(vmem_limit_bytes=2**20),
    )(*ins)


def attend_kernel(C, tok, hq, kh, DH, H, R, lengths, *refs):
    msgs = refs[:C]
    teacher, up_q, up_k, pack = refs[C : C + 4]
    keep_out, send_out, packed_own, packed_far = refs[C + 4 : C + 8]
    q_buf, k_buf, a_buf, dq_buf, dk_buf, low_buf = refs[C + 8 :]
    me, length = lax.axis_index("ctx"), lengths[0]
    W, Wk = hq * DH, kh * DH
    per_key = hq // kh
    scale = 1.0 / math.sqrt(DH)
    exp_scale = scale * math.log2(math.e)
    for s in range(C):
        row = pl.multiple_of(jnp.bitwise_xor(me, s) * tok, tok)
        for h in range(hq):
            q_buf[h, pl.ds(row, tok), :] = msgs[s][:, h * DH : (h + 1) * DH]
        k_buf[pl.ds(row, tok), :] = msgs[s][:, W : W + Wk]
        a_buf[pl.ds(row, tok), :] = msgs[s][:, W + Wk :]
    dk_buf[...] = jnp.zeros_like(dk_buf)
    row_in = lax.broadcasted_iota(jnp.int32, (tok, 1), 0)
    col_in = lax.broadcasted_iota(jnp.int32, (tok, tok), 1)
    for p in range(C):
        start, ext = p * tok, (p + 1) * tok
        row_pos = row_in + start
        visible = (col_in + start) <= jnp.minimum(row_pos, length - 1)
        weight = jnp.where(row_pos < length, 1.0 / H, 0.0)
        for g in range(kh):
            keys = k_buf[:ext, g * DH : (g + 1) * DH]
            heads = range(g * per_key, (g + 1) * per_key)
            q_all = q_buf[g * per_key : (g + 1) * per_key, start:ext, :].reshape(per_key * tok, DH)
            scores = dot32(q_all, keys, NT)
            grads = []
            for n, h in enumerate(heads):
                sc = scores[n * tok : (n + 1) * tok]
                diag = jnp.where(visible, sc[:, start:], -1e30)
                sc = diag if p == 0 else jnp.concatenate([sc[:, :start], diag], axis=1)
                te_d = jnp.where(visible, teacher[h, start:ext, start:ext].astype(jnp.float32), 0.0)
                te = te_d if p == 0 else jnp.concatenate(
                    [teacher[h, start:ext, :start].astype(jnp.float32), te_d], axis=1
                )
                ex = jnp.exp2((sc - jnp.max(sc, axis=1, keepdims=True)) * exp_scale)
                w_s = weight / jnp.sum(ex, axis=1, keepdims=True)
                w_t = weight / jnp.sum(te, axis=1, keepdims=True)
                grads.append((ex * w_s - te * w_t).astype(jnp.bfloat16))
            grad = grads[0] if per_key == 1 else jnp.concatenate(grads, axis=0)
            dq = (dot32(grad, keys) * scale).astype(jnp.bfloat16)
            for n, h in enumerate(heads):
                dq_buf[start:ext, h * DH : (h + 1) * DH] = dq[n * tok : (n + 1) * tok]
            dk_buf[g * DH : (g + 1) * DH, :ext] += dot32(q_all, grad, TN)
    dq = dq_buf[...]
    dk = (dk_buf[...] * scale).astype(jnp.bfloat16)
    low_buf[:R, :] = dot32(up_q[...], dq, NT)
    low_buf[R:, :] = dot32(up_k[...], dk)
    far, mine = jnp.right_shift(me, 1), jnp.bitwise_and(me, 1)
    for n in range(C // 2):
        here = jnp.bitwise_xor(far, n) * 2
        keep_out[n] = low_buf[:, pl.ds(pl.multiple_of((here + mine) * tok, tok), tok)]
        send_out[n * 2 * R : (n + 1) * 2 * R, :] = low_buf[:, pl.ds(pl.multiple_of((here + 1 - mine) * tok, tok), tok)]
    a_q, a_k = a_buf[:, :R], a_buf[:, R:]
    grad_up = jnp.concatenate(
        [dot32(a_q, dq, TN).astype(jnp.bfloat16), dot32(a_k.T, dk, NT).astype(jnp.bfloat16)], axis=1
    )
    where_to = pack[pl.ds(me * 2 + jnp.bitwise_and(lax.axis_index("dp"), 1), 1), :]
    pick = lax.broadcasted_iota(jnp.int32, (grad_up.shape[1], where_to.shape[1]), 0) == where_to
    pick = jnp.where(pick, 1.0, 0.0).astype(jnp.bfloat16)
    rows = dot32(grad_up, pick)
    blks = where_to.shape[1] // 4 // tok
    for n in range(4 * blks):
        to, part = n // blks, n % blks
        dst = (packed_own, send_out, packed_far, send_out)[to]
        at = (0, C * R, 0, C * R + blks * R)[to] + part * R
        dst[at : at + R, :] = rows[:, n * tok : (n + 1) * tok].astype(dst.dtype)


def down_kernel(R, rblk, low_pair, low_other, got_own, got_pair, got_far, h0, h1, h2, h3, land, send, keep):
    lows = (low_pair[0], low_other[0], low_pair[1], low_other[1])
    acc = None
    for low, hid in zip(lows, (h0, h1, h2, h3)):
        term = dot32(low, hid[...])
        acc = term if acc is None else acc + term
    blks = got_own.shape[0] // R
    pieces = [got_own[n * R : (n + 1) * R, :] for n in range(blks)]
    pieces += [got_pair[n * R : (n + 1) * R, :].astype(jnp.bfloat16) for n in range(blks)]
    pieces += [got_far[n * R : (n + 1) * R, :] for n in range(2 * blks)]
    rows = jnp.concatenate(pieces, axis=1)
    me, me_d = lax.axis_index("ctx"), lax.axis_index("dp")
    half_c = lax.axis_size("ctx") // 2
    here = jnp.right_shift(me_d, 1) * half_c + jnp.right_shift(me, 1)
    where_to = jnp.bitwise_xor(land[pl.ds(me * 2 + jnp.bitwise_and(me_d, 1), 1), :], here * rblk)
    place = lax.broadcasted_iota(jnp.int32, (h0.shape[1], rows.shape[1]), 0) == where_to
    place = jnp.where(place, 1.0, 0.0).astype(jnp.bfloat16)
    ups = dot32(rows, place, NT)
    for e in range(h0.shape[1] // rblk):
        dst = send if e % 2 else keep
        dst[e // 2, : 2 * R, :] = acc[:, e * rblk : (e + 1) * rblk].astype(dst.dtype)
        dst[e // 2, 2 * R :, :] = ups[:, e * rblk : (e + 1) * rblk].astype(dst.dtype)


def final_kernel(R, rows_each, kept, got, down, up):
    total = kept[0] + got[0].astype(jnp.float32)
    down[...] = total[: 2 * R].T
    up[...] = total[2 * R :, :rows_each]


def solution(mesh):
    C, Dp = mesh.shape["ctx"], mesh.shape["dp"]

    def swap(x, s, axis="ctx"):
        return lax.ppermute(x, axis, [(i, i ^ s) for i in range(mesh.shape[axis])])

    def swap_diag(x):
        pairs = [(d * C + c, (d ^ 1) * C + (c ^ 1)) for d in range(Dp) for c in range(C)]
        return lax.ppermute(x, ("dp", "ctx"), pairs)

    def near(x):
        return pltpu.with_memory_space_constraint(x, pltpu.VMEM)

    def body(queries, keys, teacher, lengths, hidden, adapter, adapter_up):
        tok = queries.shape[1]
        hq = teacher.shape[1]
        S = teacher.shape[2]
        H = hq * C
        DH = queries.shape[2] // H
        KV = keys.shape[2] // DH
        R = adapter.shape[2] // 2
        D = hidden.shape[2]
        q_width = H * DH
        rows_total = adapter_up.shape[0]
        kh = max(1, KV // C)
        W, Wk = hq * DH, kh * DH
        rblk = D // (C * Dp)
        group_cols = (H // KV) * DH
        bf, f32 = jnp.bfloat16, jnp.float32

        def key_col(dst):
            return (dst * W // group_cols) * DH

        def first_plan(me, me_d):
            for s in range(C):
                dst = jnp.bitwise_xor(me, s)
                yield 0, pl.multiple_of(dst * W, 128), s, 0, W
                yield 1, pl.multiple_of(key_col(dst), 128), s, W, Wk
                yield 2, 0, s, W + Wk, 2 * R

        def second_plan(me, me_d):
            yield 0, None, 0, None, None
            yield 1, pl.multiple_of(me * W, 128), 1, 0, W
            yield 1, pl.multiple_of(q_width + key_col(me), 128), 2, 0, Wk
            yield 2, None, 3, None, None
            yield 3, None, 4, None, None
            if rblk % 128 == 0:
                for n in range(4):
                    for e in range(E):
                        yield 4, pl.multiple_of(column(me, me_d, n, e), 128), 5 + n, e * rblk, rblk

        E = C * Dp // 4

        def column(me, me_d, n, e):
            d = jnp.bitwise_xor(me_d, n // 2 + e // (C // 2) * 2)
            return (d * C + jnp.bitwise_xor(me, n % 2 + e % (C // 2) * 2)) * rblk

        pack, land, slot, rows_each = owner_tables(C, Dp, W, Wk, DH, q_width, group_cols, rows_total, rblk, tok)
        pack, land = jnp.asarray(pack), jnp.asarray(land)
        msgs = list(slices(first_plan, 3 * C, (queries[0], keys[0], adapter[0]), [pltpu.VMEM((tok, W + Wk + 2 * R), bf)] * C))
        for s in range(1, C):
            msgs[s] = swap(msgs[s], s)
        by_dma = rblk % 128 == 0
        outs = [
            pltpu.VMEM(teacher.shape[1:], bf),
            pltpu.VMEM((R, W), bf),
            pltpu.VMEM((R, Wk), bf),
            pltpu.VMEM(pack.shape, jnp.int32),
            pltpu.VMEM(land.shape, jnp.int32),
        ] + [pltpu.VMEM((tok, E * rblk), bf)] * (4 if by_dma else 0)
        ins = (teacher[0], adapter_up.T, pack, land) + ((hidden[0],) if by_dma else ())
        teach, up_q, up_k, pack, land, *hids = slices(second_plan, 5 + (4 * E if by_dma else 0), ins, outs)
        if not by_dma:
            blocks = hidden[0].reshape(tok, C * Dp, rblk)
            me, me_d = lax.axis_index("ctx"), lax.axis_index("dp")
            hids = []
            for n in range(4):
                order = jnp.stack([column(me, me_d, n, e) // rblk for e in range(E)])
                hids.append(jnp.take(blocks, order, axis=1).reshape(tok, E * rblk))
        hids[1] = swap(hids[1], 1)
        hids[2] = swap(hids[2], 1, "dp")
        hids[3] = swap_diag(hids[3])

        smem = pl.BlockSpec(memory_space=pltpu.SMEM)
        vmem = pl.BlockSpec(memory_space=pltpu.VMEM)
        params = pltpu.CompilerParams(vmem_limit_bytes=24 * 2**20)
        low_rows, piece = C * R, slot // tok * R
        keep, send, own, even = pl.pallas_call(
            functools.partial(attend_kernel, C, tok, hq, kh, DH, H, R),
            out_shape=(
                pltpu.VMEM((C // 2, 2 * R, tok), f32),
                pltpu.VMEM((low_rows + 2 * piece, tok), f32),
                pltpu.VMEM((piece, tok), bf),
                pltpu.VMEM((piece, tok), bf),
            ),
            in_specs=[smem] + [vmem] * (C + 4),
            out_specs=tuple([vmem] * 4),
            scratch_shapes=[
                pltpu.VMEM((hq, S, DH), bf),
                pltpu.VMEM((S, Wk), bf),
                pltpu.VMEM((S, 2 * R), bf),
                pltpu.VMEM((S, W), bf),
                pltpu.VMEM((Wk, S), f32),
                pltpu.VMEM((2 * R, S), f32),
            ],
            compiler_params=params,
            name="attend",
        )(lengths, *[near(m) for m in msgs], near(teach), near(up_q), near(up_k), near(pack))

        pair = swap(send, 1)
        low = keep + pair[:low_rows].reshape(keep.shape)
        bit = 2
        while bit < C:
            both = low.reshape((-1, 2) + low.shape[1:])
            low = both[:, 0] + swap(both[:, 1].astype(bf), bit).astype(f32)
            bit *= 2
        relay = pair[low_rows + piece :].astype(bf)
        far = swap(jnp.concatenate([even, relay]), 1, "dp")
        low = low.astype(bf)
        low = jnp.concatenate([low, swap(low, 1, "dp")])
        other = swap(low, 1)

        send, keep = pl.pallas_call(
            functools.partial(down_kernel, R, rblk),
            out_shape=(pltpu.VMEM((E // 2, 3 * R, rblk), bf), pltpu.VMEM((E // 2, 3 * R, rblk), f32)),
            in_specs=[vmem] * 10,
            out_specs=(vmem, vmem),
            compiler_params=params,
            name="down",
        )(
            near(low), near(other), near(own), near(pair[low_rows : low_rows + piece]), near(far),
            *[near(h) for h in hids], near(land),
        )
        rounds = [("ctx", 2 << i) for i in range(C.bit_length() - 2)]
        rounds += [("dp", 2 << i) for i in range(Dp.bit_length() - 2)]
        for n, (axis, bit) in enumerate(rounds):
            if n:
                both = keep.reshape((-1, 2) + keep.shape[1:])
                keep, send = both[:, 0], both[:, 1].astype(bf)
            got = swap(send, bit, axis)
            if n < len(rounds) - 1:
                keep = keep + got.astype(f32)
        down, up = pl.pallas_call(
            functools.partial(final_kernel, R, rows_each),
            out_shape=(jax.ShapeDtypeStruct((rblk, 2 * R), f32), jax.ShapeDtypeStruct((R, rows_each), f32)),
            in_specs=[vmem, vmem],
            out_specs=(vmem, vmem),
            compiler_params=params,
            name="final",
        )(near(keep), near(got))
        return down, up.T

    placed = (
        P("dp", "ctx", None),
        P("dp", "ctx", None),
        P("dp", "ctx", None, None),
        P("dp"),
        P("dp", "ctx", None),
        P("dp", "ctx", None),
        P(),
    )
    return jax.shard_map(
        body,
        mesh=mesh,
        in_specs=placed,
        out_specs=(P(("dp", "ctx"), None), P(("dp", "ctx"), None)),
        check_vma=False,
    )
```

time: 62.3 us -> 56.4 us (0.905)
  waiting for transfers between devices: 7.13 us -> 32.7 us
  blocking collectives: 17.7 us -> 0 us
  local copies, waits for them, and re-layouts: 11.5 us -> 0.06 us
  Pallas kernels: 10.4 us -> 8.25 us
  starting transfers between devices: 11.7 us -> 13.7 us
  other arithmetic: 1.53 us -> 0.09 us
    ppermute x17 -> x14, waiting for transfers between devices: 7.13 us -> 32.7 us  [the longest x13 32.7 us: swap(): return lax.ppermute(x, axis, [(i, i ^ s) for i in range(mesh.shape[axis])])]
    all_to_all x1 -> x0, blocking collectives: 17.7 us -> none  [body(): msg = lax.all_to_all(msg, 'dp', split_axis=0, concat_axis=0, tiled=True)]
    dynamic_slice x4 -> x0, local copies, waits for them, and re-layouts: 4.61 us -> none  [the longest x1 1.78 us: body(): q_blk.append(lax.dynamic_slice_in_dim(queries, dst * W, W, 1))]
    unnamed x49 -> x0, local copies, waits for them, and re-layouts: 2.8 us -> none
    pallas_call x1, Pallas kernels: 5.57 us -> 2.94 us  [body(): pl.pallas_call(functools.partial(attend_kernel, C, tok, hq, kh, DH, H, R)...]
    squeeze x2 -> x1, local copies, waits for them, and re-layouts: 2.57 us -> 0.01 us  [body(): keep, send = (both[:, 0], both[:, 1].astype(bf))]
    ppermute x17 -> x14, starting transfers between devices: 11.7 us -> 13.7 us  [the longest x13 13.4 us: swap(): return lax.ppermute(x, axis, [(i, i ^ s) for i in range(mesh.shape[axis])])]
    pallas_call x1 -> x3, Pallas kernels: 3.11 us -> 4.58 us  [the longest x2 3.55 us: slices(): pl.pallas_call(functools.partial(slice_kernel, plan, len(ins)), out_shape...]
  transfers between devices with their start and end apart: 17 -> 14, of which waited for: 4 -> 10; matrix products, arithmetic and copies ran while one was open for 16% -> 0% of each run, Pallas kernels for 9% -> 4%
where the time goes in v2:
time: 56.4 us; the launch traced here: 56.2 us
  waiting for transfers between devices  32.7 us (58%)
  starting transfers between devices  13.7 us (24%)
  Pallas kernels  8.25 us (15%)
  between operations  1.42 us (3%)
    ppermute x13, waiting for transfers between devices, swap(): return lax.ppermute(x, axis, [(i, i ^ s) for i in range(mesh.shape[axis])])  32.7 us
    ppermute x13, starting transfers between devices, swap(): return lax.ppermute(x, axis, [(i, i ^ s) for i in range(mesh.shape[axis])])  13.4 us
    pallas_call x2, Pallas kernels, slices(): pl.pallas_call(functools.partial(slice_kernel, plan, len(ins)), out_shape...  3.55 us
    pallas_call x1, Pallas kernels, body(): pl.pallas_call(functools.partial(attend_kernel, C, tok, hq, kh, DH, H, R)...  2.94 us
  transfers between devices with their start and end apart: 14, of which 10 were waited for; matrix products, arithmetic and copies ran while one was open for 0% of the time, Pallas kernels for 4%

profile of v2, /device:TPU:0, one launch (start us, length us, event | category | flops | bytes accessed | tf_op | source)
XLA Modules:
  0.0 56.2 jit_solution(14300204125147501693)
XLA Ops:
  0.6 1.3 %shard_map.104 = (bf16[128,768]{1,0:T(8,128)(2,1)S(1)}, bf16[128,768]{1,0:T(8,128)(2,1)S(1)}, bf16[128,768]{1,0:T(8,128)(2,1)S(1)}, bf16[128,768]{1,0:T(8,128)(2,1)S(1)}) custom-call(bf16[128,2048]{1,0:T(8,128)(2,1)} %bitcast.38, bf16[128,512]{1,0:T(8,128)(2,1)} %bitcast.40, bf16[128,128]{1,0:T(8,128)(2,1)} %bitcast.41), custom_call_target="tpu_custom_call" | custom-call | tf_op jit(solution)/shard_map/pallas_call | solution.py:66
  2.0 0.6 collective-permute-start
  2.5 2.6 %collective-permute-start.1 = (bf16[128,768]{1,0:T(8,128)(2,1)S(1)}, bf16[128,768]{1,0:T(8,128)(2,1)S(1)}, u32[]{:S(2)}, u32[]{:S(2)}) collective-permute-start(bf16[128,768]{1,0:T(8,128)(2,1)S(1)} %get-tuple-element.25), channel_id=1, source_target_pairs={{0,2},{1,3},{2,0},{3,1},{4,6},{5,7},{6,4},{7,5},{8,10},{9,11},{10,... | collective-permute-start | bytes 589832 | tf_op jit(solution)/shard_map/ppermute | solution.py:182
  5.8 2.2 %shard_map.105 = (bf16[4,512,512]{2,1,0:T(8,128)(2,1)S(1)}, bf16[64,512]{1,0:T(8,128)(2,1)S(1)}, bf16[64,128]{1,0:T(8,128)(2,1)S(1)}, s32[8,1024]{1,0:T(8,128)S(...) custom-call(bf16[4,512,512]{2,1,0:T(8,128)(2,1)} %bitcast.33, ...), custom_call_target="tpu_custom_call" | custom-call | tf_op jit(solution)/shard_map/pallas_call | solution.py:66
  8.0 2.8 %collective-permute-done.1.refs_2_ = bf16[128,768]{1,0:T(8,128)(2,1)S(1)} collective-permute-done((bf16[128,768]{1,0:T(8,128)(2,1)S(1)}, bf16[128,768]{1,0:T(8,128)(2,1)S(1)}, u32[]{:S(2)}, u32[]{:S(2)}) %collective-permute-start.1) | collective-permute-done | bytes 196640 | tf_op jit(solution)/shard_map/ppermute | solution.py:182
  10.8 3.7 %collective-permute-done.2.refs_3_ = bf16[128,768]{1,0:T(8,128)(2,1)S(1)} collective-permute-done((bf16[128,768]{1,0:T(8,128)(2,1)S(1)}, bf16[128,768]{1,0:T(8,128)(2,1)S(1)}, u32[]{:S(2)}, u32[]{:S(2)}) %collective-permute-start.2) | collective-permute-done | bytes 196640 | tf_op jit(solution)/shard_map/ppermute | solution.py:182
  14.5 2.9 %attend.1 = (f32[2,128,128]{2,1,0:T(8,128)S(1)}, f32[512,128]{1,0:T(8,128)S(1)}, bf16[128,128]{1,0:T(8,128)(2,1)S(1)}, bf16[128,128]{1,0:T(8,128)(2,1)S(1)}) custom-call(s32[1]{0:T(128)S(6)} %copy.23.lengths, bf16[128,768]{1,0:T(8,128)(2,1)S(1)} %get-tuple-element.23.refs_0_, bf16[128,768]{1,0:T(8,128)(2,1)S(1)} %collective-permute-done.refs_1_, ...), custom_call_target="tpu_custom_call" | custom-call | tf_op jit(solution)/shard_map/attend/pallas_call | solution.py:265
  17.6 1.4 %collective-permute-done.3 = f32[512,128]{1,0:T(8,128)S(1)} collective-permute-done((f32[512,128]{1,0:T(8,128)S(1)}, f32[512,128]{1,0:T(8,128)S(1)}, u32[]{:S(2)}, u32[]{:S(2)}) %collective-permute-start.3) | collective-permute-done | bytes 262176 | tf_op jit(solution)/shard_map/ppermute | solution.py:182
  19.1 1.5 %collective-permute-start.4 = (bf16[1,128,128]{2,1,0:T(8,128)(2,1)S(1)}, bf16[1,128,128]{2,1,0:T(8,128)(2,1)S(1)}, u32[]{:S(2)}, u32[]{:S(2)}) collective-permute-start(bf16[1,128,128]{2,1,0:T(8,128)(2,1)S(1)} %fusion.6), channel_id=1, source_target_pairs={{0,2},{1,3},{2,0},{3,1},{4,6},{5,7},{6,4},{7,5},{8,10},{9,11},{10,... | collective-permute-start | bytes 98312 | tf_op jit(solution)/shard_map/ppermute | solution.py:182
  20.7 1.5 %collective-permute-start.9 = (bf16[128,1024]{1,0:T(8,128)(2,1)S(1)}, bf16[128,1024]{1,0:T(8,128)(2,1)S(1)}, u32[]{:S(2)}, u32[]{:S(2)}) collective-permute-start(bf16[128,1024]{1,0:T(8,128)(2,1)S(1)} %get-tuple-element.37), channel_id=1, source_target_pairs={{0,4},{4,0},{8,12},{12,8},{16,20},{20,16},{24,28},{28,24},{1,5},{5... | collective-permute-start | bytes 786440 | tf_op jit(solution)/shard_map/ppermute | solution.py:182
  22.5 0.6 %collective-permute-done.4 = bf16[1,128,128]{2,1,0:T(8,128)(2,1)S(1)} collective-permute-done((bf16[1,128,128]{2,1,0:T(8,128)(2,1)S(1)}, bf16[1,128,128]{2,1,0:T(8,128)(2,1)S(1)}, u32[]{:S(2)}, u32[]{:S(2)}) %collective-permute-start.4) | collective-permute-done | bytes 32800 | tf_op jit(solution)/shard_map/ppermute | solution.py:182
  23.1 1.6 %collective-permute-start.5 = (bf16[1,128,128]{2,1,0:T(8,128)(2,1)S(1)}, bf16[1,128,128]{2,1,0:T(8,128)(2,1)S(1)}, u32[]{:S(2)}, u32[]{:S(2)}) collective-permute-start(bf16[1,128,128]{2,1,0:T(8,128)(2,1)S(1)} %fusion.4), channel_id=1, source_target_pairs={{0,4},{4,0},{8,12},{12,8},{16,20},{20,16},{24,28},{28,24},{1,5},{5... | collective-permute-start | bytes 98312 | tf_op jit(solution)/shard_map/ppermute | solution.py:182
  24.7 0.5 collective-permute-start.7
  25.2 11.0 %collective-permute-done.5 = bf16[1,128,128]{2,1,0:T(8,128)(2,1)S(1)} collective-permute-done((bf16[1,128,128]{2,1,0:T(8,128)(2,1)S(1)}, bf16[1,128,128]{2,1,0:T(8,128)(2,1)S(1)}, u32[]{:S(2)}, u32[]{:S(2)}) %collective-permute-start.5) | collective-permute-done | bytes 32800 | tf_op jit(solution)/shard_map/ppermute | solution.py:182
  36.4 0.7 %collective-permute-done.7.got_far = bf16[256,128]{1,0:T(8,128)(2,1)S(1)} collective-permute-done((bf16[256,128]{1,0:T(8,128)(2,1)S(1)}, bf16[256,128]{1,0:T(8,128)(2,1)S(1)}, u32[]{:S(2)}, u32[]{:S(2)}) %collective-permute-start.7) | collective-permute-done | bytes 65568 | tf_op jit(solution)/shard_map/ppermute | solution.py:182
  37.1 0.5 collective-permute-done.6.low_other
  37.6 1.0 %down.1 = (bf16[4,192,128]{2,1,0:T(8,128)(2,1)S(1)}, f32[4,192,128]{2,1,0:T(8,128)S(1)}) custom-call(bf16[2,128,128]{2,1,0:T(8,128)(2,1)S(1)} %pad_maximum_fusion.low_pair, bf16[2,128,128]{2,1,0:T(8,128)(2,1)S(1)} %collective-permute-done.6.low_other, bf16[128,128]{1,0:T(8,128)(2,1)S(1)} %get-tuple-element.33.got_own, f32[128,128]{1,0:T(8,128)S(1)} %slice.43.got_pair, ...), custom_call_target="tpu_custom_call" | custom-call | tf_op jit(solution)/shard_map/down/pallas_call | solution.py:300
  38.6 0.5 collective-permute-start.11
  39.1 6.5 %collective-permute-done.11 = bf16[4,192,128]{2,1,0:T(8,128)(2,1)S(1)} collective-permute-done((bf16[4,192,128]{2,1,0:T(8,128)(2,1)S(1)}, bf16[4,192,128]{2,1,0:T(8,128)(2,1)S(1)}, u32[]{:S(2)}, u32[]{:S(2)}) %collective-permute-start.11) | collective-permute-done | bytes 196640 | tf_op jit(solution)/shard_map/ppermute | solution.py:182
  45.7 1.6 %collective-permute-start.12 = (bf16[2,192,128]{2,1,0:T(8,128)(2,1)S(1)}, bf16[2,192,128]{2,1,0:T(8,128)(2,1)S(1)}, u32[]{:S(2)}, u32[]{:S(2)}) collective-permute-start(bf16[2,192,128]{2,1,0:T(8,128)(2,1)S(1)} %fusion.2), channel_id=1, source_target_pairs={{0,8},{4,12},{8,0},{12,4},{16,24},{20,28},{24,16},{28,20},{1,9},{5... | collective-permute-start | bytes 294920 | tf_op jit(solution)/shard_map/ppermute | solution.py:182
  47.3 3.0 %collective-permute-done.12 = bf16[2,192,128]{2,1,0:T(8,128)(2,1)S(1)} collective-permute-done((bf16[2,192,128]{2,1,0:T(8,128)(2,1)S(1)}, bf16[2,192,128]{2,1,0:T(8,128)(2,1)S(1)}, u32[]{:S(2)}, u32[]{:S(2)}) %collective-permute-start.12) | collective-permute-done | bytes 98336 | tf_op jit(solution)/shard_map/ppermute | solution.py:182
  50.4 2.6 %collective-permute-start.13 = (bf16[1,192,128]{2,1,0:T(8,128)(2,1)S(1)}, bf16[1,192,128]{2,1,0:T(8,128)(2,1)S(1)}, u32[]{:S(2)}, u32[]{:S(2)}) collective-permute-start(bf16[1,192,128]{2,1,0:T(8,128)(2,1)S(1)} %fusion.5), channel_id=1, source_target_pairs={{0,16},{4,20},{8,24},{12,28},{16,0},{20,4},{24,8},{28,12},{1,17},{... | collective-permute-start | bytes 147464 | tf_op jit(solution)/shard_map/ppermute | solution.py:182
  53.1 2.4 %collective-permute-done.13.got = bf16[1,192,128]{2,1,0:T(8,128)(2,1)S(1)} collective-permute-done((bf16[1,192,128]{2,1,0:T(8,128)(2,1)S(1)}, bf16[1,192,128]{2,1,0:T(8,128)(2,1)S(1)}, u32[]{:S(2)}, u32[]{:S(2)}) %collective-permute-start.13) | collective-permute-done | bytes 49184 | tf_op jit(solution)/shard_map/ppermute | solution.py:182
  55.5 0.7 %final.1 = (f32[128,128]{1,0:T(8,128)}, f32[64,80]{1,0:T(8,128)}) custom-call(f32[1,192,128]{2,1,0:T(8,128)S(1)} %slice_bitcast_fusion.kept, bf16[1,192,128]{2,1,0:T(8,128)(2,1)S(1)} %collective-permute-done.13.got), custom_call_target="tpu_custom_call" | custom-call | tf_op jit(solution)/shard_map/final/pallas_call | solution.py:320
  (22 shorter events, 0.8 us)
Async XLA Ops:
  2.0 6.0 %collective-permute-start = (bf16[128,768]{1,0:T(8,128)(2,1)S(1)}, bf16[128,768]{1,0:T(8,128)(2,1)S(1)}, u32[]{:S(2)}, u32[]{:S(2)}) collective-permute-start(bf16[128,768]{1,0:T(8,128)(2,1)S(1)} %get-tuple-element.24), channel_id=1, source_target_pairs={{0,1},{1,0},{2,3},{3,2},{4,5},{5,4},{6,7},{7,6},{8,9},{9,8},{10,11... | collective-permute-start | bytes 589832 | tf_op jit(solution)/shard_map/ppermute | solution.py:182
  2.5 8.3 %collective-permute-start.1 = (bf16[128,768]{1,0:T(8,128)(2,1)S(1)}, bf16[128,768]{1,0:T(8,128)(2,1)S(1)}, u32[]{:S(2)}, u32[]{:S(2)}) collective-permute-start(bf16[128,768]{1,0:T(8,128)(2,1)S(1)} %get-tuple-element.25), channel_id=1, source_target_pairs={{0,2},{1,3},{2,0},{3,1},{4,6},{5,7},{6,4},{7,5},{8,10},{9,11},{10,... | collective-permute-start | bytes 589832 | tf_op jit(solution)/shard_map/ppermute | solution.py:182
  5.1 9.4 %collective-permute-start.2 = (bf16[128,768]{1,0:T(8,128)(2,1)S(1)}, bf16[128,768]{1,0:T(8,128)(2,1)S(1)}, u32[]{:S(2)}, u32[]{:S(2)}) collective-permute-start(bf16[128,768]{1,0:T(8,128)(2,1)S(1)} %get-tuple-element.26), channel_id=1, source_target_pairs={{0,3},{1,2},{2,1},{3,0},{4,7},{5,6},{6,5},{7,4},{8,11},{9,10},{10,... | collective-permute-start | bytes 589832 | tf_op jit(solution)/shard_map/ppermute | solution.py:182
  17.5 1.6 %collective-permute-start.3 = (f32[512,128]{1,0:T(8,128)S(1)}, f32[512,128]{1,0:T(8,128)S(1)}, u32[]{:S(2)}, u32[]{:S(2)}) collective-permute-start(f32[512,128]{1,0:T(8,128)S(1)} %get-tuple-element.32), channel_id=1, source_target_pairs={{0,1},{1,0},{2,3},{3,2},{4,5},{5,4},{6,7},{7,6},{8,9},{9,8},{10,11... | collective-permute-start | bytes 786440 | tf_op jit(solution)/shard_map/ppermute | solution.py:182
  19.1 4.0 %collective-permute-start.4 = (bf16[1,128,128]{2,1,0:T(8,128)(2,1)S(1)}, bf16[1,128,128]{2,1,0:T(8,128)(2,1)S(1)}, u32[]{:S(2)}, u32[]{:S(2)}) collective-permute-start(bf16[1,128,128]{2,1,0:T(8,128)(2,1)S(1)} %fusion.6), channel_id=1, source_target_pairs={{0,2},{1,3},{2,0},{3,1},{4,6},{5,7},{6,4},{7,5},{8,10},{9,11},{10,... | collective-permute-start | bytes 98312 | tf_op jit(solution)/shard_map/ppermute | solution.py:182
  20.6 15.7 %collective-permute-start.8 = (bf16[128,1024]{1,0:T(8,128)(2,1)S(1)}, bf16[128,1024]{1,0:T(8,128)(2,1)S(1)}, u32[]{:S(2)}, u32[]{:S(2)}) collective-permute-start(bf16[128,1024]{1,0:T(8,128)(2,1)S(1)} %get-tuple-element.36), channel_id=1, source_target_pairs={{0,1},{1,0},{2,3},{3,2},{4,5},{5,4},{6,7},{7,6},{8,9},{9,8},{10,11... | collective-permute-start | bytes 786440 | tf_op jit(solution)/shard_map/ppermute | solution.py:182
  20.7 15.6 %collective-permute-start.9 = (bf16[128,1024]{1,0:T(8,128)(2,1)S(1)}, bf16[128,1024]{1,0:T(8,128)(2,1)S(1)}, u32[]{:S(2)}, u32[]{:S(2)}) collective-permute-start(bf16[128,1024]{1,0:T(8,128)(2,1)S(1)} %get-tuple-element.37), channel_id=1, source_target_pairs={{0,4},{4,0},{8,12},{12,8},{16,20},{20,16},{24,28},{28,24},{1,5},{5... | collective-permute-start | bytes 786440 | tf_op jit(solution)/shard_map/ppermute | solution.py:182
  22.2 14.1 %collective-permute-start.10 = (bf16[128,1024]{1,0:T(8,128)(2,1)S(1)}, bf16[128,1024]{1,0:T(8,128)(2,1)S(1)}, u32[]{:S(2)}, u32[]{:S(2)}) collective-permute-start(bf16[128,1024]{1,0:T(8,128)(2,1)S(1)} %get-tuple-element.38), channel_id=1, source_target_pairs={{0,5},{1,4},{2,7},{3,6},{4,1},{5,0},{6,3},{7,2},{8,13},{9,12},{10,... | collective-permute-start | bytes 786440 | tf_op jit(solution)/shard_map/ppermute | solution.py:186
  23.1 13.1 %collective-permute-start.5 = (bf16[1,128,128]{2,1,0:T(8,128)(2,1)S(1)}, bf16[1,128,128]{2,1,0:T(8,128)(2,1)S(1)}, u32[]{:S(2)}, u32[]{:S(2)}) collective-permute-start(bf16[1,128,128]{2,1,0:T(8,128)(2,1)S(1)} %fusion.4), channel_id=1, source_target_pairs={{0,4},{4,0},{8,12},{12,8},{16,20},{20,16},{24,28},{28,24},{1,5},{5... | collective-permute-start | bytes 98312 | tf_op jit(solution)/shard_map/ppermute | solution.py:182
  24.7 12.4 %collective-permute-start.7 = (bf16[256,128]{1,0:T(8,128)(2,1)S(1)}, bf16[256,128]{1,0:T(8,128)(2,1)S(1)}, u32[]{:S(2)}, u32[]{:S(2)}) collective-permute-start(bf16[256,128]{1,0:T(8,128)(2,1)S(1)} %pad_maximum_fusion.1), channel_id=1, source_target_pairs={{0,4},{4,0},{8,12},{12,8},{16,20},{20,16},{24,28},{28,24},{1,5},{5... | collective-permute-start | bytes 196616 | tf_op jit(solution)/shard_map/ppermute | solution.py:182
  36.2 1.3 %collective-permute-start.6 = (bf16[2,128,128]{2,1,0:T(8,128)(2,1)S(1)}, bf16[2,128,128]{2,1,0:T(8,128)(2,1)S(1)}, u32[]{:S(2)}, u32[]{:S(2)}) collective-permute-start(bf16[2,128,128]{2,1,0:T(8,128)(2,1)S(1)} %pad_maximum_fusion.low_pair), channel_id=1, source_target_pairs={{0,1},{1,0},{2,3},{3,2},{4,5},{5,4},{6,7},{7,6},{8,9},{9,8},{10,11... | collective-permute-start | bytes 196616 | tf_op jit(solution)/shard_map/ppermute | solution.py:182
  38.6 7.0 %collective-permute-start.11 = (bf16[4,192,128]{2,1,0:T(8,128)(2,1)S(1)}, bf16[4,192,128]{2,1,0:T(8,128)(2,1)S(1)}, u32[]{:S(2)}, u32[]{:S(2)}) collective-permute-start(bf16[4,192,128]{2,1,0:T(8,128)(2,1)S(1)} %get-tuple-element.41), channel_id=1, source_target_pairs={{0,2},{1,3},{2,0},{3,1},{4,6},{5,7},{6,4},{7,5},{8,10},{9,11},{10,... | collective-permute-start | bytes 589832 | tf_op jit(solution)/shard_map/ppermute | solution.py:182
  45.7 4.7 %collective-permute-start.12 = (bf16[2,192,128]{2,1,0:T(8,128)(2,1)S(1)}, bf16[2,192,128]{2,1,0:T(8,128)(2,1)S(1)}, u32[]{:S(2)}, u32[]{:S(2)}) collective-permute-start(bf16[2,192,128]{2,1,0:T(8,128)(2,1)S(1)} %fusion.2), channel_id=1, source_target_pairs={{0,8},{4,12},{8,0},{12,4},{16,24},{20,28},{24,16},{28,20},{1,9},{5... | collective-permute-start | bytes 294920 | tf_op jit(solution)/shard_map/ppermute | solution.py:182
  50.4 5.1 %collective-permute-start.13 = (bf16[1,192,128]{2,1,0:T(8,128)(2,1)S(1)}, bf16[1,192,128]{2,1,0:T(8,128)(2,1)S(1)}, u32[]{:S(2)}, u32[]{:S(2)}) collective-permute-start(bf16[1,192,128]{2,1,0:T(8,128)(2,1)S(1)} %fusion.5), channel_id=1, source_target_pairs={{0,16},{4,20},{8,24},{12,28},{16,0},{20,4},{24,8},{28,12},{1,17},{... | collective-permute-start | bytes 147464 | tf_op jit(solution)/shard_map/ppermute | solution.py:182

commit v3 on v2

--- a/solution.py
+++ b/solution.py
@@ -19,31 +19,22 @@
 
 def owner_tables(C, Dp, W, Wk, DH, q_width, group_cols, rows_total, lane_block, lanes):
     rows_each = rows_total // (C * Dp)
-    local = []
+    local, groups = [], []
     for c in range(C):
         k_start = q_width + (c * W // group_cols) * DH
         local.append(np.concatenate([c * W + np.arange(W), k_start + np.arange(Wk)]))
-
-    def chosen(c, core, y):
-        owner = local[c] // rows_each
-        return np.nonzero((owner % C % 2 == core) & (owner // C % 2 == y))[0]
-
-    most = max(len(chosen(c, core, y)) for c in range(C) for core in (0, 1) for y in (0, 1))
-    slot = -(-most // lanes) * lanes
-    pack = np.full((C, 2, 4, slot), -1, np.int32)
-    land = np.full((C, 2, 4, slot), -1, np.int32)
+        groups.append([np.nonzero(local[c] // rows_each // C % 4 == m)[0] for m in range(4)])
+    slot = -(-max(len(g) for four in groups for g in four) // lanes) * lanes
+    pack = np.full((C, 4, 4, slot), -1, np.int32)
+    land = np.full((C, 4, slot), -1, np.int32)
     for c in range(C):
-        for y in (0, 1):
+        for m in range(4):
+            rows = local[c][groups[c][m]]
+            owner = rows // rows_each
+            land[c, m, : len(rows)] = (owner // C // 4 * C + owner % C) * lane_block + rows % rows_each
             for n in range(4):
-                there, across = n % 2, n // 2
-                rows = chosen(c, c % 2 ^ there, y ^ across)
-                pack[c, y, n, : len(rows)] = rows
-                src = c ^ there
-                rows = local[src][chosen(src, c % 2, y)]
-                owner = rows // rows_each
-                block = (owner // C // 2) * (C // 2) + owner % C // 2
-                land[c, y, n, : len(rows)] = block * lane_block + rows % rows_each
-    return pack.reshape(C * 2, 4 * slot), land.reshape(C * 2, 4 * slot), slot, rows_each
+                pack[c, m, n, : len(groups[c][m ^ n])] = groups[c][m ^ n]
+    return pack.reshape(C * 4, 4 * slot), land.reshape(C * 4, slot), slot, rows_each
 
 
 def slice_kernel(plan, n_in, *refs):
@@ -75,11 +66,10 @@
 
 def attend_kernel(C, tok, hq, kh, DH, H, R, lengths, *refs):
     msgs = refs[:C]
-    teacher, up_q, up_k, pack = refs[C : C + 4]
-    keep_out, send_out, packed_own, packed_far = refs[C + 4 : C + 8]
-    q_buf, k_buf, a_buf, dq_buf, dk_buf, low_buf = refs[C + 8 :]
+    teacher, up_q, up_k = refs[C : C + 3]
+    keep_out, send_out, dq_buf, dk_out, q_buf, k_buf, dk_buf, low_buf = refs[C + 3 :]
     me, length = lax.axis_index("ctx"), lengths[0]
-    W, Wk = hq * DH, kh * DH
+    W = hq * DH
     per_key = hq // kh
     scale = 1.0 / math.sqrt(DH)
     exp_scale = scale * math.log2(math.e)
@@ -87,8 +77,7 @@
         row = pl.multiple_of(jnp.bitwise_xor(me, s) * tok, tok)
         for h in range(hq):
             q_buf[h, pl.ds(row, tok), :] = msgs[s][:, h * DH : (h + 1) * DH]
-        k_buf[pl.ds(row, tok), :] = msgs[s][:, W : W + Wk]
-        a_buf[pl.ds(row, tok), :] = msgs[s][:, W + Wk :]
+        k_buf[pl.ds(row, tok), :] = msgs[s][:, W:]
     dk_buf[...] = jnp.zeros_like(dk_buf)
     row_in = lax.broadcasted_iota(jnp.int32, (tok, 1), 0)
     col_in = lax.broadcasted_iota(jnp.int32, (tok, tok), 1)
@@ -122,48 +111,47 @@
             dk_buf[g * DH : (g + 1) * DH, :ext] += dot32(q_all, grad, TN)
     dq = dq_buf[...]
     dk = (dk_buf[...] * scale).astype(jnp.bfloat16)
+    dk_out[...] = dk
     low_buf[:R, :] = dot32(up_q[...], dq, NT)
     low_buf[R:, :] = dot32(up_k[...], dk)
-    far, mine = jnp.right_shift(me, 1), jnp.bitwise_and(me, 1)
-    for n in range(C // 2):
-        here = jnp.bitwise_xor(far, n) * 2
-        keep_out[n] = low_buf[:, pl.ds(pl.multiple_of((here + mine) * tok, tok), tok)]
-        send_out[n * 2 * R : (n + 1) * 2 * R, :] = low_buf[:, pl.ds(pl.multiple_of((here + 1 - mine) * tok, tok), tok)]
+    for s in range(C):
+        pos = pl.multiple_of(jnp.bitwise_xor(me, s) * tok, tok)
+        (send_out if s % 2 else keep_out)[s // 2] = low_buf[:, pl.ds(pos, tok)]
+
+
+def up_kernel(C, tok, R, *refs):
+    adapters = refs[:C]
+    dq, dk, pack, keep, send, a_buf = refs[C:]
+    me, me_d = lax.axis_index("ctx"), lax.axis_index("dp")
+    for s in range(C):
+        a_buf[pl.ds(pl.multiple_of(jnp.bitwise_xor(me, s) * tok, tok), tok), :] = adapters[s][...]
     a_q, a_k = a_buf[:, :R], a_buf[:, R:]
     grad_up = jnp.concatenate(
-        [dot32(a_q, dq, TN).astype(jnp.bfloat16), dot32(a_k.T, dk, NT).astype(jnp.bfloat16)], axis=1
+        [dot32(a_q, dq[...], TN).astype(jnp.bfloat16), dot32(a_k.T, dk[...], NT).astype(jnp.bfloat16)], axis=1
     )
-    where_to = pack[pl.ds(me * 2 + jnp.bitwise_and(lax.axis_index("dp"), 1), 1), :]
+    where_to = pack[pl.ds(me * 4 + jnp.bitwise_and(me_d, 3), 1), :]
     pick = lax.broadcasted_iota(jnp.int32, (grad_up.shape[1], where_to.shape[1]), 0) == where_to
     pick = jnp.where(pick, 1.0, 0.0).astype(jnp.bfloat16)
     rows = dot32(grad_up, pick)
-    blks = where_to.shape[1] // 4 // tok
-    for n in range(4 * blks):
-        to, part = n // blks, n % blks
-        dst = (packed_own, send_out, packed_far, send_out)[to]
-        at = (0, C * R, 0, C * R + blks * R)[to] + part * R
-        dst[at : at + R, :] = rows[:, n * tok : (n + 1) * tok].astype(dst.dtype)
-
-
-def down_kernel(R, rblk, low_pair, low_other, got_own, got_pair, got_far, h0, h1, h2, h3, land, send, keep):
-    lows = (low_pair[0], low_other[0], low_pair[1], low_other[1])
+    slot = where_to.shape[1] // 4
+    for n in range(4):
+        dst = send if n // 2 else keep
+        dst[n % 2] = rows[:, n * slot : (n + 1) * slot].astype(dst.dtype)
+
+
+def down_kernel(R, rblk, low_a, low_b, ups_a, ups_b, h0, h1, h2, h3, land, send, keep):
     acc = None
-    for low, hid in zip(lows, (h0, h1, h2, h3)):
+    for low, hid in zip((low_a[0], low_a[1], low_b[0], low_b[1]), (h0, h1, h2, h3)):
         term = dot32(low, hid[...])
         acc = term if acc is None else acc + term
-    blks = got_own.shape[0] // R
-    pieces = [got_own[n * R : (n + 1) * R, :] for n in range(blks)]
-    pieces += [got_pair[n * R : (n + 1) * R, :].astype(jnp.bfloat16) for n in range(blks)]
-    pieces += [got_far[n * R : (n + 1) * R, :] for n in range(2 * blks)]
-    rows = jnp.concatenate(pieces, axis=1)
-    me, me_d = lax.axis_index("ctx"), lax.axis_index("dp")
-    half_c = lax.axis_size("ctx") // 2
-    here = jnp.right_shift(me_d, 1) * half_c + jnp.right_shift(me, 1)
-    where_to = jnp.bitwise_xor(land[pl.ds(me * 2 + jnp.bitwise_and(me_d, 1), 1), :], here * rblk)
-    place = lax.broadcasted_iota(jnp.int32, (h0.shape[1], rows.shape[1]), 0) == where_to
+    rows = (ups_a[...] + ups_b[...].astype(jnp.float32)).astype(jnp.bfloat16)
+    me, me_d, width = lax.axis_index("ctx"), lax.axis_index("dp"), h0.shape[1]
+    here = jnp.right_shift(me_d, 2) * lax.axis_size("ctx") + me
+    where_to = jnp.bitwise_xor(land[pl.ds(me * 4 + jnp.bitwise_and(me_d, 3), 1), :], here * rblk)
+    place = lax.broadcasted_iota(jnp.int32, (width, rows.shape[1]), 0) == where_to
     place = jnp.where(place, 1.0, 0.0).astype(jnp.bfloat16)
     ups = dot32(rows, place, NT)
-    for e in range(h0.shape[1] // rblk):
+    for e in range(width // rblk):
         dst = send if e % 2 else keep
         dst[e // 2, : 2 * R, :] = acc[:, e * rblk : (e + 1) * rblk].astype(dst.dtype)
         dst[e // 2, 2 * R :, :] = ups[:, e * rblk : (e + 1) * rblk].astype(dst.dtype)
@@ -180,10 +168,6 @@
 
     def swap(x, s, axis="ctx"):
         return lax.ppermute(x, axis, [(i, i ^ s) for i in range(mesh.shape[axis])])
-
-    def swap_diag(x):
-        pairs = [(d * C + c, (d ^ 1) * C + (c ^ 1)) for d in range(Dp) for c in range(C)]
-        return lax.ppermute(x, ("dp", "ctx"), pairs)
 
     def near(x):
         return pltpu.with_memory_space_constraint(x, pltpu.VMEM)
@@ -213,7 +197,6 @@
                 dst = jnp.bitwise_xor(me, s)
                 yield 0, pl.multiple_of(dst * W, 128), s, 0, W
                 yield 1, pl.multiple_of(key_col(dst), 128), s, W, Wk
-                yield 2, 0, s, W + Wk, 2 * R
 
         def second_plan(me, me_d):
             yield 0, None, 0, None, None
@@ -229,14 +212,14 @@
         E = C * Dp // 4
 
         def column(me, me_d, n, e):
-            d = jnp.bitwise_xor(me_d, n // 2 + e // (C // 2) * 2)
-            return (d * C + jnp.bitwise_xor(me, n % 2 + e % (C // 2) * 2)) * rblk
+            return (jnp.bitwise_xor(me_d, n + e // C * 4) * C + jnp.bitwise_xor(me, e % C)) * rblk
 
         pack, land, slot, rows_each = owner_tables(C, Dp, W, Wk, DH, q_width, group_cols, rows_total, rblk, tok)
         pack, land = jnp.asarray(pack), jnp.asarray(land)
-        msgs = list(slices(first_plan, 3 * C, (queries[0], keys[0], adapter[0]), [pltpu.VMEM((tok, W + Wk + 2 * R), bf)] * C))
+        msgs = list(slices(first_plan, 2 * C, (queries[0], keys[0]), [pltpu.VMEM((tok, W + Wk), bf)] * C))
         for s in range(1, C):
             msgs[s] = swap(msgs[s], s)
+        adapters = [adapter[0]] + [swap(adapter[0], s) for s in range(1, C)]
         by_dma = rblk % 128 == 0
         outs = [
             pltpu.VMEM(teacher.shape[1:], bf),
@@ -254,62 +237,60 @@
             for n in range(4):
                 order = jnp.stack([column(me, me_d, n, e) // rblk for e in range(E)])
                 hids.append(jnp.take(blocks, order, axis=1).reshape(tok, E * rblk))
-        hids[1] = swap(hids[1], 1)
-        hids[2] = swap(hids[2], 1, "dp")
-        hids[3] = swap_diag(hids[3])
+        hids = [hids[0]] + [swap(hids[n], n, "dp") for n in range(1, 4)]
 
         smem = pl.BlockSpec(memory_space=pltpu.SMEM)
         vmem = pl.BlockSpec(memory_space=pltpu.VMEM)
         params = pltpu.CompilerParams(vmem_limit_bytes=24 * 2**20)
-        low_rows, piece = C * R, slot // tok * R
-        keep, send, own, even = pl.pallas_call(
+        keep, send, dq, dk = pl.pallas_call(
             functools.partial(attend_kernel, C, tok, hq, kh, DH, H, R),
             out_shape=(
                 pltpu.VMEM((C // 2, 2 * R, tok), f32),
-                pltpu.VMEM((low_rows + 2 * piece, tok), f32),
-                pltpu.VMEM((piece, tok), bf),
-                pltpu.VMEM((piece, tok), bf),
+                pltpu.VMEM((C // 2, 2 * R, tok), f32),
+                pltpu.VMEM((S, W), bf),
+                pltpu.VMEM((Wk, S), bf),
             ),
-            in_specs=[smem] + [vmem] * (C + 4),
+            in_specs=[smem] + [vmem] * (C + 3),
             out_specs=tuple([vmem] * 4),
             scratch_shapes=[
                 pltpu.VMEM((hq, S, DH), bf),
                 pltpu.VMEM((S, Wk), bf),
-                pltpu.VMEM((S, 2 * R), bf),
-                pltpu.VMEM((S, W), bf),
                 pltpu.VMEM((Wk, S), f32),
                 pltpu.VMEM((2 * R, S), f32),
             ],
             compiler_params=params,
             name="attend",
-        )(lengths, *[near(m) for m in msgs], near(teach), near(up_q), near(up_k), near(pack))
-
-        pair = swap(send, 1)
-        low = keep + pair[:low_rows].reshape(keep.shape)
+        )(lengths, *[near(m) for m in msgs], near(teach), near(up_q), near(up_k))
+        low = keep + swap(send, 1)
         bit = 2
         while bit < C:
             both = low.reshape((-1, 2) + low.shape[1:])
             low = both[:, 0] + swap(both[:, 1].astype(bf), bit).astype(f32)
             bit *= 2
-        relay = pair[low_rows + piece :].astype(bf)
-        far = swap(jnp.concatenate([even, relay]), 1, "dp")
+        ups, send = pl.pallas_call(
+            functools.partial(up_kernel, C, tok, R),
+            out_shape=(pltpu.VMEM((2, R, slot), f32), pltpu.VMEM((2, R, slot), bf)),
+            in_specs=[vmem] * (C + 3),
+            out_specs=(vmem, vmem),
+            scratch_shapes=[pltpu.VMEM((S, 2 * R), bf)],
+            compiler_params=params,
+            name="upgrad",
+        )(*[near(a) for a in adapters], near(dq), near(dk), near(pack))
+        ups = ups + swap(send, 2, "dp").astype(f32)
         low = low.astype(bf)
         low = jnp.concatenate([low, swap(low, 1, "dp")])
-        other = swap(low, 1)
-
+        got = swap(ups[1].astype(bf), 1, "dp")
+        other = swap(low, 2, "dp")
         send, keep = pl.pallas_call(
             functools.partial(down_kernel, R, rblk),
             out_shape=(pltpu.VMEM((E // 2, 3 * R, rblk), bf), pltpu.VMEM((E // 2, 3 * R, rblk), f32)),
-            in_specs=[vmem] * 10,
+            in_specs=[vmem] * 9,
             out_specs=(vmem, vmem),
             compiler_params=params,
             name="down",
-        )(
-            near(low), near(other), near(own), near(pair[low_rows : low_rows + piece]), near(far),
-            *[near(h) for h in hids], near(land),
-        )
-        rounds = [("ctx", 2 << i) for i in range(C.bit_length() - 2)]
-        rounds += [("dp", 2 << i) for i in range(Dp.bit_length() - 2)]
+        )(*[near(x) for x in (low, other, ups[0], got, *hids, land)])
+        rounds = [("ctx", 1 << i) for i in range(C.bit_length() - 1)]
+        rounds += [("dp", 4 << i) for i in range(Dp.bit_length() - 3)]
         for n, (axis, bit) in enumerate(rounds):
             if n:
                 both = keep.reshape((-1, 2) + keep.shape[1:])

time: 56.4 us -> 57 us (1.011)
  starting transfers between devices: 13.7 us -> 20.6 us
  waiting for transfers between devices: 32.7 us -> 26.4 us
    ppermute x13 -> x18, starting transfers between devices: 13.4 us -> 20.6 us  [swap(): return lax.ppermute(x, axis, [(i, i ^ s) for i in range(mesh.shape[axis])])]
    ppermute x13 -> x18, waiting for transfers between devices: 32.7 us -> 26.4 us  [swap(): return lax.ppermute(x, axis, [(i, i ^ s) for i in range(mesh.shape[axis])])]
    pallas_call x0 -> x1, Pallas kernels: none -> 0.71 us  [body(): pl.pallas_call(functools.partial(up_kernel, C, tok, R), out_shape=(pltpu....]
  transfers between devices with their start and end apart: 14 -> 18, of which waited for: 10 -> 8; matrix products, arithmetic and copies ran while one was open for 0% -> 0% of each run, Pallas kernels for 4% -> 5%
where the time goes in v3:
time: 57 us; the launch traced here: 56.8 us
  waiting for transfers between devices  26.4 us (46%)
  starting transfers between devices  20.6 us (36%)
  Pallas kernels  8.15 us (14%)
  between operations  1.45 us (3%)
    ppermute x18, waiting for transfers between devices, swap(): return lax.ppermute(x, axis, [(i, i ^ s) for i in range(mesh.shape[axis])])  26.4 us
    ppermute x18, starting transfers between devices, swap(): return lax.ppermute(x, axis, [(i, i ^ s) for i in range(mesh.shape[axis])])  20.6 us
    pallas_call x2, Pallas kernels, slices(): pl.pallas_call(functools.partial(slice_kernel, plan, len(ins)), out_shape...  3.48 us
    pallas_call x1, Pallas kernels, body(): pl.pallas_call(functools.partial(attend_kernel, C, tok, hq, kh, DH, H, R)...  2.59 us
  transfers between devices with their start and end apart: 18, of which 8 were waited for; matrix products, arithmetic and copies ran while one was open for 0% of the time, Pallas kernels for 5%

profile of v3, /device:TPU:0, one launch (start us, length us, event | category | flops | bytes accessed | tf_op | source)
XLA Modules:
  0.0 56.8 jit_solution(9288612150084596707)
XLA Ops:
  0.6 1.2 %shard_map.104 = (bf16[128,640]{1,0:T(8,128)(2,1)S(1)}, bf16[128,640]{1,0:T(8,128)(2,1)S(1)}, bf16[128,640]{1,0:T(8,128)(2,1)S(1)}, bf16[128,640]{1,0:T(8,128)(2,1)S(1)}) custom-call(bf16[128,2048]{1,0:T(8,128)(2,1)} %bitcast.44, bf16[128,512]{1,0:T(8,128)(2,1)} %bitcast.46), custom_call_target="tpu_custom_call" | custom-call | tf_op jit(solution)/shard_map/pallas_call | solution.py:57
  2.4 2.6 %collective-permute-start.1 = (bf16[128,640]{1,0:T(8,128)(2,1)S(1)}, bf16[128,640]{1,0:T(8,128)(2,1)S(1)}, u32[]{:S(2)}, u32[]{:S(2)}) collective-permute-start(bf16[128,640]{1,0:T(8,128)(2,1)S(1)} %get-tuple-element.27), channel_id=1, source_target_pairs={{0,2},{1,3},{2,0},{3,1},{4,6},{5,7},{6,4},{7,5},{8,10},{9,11},{10,... | collective-permute-start | bytes 491528 | tf_op jit(solution)/shard_map/ppermute | solution.py:170
  5.7 2.2 %shard_map.105 = (bf16[4,512,512]{2,1,0:T(8,128)(2,1)S(1)}, bf16[64,512]{1,0:T(8,128)(2,1)S(1)}, bf16[64,128]{1,0:T(8,128)(2,1)S(1)}, s32[16,1536]{1,0:T(8,128)S...) custom-call(bf16[4,512,512]{2,1,0:T(8,128)(2,1)} %bitcast.40, ...), custom_call_target="tpu_custom_call" | custom-call | tf_op jit(solution)/shard_map/pallas_call | solution.py:57
  7.9 2.1 %collective-permute-done.1.refs_2_ = bf16[128,640]{1,0:T(8,128)(2,1)S(1)} collective-permute-done((bf16[128,640]{1,0:T(8,128)(2,1)S(1)}, bf16[128,640]{1,0:T(8,128)(2,1)S(1)}, u32[]{:S(2)}, u32[]{:S(2)}) %collective-permute-start.1) | collective-permute-done | bytes 163872 | tf_op jit(solution)/shard_map/ppermute | solution.py:170
  10.0 3.0 %collective-permute-done.2.refs_3_ = bf16[128,640]{1,0:T(8,128)(2,1)S(1)} collective-permute-done((bf16[128,640]{1,0:T(8,128)(2,1)S(1)}, bf16[128,640]{1,0:T(8,128)(2,1)S(1)}, u32[]{:S(2)}, u32[]{:S(2)}) %collective-permute-start.2) | collective-permute-done | bytes 163872 | tf_op jit(solution)/shard_map/ppermute | solution.py:170
  13.0 2.6 %attend.1 = (f32[2,128,128]{2,1,0:T(8,128)S(1)}, f32[2,128,128]{2,1,0:T(8,128)S(1)}, bf16[512,512]{1,0:T(8,128)(2,1)S(1)}, bf16[128,512]{1,0:T(8,128)(2,1)S(1)}) custom-call(s32[1]{0:T(128)S(6)} %copy.23.lengths, bf16[128,640]{1,0:T(8,128)(2,1)S(1)} %get-tuple-element.25.refs_0_, bf16[128,640]{1,0:T(8,128)(2,1)S(1)} %collective-permute-done.refs_1_, ...), custom_call_target="tpu_custom_call" | custom-call | tf_op jit(solution)/shard_map/attend/pallas_call | solution.py:245
  16.2 1.5 %collective-permute-start.8 = (bf16[128,128]{1,0:T(8,128)(2,1)S(1)}, bf16[128,128]{1,0:T(8,128)(2,1)S(1)}, u32[]{:S(2)}, u32[]{:S(2)}) collective-permute-start(bf16[128,128]{1,0:T(8,128)(2,1)S(1)} %bitcast.37), channel_id=1, source_target_pairs={{0,2},{1,3},{2,0},{3,1},{4,6},{5,7},{6,4},{7,5},{8,10},{9,11},{10,... | collective-permute-start | bytes 98312 | tf_op jit(solution)/shard_map/ppermute | solution.py:170
  17.7 1.7 %collective-permute-start.12 = (bf16[128,1024]{1,0:T(8,128)(2,1)S(1)}, bf16[128,1024]{1,0:T(8,128)(2,1)S(1)}, u32[]{:S(2)}, u32[]{:S(2)}) collective-permute-start(bf16[128,1024]{1,0:T(8,128)(2,1)S(1)} %get-tuple-element.40), channel_id=1, source_target_pairs={{0,4},{4,0},{8,12},{12,8},{16,20},{20,16},{24,28},{28,24},{1,5},{5... | collective-permute-start | bytes 786440 | tf_op jit(solution)/shard_map/ppermute | solution.py:170
  19.4 1.6 %collective-permute-start.13 = (bf16[128,1024]{1,0:T(8,128)(2,1)S(1)}, bf16[128,1024]{1,0:T(8,128)(2,1)S(1)}, u32[]{:S(2)}, u32[]{:S(2)}) collective-permute-start(bf16[128,1024]{1,0:T(8,128)(2,1)S(1)} %get-tuple-element.41), channel_id=1, source_target_pairs={{0,8},{4,12},{8,0},{12,4},{16,24},{20,28},{24,16},{28,20},{1,9},{5... | collective-permute-start | bytes 786440 | tf_op jit(solution)/shard_map/ppermute | solution.py:170
  21.0 1.6 %collective-permute-start.14 = (bf16[128,1024]{1,0:T(8,128)(2,1)S(1)}, bf16[128,1024]{1,0:T(8,128)(2,1)S(1)}, u32[]{:S(2)}, u32[]{:S(2)}) collective-permute-start(bf16[128,1024]{1,0:T(8,128)(2,1)S(1)} %get-tuple-element.42), channel_id=1, source_target_pairs={{0,12},{4,8},{8,4},{12,0},{16,28},{20,24},{24,20},{28,16},{1,13},{... | collective-permute-start | bytes 786440 | tf_op jit(solution)/shard_map/ppermute | solution.py:170
  22.6 0.7 %upgrad.1 = (f32[2,64,384]{2,1,0:T(8,128)S(1)}, bf16[2,64,384]{2,1,0:T(8,128)(2,1)S(1)}) custom-call(bf16[128,128]{1,0:T(8,128)(2,1)S(1)} %bitcast.39, bf16[128,128]{1,0:T(8,128)(2,1)S(1)} %collective-permute-done.7.refs_1_, bf16[128,128]{1,0:T(8,128)(2,1)S(1)} %collective-permute-done.8.refs_2_, bf16[128,128]{1,0:T(8,128)(2,1)S(1)} %collective-permute-done.9.refs_3_, ...), custom_call_target="tpu_custom_call" | custom-call | tf_op jit(solution)/shard_map/upgrad/pallas_call | solution.py:270
  23.9 1.9 %collective-permute-start.4 = (bf16[1,128,128]{2,1,0:T(8,128)(2,1)S(1)}, bf16[1,128,128]{2,1,0:T(8,128)(2,1)S(1)}, u32[]{:S(2)}, u32[]{:S(2)}) collective-permute-start(bf16[1,128,128]{2,1,0:T(8,128)(2,1)S(1)} %fusion.7), channel_id=1, source_target_pairs={{0,2},{1,3},{2,0},{3,1},{4,6},{5,7},{6,4},{7,5},{8,10},{9,11},{10,... | collective-permute-start | bytes 98312 | tf_op jit(solution)/shard_map/ppermute | solution.py:170
  25.8 9.7 %collective-permute-done.10 = bf16[2,64,384]{2,1,0:T(8,128)(2,1)S(1)} collective-permute-done((bf16[2,64,384]{2,1,0:T(8,128)(2,1)S(1)}, bf16[2,64,384]{2,1,0:T(8,128)(2,1)S(1)}, u32[]{:S(2)}, u32[]{:S(2)}) %collective-permute-start.10) | collective-permute-done | bytes 98336 | tf_op jit(solution)/shard_map/ppermute | solution.py:170
  36.2 1.6 %collective-permute-start.11 = (bf16[64,384]{1,0:T(8,128)(2,1)S(1)}, bf16[64,384]{1,0:T(8,128)(2,1)S(1)}, u32[]{:S(2)}, u32[]{:S(2)}) collective-permute-start(bf16[64,384]{1,0:T(8,128)(2,1)S(1)} %fusion.5), channel_id=1, source_target_pairs={{0,4},{4,0},{8,12},{12,8},{16,20},{20,16},{24,28},{28,24},{1,5},{5... | collective-permute-start | bytes 147464 | tf_op jit(solution)/shard_map/ppermute | solution.py:170
  37.7 1.8 %collective-permute-done.5 = bf16[1,128,128]{2,1,0:T(8,128)(2,1)S(1)} collective-permute-done((bf16[1,128,128]{2,1,0:T(8,128)(2,1)S(1)}, bf16[1,128,128]{2,1,0:T(8,128)(2,1)S(1)}, u32[]{:S(2)}, u32[]{:S(2)}) %collective-permute-start.5) | collective-permute-done | bytes 32800 | tf_op jit(solution)/shard_map/ppermute | solution.py:170
  39.5 1.6 %collective-permute-start.6 = (bf16[2,128,128]{2,1,0:T(8,128)(2,1)S(1)}, bf16[2,128,128]{2,1,0:T(8,128)(2,1)S(1)}, u32[]{:S(2)}, u32[]{:S(2)}) collective-permute-start(bf16[2,128,128]{2,1,0:T(8,128)(2,1)S(1)} %pad_maximum_fusion.low_a), channel_id=1, source_target_pairs={{0,8},{4,12},{8,0},{12,4},{16,24},{20,28},{24,16},{28,20},{1,9},{5... | collective-permute-start | bytes 196616 | tf_op jit(solution)/shard_map/ppermute | solution.py:170
  41.2 2.6 %collective-permute-done.6.low_b = bf16[2,128,128]{2,1,0:T(8,128)(2,1)S(1)} collective-permute-done((bf16[2,128,128]{2,1,0:T(8,128)(2,1)S(1)}, bf16[2,128,128]{2,1,0:T(8,128)(2,1)S(1)}, u32[]{:S(2)}, u32[]{:S(2)}) %collective-permute-start.6) | collective-permute-done | bytes 65568 | tf_op jit(solution)/shard_map/ppermute | solution.py:170
  43.9 0.6 %down.1 = (bf16[4,192,128]{2,1,0:T(8,128)(2,1)S(1)}, f32[4,192,128]{2,1,0:T(8,128)S(1)}) custom-call(bf16[2,128,128]{2,1,0:T(8,128)(2,1)S(1)} %pad_maximum_fusion.low_a, bf16[2,128,128]{2,1,0:T(8,128)(2,1)S(1)} %collective-permute-done.6.low_b, f32[64,384]{1,0:T(8,128)S(1)} %slice_bitcast_fusion.1.ups_a, bf16[64,384]{1,0:T(8,128)(2,1)S(1)} %collective-permute-done.11.ups_b, ...), custom_call_target="tpu_custom_call" | custom-call | tf_op jit(solution)/shard_map/down/pallas_call | solution.py:284
  44.6 1.4 %collective-permute-done.15 = bf16[4,192,128]{2,1,0:T(8,128)(2,1)S(1)} collective-permute-done((bf16[4,192,128]{2,1,0:T(8,128)(2,1)S(1)}, bf16[4,192,128]{2,1,0:T(8,128)(2,1)S(1)}, u32[]{:S(2)}, u32[]{:S(2)}) %collective-permute-start.15) | collective-permute-done | bytes 196640 | tf_op jit(solution)/shard_map/ppermute | solution.py:170
  46.1 1.6 %collective-permute-start.16 = (bf16[2,192,128]{2,1,0:T(8,128)(2,1)S(1)}, bf16[2,192,128]{2,1,0:T(8,128)(2,1)S(1)}, u32[]{:S(2)}, u32[]{:S(2)}) collective-permute-start(bf16[2,192,128]{2,1,0:T(8,128)(2,1)S(1)} %fusion.2), channel_id=1, source_target_pairs={{0,2},{1,3},{2,0},{3,1},{4,6},{5,7},{6,4},{7,5},{8,10},{9,11},{10,... | collective-permute-start | bytes 294920 | tf_op jit(solution)/shard_map/ppermute | solution.py:170
  47.6 3.3 %collective-permute-done.16 = bf16[2,192,128]{2,1,0:T(8,128)(2,1)S(1)} collective-permute-done((bf16[2,192,128]{2,1,0:T(8,128)(2,1)S(1)}, bf16[2,192,128]{2,1,0:T(8,128)(2,1)S(1)}, u32[]{:S(2)}, u32[]{:S(2)}) %collective-permute-start.16) | collective-permute-done | bytes 98336 | tf_op jit(solution)/shard_map/ppermute | solution.py:170
  51.0 2.7 %collective-permute-start.17 = (bf16[1,192,128]{2,1,0:T(8,128)(2,1)S(1)}, bf16[1,192,128]{2,1,0:T(8,128)(2,1)S(1)}, u32[]{:S(2)}, u32[]{:S(2)}) collective-permute-start(bf16[1,192,128]{2,1,0:T(8,128)(2,1)S(1)} %fusion.6), channel_id=1, source_target_pairs={{0,16},{4,20},{8,24},{12,28},{16,0},{20,4},{24,8},{28,12},{1,17},{... | collective-permute-start | bytes 147464 | tf_op jit(solution)/shard_map/ppermute | solution.py:170
  53.7 2.4 %collective-permute-done.17.got = bf16[1,192,128]{2,1,0:T(8,128)(2,1)S(1)} collective-permute-done((bf16[1,192,128]{2,1,0:T(8,128)(2,1)S(1)}, bf16[1,192,128]{2,1,0:T(8,128)(2,1)S(1)}, u32[]{:S(2)}, u32[]{:S(2)}) %collective-permute-start.17) | collective-permute-done | bytes 49184 | tf_op jit(solution)/shard_map/ppermute | solution.py:170
  56.1 0.7 %final.1 = (f32[128,128]{1,0:T(8,128)}, f32[64,80]{1,0:T(8,128)}) custom-call(f32[1,192,128]{2,1,0:T(8,128)S(1)} %slice_bitcast_fusion.kept, bf16[1,192,128]{2,1,0:T(8,128)(2,1)S(1)} %collective-permute-done.17.got), custom_call_target="tpu_custom_call" | custom-call | tf_op jit(solution)/shard_map/final/pallas_call | solution.py:301
  (32 shorter events, 2.6 us)
Async XLA Ops:
  1.9 6.1 %collective-permute-start = (bf16[128,640]{1,0:T(8,128)(2,1)S(1)}, bf16[128,640]{1,0:T(8,128)(2,1)S(1)}, u32[]{:S(2)}, u32[]{:S(2)}) collective-permute-start(bf16[128,640]{1,0:T(8,128)(2,1)S(1)} %get-tuple-element.26), channel_id=1, source_target_pairs={{0,1},{1,0},{2,3},{3,2},{4,5},{5,4},{6,7},{7,6},{8,9},{9,8},{10,11... | collective-permute-start | bytes 491528 | tf_op jit(solution)/shard_map/ppermute | solution.py:170
  2.4 7.6 %collective-permute-start.1 = (bf16[128,640]{1,0:T(8,128)(2,1)S(1)}, bf16[128,640]{1,0:T(8,128)(2,1)S(1)}, u32[]{:S(2)}, u32[]{:S(2)}) collective-permute-start(bf16[128,640]{1,0:T(8,128)(2,1)S(1)} %get-tuple-element.27), channel_id=1, source_target_pairs={{0,2},{1,3},{2,0},{3,1},{4,6},{5,7},{6,4},{7,5},{8,10},{9,11},{10,... | collective-permute-start | bytes 491528 | tf_op jit(solution)/shard_map/ppermute | solution.py:170
  5.0 8.0 %collective-permute-start.2 = (bf16[128,640]{1,0:T(8,128)(2,1)S(1)}, bf16[128,640]{1,0:T(8,128)(2,1)S(1)}, u32[]{:S(2)}, u32[]{:S(2)}) collective-permute-start(bf16[128,640]{1,0:T(8,128)(2,1)S(1)} %get-tuple-element.28), channel_id=1, source_target_pairs={{0,3},{1,2},{2,1},{3,0},{4,7},{5,6},{6,5},{7,4},{8,11},{9,10},{10,... | collective-permute-start | bytes 491528 | tf_op jit(solution)/shard_map/ppermute | solution.py:170
  7.9 7.9 %copy-start = (bf16[1,128,128]{2,1,0:T(8,128)(2,1)S(1)}, bf16[1,128,128]{2,1,0:T(8,128)(2,1)}, u32[]{:S(2)}) copy-start(bf16[1,128,128]{2,1,0:T(8,128)(2,1)} %param.14) | copy-start | bytes 98308
  15.6 8.2 %collective-permute-start.3 = (f32[2,128,128]{2,1,0:T(8,128)S(1)}, f32[2,128,128]{2,1,0:T(8,128)S(1)}, u32[]{:S(2)}, u32[]{:S(2)}) collective-permute-start(f32[2,128,128]{2,1,0:T(8,128)S(1)} %get-tuple-element.33), channel_id=1, source_target_pairs={{0,1},{1,0},{2,3},{3,2},{4,5},{5,4},{6,7},{7,6},{8,9},{9,8},{10,11... | collective-permute-start | bytes 393224 | tf_op jit(solution)/shard_map/ppermute | solution.py:170
  15.8 3.6 %collective-permute-start.7 = (bf16[128,128]{1,0:T(8,128)(2,1)S(1)}, bf16[128,128]{1,0:T(8,128)(2,1)S(1)}, u32[]{:S(2)}, u32[]{:S(2)}) collective-permute-start(bf16[128,128]{1,0:T(8,128)(2,1)S(1)} %bitcast.36), channel_id=1, source_target_pairs={{0,1},{1,0},{2,3},{3,2},{4,5},{5,4},{6,7},{7,6},{8,9},{9,8},{10,11... | collective-permute-start | bytes 98312 | tf_op jit(solution)/shard_map/ppermute | solution.py:170
  16.2 4.8 %collective-permute-start.8 = (bf16[128,128]{1,0:T(8,128)(2,1)S(1)}, bf16[128,128]{1,0:T(8,128)(2,1)S(1)}, u32[]{:S(2)}, u32[]{:S(2)}) collective-permute-start(bf16[128,128]{1,0:T(8,128)(2,1)S(1)} %bitcast.37), channel_id=1, source_target_pairs={{0,2},{1,3},{2,0},{3,1},{4,6},{5,7},{6,4},{7,5},{8,10},{9,11},{10,... | collective-permute-start | bytes 98312 | tf_op jit(solution)/shard_map/ppermute | solution.py:170
  17.7 5.0 %collective-permute-start.9 = (bf16[128,128]{1,0:T(8,128)(2,1)S(1)}, bf16[128,128]{1,0:T(8,128)(2,1)S(1)}, u32[]{:S(2)}, u32[]{:S(2)}) collective-permute-start(bf16[128,128]{1,0:T(8,128)(2,1)S(1)} %bitcast.38), channel_id=1, source_target_pairs={{0,3},{1,2},{2,1},{3,0},{4,7},{5,6},{6,5},{7,4},{8,11},{9,10},{10,... | collective-permute-start | bytes 98312 | tf_op jit(solution)/shard_map/ppermute | solution.py:170
  17.7 23.5 %collective-permute-start.12 = (bf16[128,1024]{1,0:T(8,128)(2,1)S(1)}, bf16[128,1024]{1,0:T(8,128)(2,1)S(1)}, u32[]{:S(2)}, u32[]{:S(2)}) collective-permute-start(bf16[128,1024]{1,0:T(8,128)(2,1)S(1)} %get-tuple-element.40), channel_id=1, source_target_pairs={{0,4},{4,0},{8,12},{12,8},{16,20},{20,16},{24,28},{28,24},{1,5},{5... | collective-permute-start | bytes 786440 | tf_op jit(solution)/shard_map/ppermute | solution.py:170
  19.4 21.8 %collective-permute-start.13 = (bf16[128,1024]{1,0:T(8,128)(2,1)S(1)}, bf16[128,1024]{1,0:T(8,128)(2,1)S(1)}, u32[]{:S(2)}, u32[]{:S(2)}) collective-permute-start(bf16[128,1024]{1,0:T(8,128)(2,1)S(1)} %get-tuple-element.41), channel_id=1, source_target_pairs={{0,8},{4,12},{8,0},{12,4},{16,24},{20,28},{24,16},{28,20},{1,9},{5... | collective-permute-start | bytes 786440 | tf_op jit(solution)/shard_map/ppermute | solution.py:170
  21.0 20.2 %collective-permute-start.14 = (bf16[128,1024]{1,0:T(8,128)(2,1)S(1)}, bf16[128,1024]{1,0:T(8,128)(2,1)S(1)}, u32[]{:S(2)}, u32[]{:S(2)}) collective-permute-start(bf16[128,1024]{1,0:T(8,128)(2,1)S(1)} %get-tuple-element.42), channel_id=1, source_target_pairs={{0,12},{4,8},{8,4},{12,0},{16,28},{20,24},{24,20},{28,16},{1,13},{... | collective-permute-start | bytes 786440 | tf_op jit(solution)/shard_map/ppermute | solution.py:170
  23.3 12.2 %collective-permute-start.10 = (bf16[2,64,384]{2,1,0:T(8,128)(2,1)S(1)}, bf16[2,64,384]{2,1,0:T(8,128)(2,1)S(1)}, u32[]{:S(2)}, u32[]{:S(2)}) collective-permute-start(bf16[2,64,384]{2,1,0:T(8,128)(2,1)S(1)} %get-tuple-element.38), channel_id=1, source_target_pairs={{0,8},{4,12},{8,0},{12,4},{16,24},{20,28},{24,16},{28,20},{1,9},{5... | collective-permute-start | bytes 294920 | tf_op jit(solution)/shard_map/ppermute | solution.py:170
  23.9 11.6 %collective-permute-start.4 = (bf16[1,128,128]{2,1,0:T(8,128)(2,1)S(1)}, bf16[1,128,128]{2,1,0:T(8,128)(2,1)S(1)}, u32[]{:S(2)}, u32[]{:S(2)}) collective-permute-start(bf16[1,128,128]{2,1,0:T(8,128)(2,1)S(1)} %fusion.7), channel_id=1, source_target_pairs={{0,2},{1,3},{2,0},{3,1},{4,6},{5,7},{6,4},{7,5},{8,10},{9,11},{10,... | collective-permute-start | bytes 98312 | tf_op jit(solution)/shard_map/ppermute | solution.py:170
  35.5 4.0 %collective-permute-start.5 = (bf16[1,128,128]{2,1,0:T(8,128)(2,1)S(1)}, bf16[1,128,128]{2,1,0:T(8,128)(2,1)S(1)}, u32[]{:S(2)}, u32[]{:S(2)}) collective-permute-start(bf16[1,128,128]{2,1,0:T(8,128)(2,1)S(1)} %fusion.4), channel_id=1, source_target_pairs={{0,4},{4,0},{8,12},{12,8},{16,20},{20,16},{24,28},{28,24},{1,5},{5... | collective-permute-start | bytes 98312 | tf_op jit(solution)/shard_map/ppermute | solution.py:170
  36.2 5.1 %collective-permute-start.11 = (bf16[64,384]{1,0:T(8,128)(2,1)S(1)}, bf16[64,384]{1,0:T(8,128)(2,1)S(1)}, u32[]{:S(2)}, u32[]{:S(2)}) collective-permute-start(bf16[64,384]{1,0:T(8,128)(2,1)S(1)} %fusion.5), channel_id=1, source_target_pairs={{0,4},{4,0},{8,12},{12,8},{16,20},{20,16},{24,28},{28,24},{1,5},{5... | collective-permute-start | bytes 147464 | tf_op jit(solution)/shard_map/ppermute | solution.py:170
  39.5 4.3 %collective-permute-start.6 = (bf16[2,128,128]{2,1,0:T(8,128)(2,1)S(1)}, bf16[2,128,128]{2,1,0:T(8,128)(2,1)S(1)}, u32[]{:S(2)}, u32[]{:S(2)}) collective-permute-start(bf16[2,128,128]{2,1,0:T(8,128)(2,1)S(1)} %pad_maximum_fusion.low_a), channel_id=1, source_target_pairs={{0,8},{4,12},{8,0},{12,4},{16,24},{20,28},{24,16},{28,20},{1,9},{5... | collective-permute-start | bytes 196616 | tf_op jit(solution)/shard_map/ppermute | solution.py:170
  44.5 1.5 %collective-permute-start.15 = (bf16[4,192,128]{2,1,0:T(8,128)(2,1)S(1)}, bf16[4,192,128]{2,1,0:T(8,128)(2,1)S(1)}, u32[]{:S(2)}, u32[]{:S(2)}) collective-permute-start(bf16[4,192,128]{2,1,0:T(8,128)(2,1)S(1)} %get-tuple-element.45), channel_id=1, source_target_pairs={{0,1},{1,0},{2,3},{3,2},{4,5},{5,4},{6,7},{7,6},{8,9},{9,8},{10,11... | collective-permute-start | bytes 589832 | tf_op jit(solution)/shard_map/ppermute | solution.py:170
  46.1 4.9 %collective-permute-start.16 = (bf16[2,192,128]{2,1,0:T(8,128)(2,1)S(1)}, bf16[2,192,128]{2,1,0:T(8,128)(2,1)S(1)}, u32[]{:S(2)}, u32[]{:S(2)}) collective-permute-start(bf16[2,192,128]{2,1,0:T(8,128)(2,1)S(1)} %fusion.2), channel_id=1, source_target_pairs={{0,2},{1,3},{2,0},{3,1},{4,6},{5,7},{6,4},{7,5},{8,10},{9,11},{10,... | collective-permute-start | bytes 294920 | tf_op jit(solution)/shard_map/ppermute | solution.py:170
  51.0 5.1 %collective-permute-start.17 = (bf16[1,192,128]{2,1,0:T(8,128)(2,1)S(1)}, bf16[1,192,128]{2,1,0:T(8,128)(2,1)S(1)}, u32[]{:S(2)}, u32[]{:S(2)}) collective-permute-start(bf16[1,192,128]{2,1,0:T(8,128)(2,1)S(1)} %fusion.6), channel_id=1, source_target_pairs={{0,16},{4,20},{8,24},{12,28},{16,0},{20,4},{24,8},{28,12},{1,17},{... | collective-permute-start | bytes 147464 | tf_op jit(solution)/shard_map/ppermute | solution.py:170

commit v4 on v3

--- a/solution.py
+++ b/solution.py
@@ -77,7 +77,7 @@
         row = pl.multiple_of(jnp.bitwise_xor(me, s) * tok, tok)
         for h in range(hq):
             q_buf[h, pl.ds(row, tok), :] = msgs[s][:, h * DH : (h + 1) * DH]
-        k_buf[pl.ds(row, tok), :] = msgs[s][:, W:]
+        k_buf[pl.ds(row, tok), :] = msgs[s][:, W : W + kh * DH]
     dk_buf[...] = jnp.zeros_like(dk_buf)
     row_in = lax.broadcasted_iota(jnp.int32, (tok, 1), 0)
     col_in = lax.broadcasted_iota(jnp.int32, (tok, tok), 1)
@@ -120,8 +120,7 @@
 
 
 def up_kernel(C, tok, R, *refs):
-    adapters = refs[:C]
-    dq, dk, pack, keep, send, a_buf = refs[C:]
+    adapters, dq, dk, pack, keep, send, a_buf = refs
     me, me_d = lax.axis_index("ctx"), lax.axis_index("dp")
     for s in range(C):
         a_buf[pl.ds(pl.multiple_of(jnp.bitwise_xor(me, s) * tok, tok), tok), :] = adapters[s][...]
@@ -139,10 +138,10 @@
         dst[n % 2] = rows[:, n * slot : (n + 1) * slot].astype(dst.dtype)
 
 
-def down_kernel(R, rblk, low_a, low_b, ups_a, ups_b, h0, h1, h2, h3, land, send, keep):
+def down_kernel(R, rblk, l0, l1, l2, l3, ups_a, ups_b, h0, h1, h2, h3, land, send, keep):
     acc = None
-    for low, hid in zip((low_a[0], low_a[1], low_b[0], low_b[1]), (h0, h1, h2, h3)):
-        term = dot32(low, hid[...])
+    for low, hid in zip((l0, l1, l2, l3), (h0, h1, h2, h3)):
+        term = dot32(low[0], hid[...])
         acc = term if acc is None else acc + term
     rows = (ups_a[...] + ups_b[...].astype(jnp.float32)).astype(jnp.bfloat16)
     me, me_d, width = lax.axis_index("ctx"), lax.axis_index("dp"), h0.shape[1]
@@ -197,6 +196,8 @@
                 dst = jnp.bitwise_xor(me, s)
                 yield 0, pl.multiple_of(dst * W, 128), s, 0, W
                 yield 1, pl.multiple_of(key_col(dst), 128), s, W, Wk
+                if s < 2:
+                    yield 2, 0, s, W + Wk, 2 * R
 
         def second_plan(me, me_d):
             yield 0, None, 0, None, None
@@ -204,10 +205,11 @@
             yield 1, pl.multiple_of(q_width + key_col(me), 128), 2, 0, Wk
             yield 2, None, 3, None, None
             yield 3, None, 4, None, None
-            if rblk % 128 == 0:
-                for n in range(4):
-                    for e in range(E):
-                        yield 4, pl.multiple_of(column(me, me_d, n, e), 128), 5 + n, e * rblk, rblk
+
+        def hidden_plan(me, me_d):
+            for n in range(4):
+                for e in range(E):
+                    yield 0, pl.multiple_of(column(me, me_d, n, e), 128), n, e * rblk, rblk
 
         E = C * Dp // 4
 
@@ -216,21 +218,13 @@
 
         pack, land, slot, rows_each = owner_tables(C, Dp, W, Wk, DH, q_width, group_cols, rows_total, rblk, tok)
         pack, land = jnp.asarray(pack), jnp.asarray(land)
-        msgs = list(slices(first_plan, 2 * C, (queries[0], keys[0]), [pltpu.VMEM((tok, W + Wk), bf)] * C))
+        shapes = [pltpu.VMEM((tok, W + Wk + (2 * R if s < 2 else 0)), bf) for s in range(C)]
+        msgs = list(slices(first_plan, 2 * C + 2, (queries[0], keys[0], adapter[0]), shapes))
         for s in range(1, C):
             msgs[s] = swap(msgs[s], s)
-        adapters = [adapter[0]] + [swap(adapter[0], s) for s in range(1, C)]
-        by_dma = rblk % 128 == 0
-        outs = [
-            pltpu.VMEM(teacher.shape[1:], bf),
-            pltpu.VMEM((R, W), bf),
-            pltpu.VMEM((R, Wk), bf),
-            pltpu.VMEM(pack.shape, jnp.int32),
-            pltpu.VMEM(land.shape, jnp.int32),
-        ] + [pltpu.VMEM((tok, E * rblk), bf)] * (4 if by_dma else 0)
-        ins = (teacher[0], adapter_up.T, pack, land) + ((hidden[0],) if by_dma else ())
-        teach, up_q, up_k, pack, land, *hids = slices(second_plan, 5 + (4 * E if by_dma else 0), ins, outs)
-        if not by_dma:
+        if rblk % 128 == 0:
+            hids = list(slices(hidden_plan, 4 * E, (hidden[0],), [pltpu.VMEM((tok, E * rblk), bf)] * 4))
+        else:
             blocks = hidden[0].reshape(tok, C * Dp, rblk)
             me, me_d = lax.axis_index("ctx"), lax.axis_index("dp")
             hids = []
@@ -238,6 +232,18 @@
                 order = jnp.stack([column(me, me_d, n, e) // rblk for e in range(E)])
                 hids.append(jnp.take(blocks, order, axis=1).reshape(tok, E * rblk))
         hids = [hids[0]] + [swap(hids[n], n, "dp") for n in range(1, 4)]
+        adapters, bit = jnp.stack([m[:, W + Wk :] for m in msgs[:2]]), 2
+        while bit < C:
+            adapters = jnp.concatenate([adapters, swap(adapters, bit)])
+            bit *= 2
+        outs = [
+            pltpu.VMEM(teacher.shape[1:], bf),
+            pltpu.VMEM((R, W), bf),
+            pltpu.VMEM((R, Wk), bf),
+            pltpu.VMEM(pack.shape, jnp.int32),
+            pltpu.VMEM(land.shape, jnp.int32),
+        ]
+        teach, up_q, up_k, pack, land = slices(second_plan, 5, (teacher[0], adapter_up.T, pack, land), outs)
 
         smem = pl.BlockSpec(memory_space=pltpu.SMEM)
         vmem = pl.BlockSpec(memory_space=pltpu.VMEM)
@@ -270,25 +276,24 @@
         ups, send = pl.pallas_call(
             functools.partial(up_kernel, C, tok, R),
             out_shape=(pltpu.VMEM((2, R, slot), f32), pltpu.VMEM((2, R, slot), bf)),
-            in_specs=[vmem] * (C + 3),
+            in_specs=[vmem] * 4,
             out_specs=(vmem, vmem),
             scratch_shapes=[pltpu.VMEM((S, 2 * R), bf)],
             compiler_params=params,
             name="upgrad",
-        )(*[near(a) for a in adapters], near(dq), near(dk), near(pack))
+        )(near(adapters), near(dq), near(dk), near(pack))
         ups = ups + swap(send, 2, "dp").astype(f32)
         low = low.astype(bf)
-        low = jnp.concatenate([low, swap(low, 1, "dp")])
+        lows = [low] + [swap(low, n, "dp") for n in range(1, 4)]
         got = swap(ups[1].astype(bf), 1, "dp")
-        other = swap(low, 2, "dp")
         send, keep = pl.pallas_call(
             functools.partial(down_kernel, R, rblk),
             out_shape=(pltpu.VMEM((E // 2, 3 * R, rblk), bf), pltpu.VMEM((E // 2, 3 * R, rblk), f32)),
-            in_specs=[vmem] * 9,
+            in_specs=[vmem] * 11,
             out_specs=(vmem, vmem),
             compiler_params=params,
             name="down",
-        )(*[near(x) for x in (low, other, ups[0], got, *hids, land)])
+        )(*[near(x) for x in (*lows, ups[0], got, *hids, land)])
         rounds = [("ctx", 1 << i) for i in range(C.bit_length() - 1)]
         rounds += [("dp", 4 << i) for i in range(Dp.bit_length() - 3)]
         for n, (axis, bit) in enumerate(rounds):

time: 57 us -> 46.9 us (0.82)
  waiting for transfers between devices: 26.4 us -> 13.6 us
  starting transfers between devices: 20.6 us -> 22.2 us
  Pallas kernels: 8.15 us -> 9.09 us
    ppermute x18 -> x17, waiting for transfers between devices: 26.4 us -> 13.6 us  [swap(): return lax.ppermute(x, axis, [(i, i ^ s) for i in range(mesh.shape[axis])])]
    ppermute x18 -> x17, starting transfers between devices: 20.6 us -> 22.2 us  [swap(): return lax.ppermute(x, axis, [(i, i ^ s) for i in range(mesh.shape[axis])])]
    pallas_call x2 -> x3, Pallas kernels: 3.48 us -> 4.42 us  [slices(): pl.pallas_call(functools.partial(slice_kernel, plan, len(ins)), out_shape...]
  transfers between devices with their start and end apart: 18 -> 17, of which waited for: 8 -> 8; matrix products, arithmetic and copies ran while one was open for 0% -> 0% of each run, Pallas kernels for 5% -> 14%
where the time goes in v4:
time: 46.9 us; the launch traced here: 46.6 us
  starting transfers between devices  22.2 us (47%)
  waiting for transfers between devices  13.6 us (29%)
  Pallas kernels  9.09 us (19%)
  between operations  1.44 us (3%)
    ppermute x17, starting transfers between devices, swap(): return lax.ppermute(x, axis, [(i, i ^ s) for i in range(mesh.shape[axis])])  22.2 us
    ppermute x17, waiting for transfers between devices, swap(): return lax.ppermute(x, axis, [(i, i ^ s) for i in range(mesh.shape[axis])])  13.6 us
    pallas_call x3, Pallas kernels, slices(): pl.pallas_call(functools.partial(slice_kernel, plan, len(ins)), out_shape...  4.42 us
    pallas_call x1, Pallas kernels, body(): pl.pallas_call(functools.partial(attend_kernel, C, tok, hq, kh, DH, H, R)...  2.59 us
  transfers between devices with their start and end apart: 17, of which 8 were waited for; matrix products, arithmetic and copies ran while one was open for 0% of the time, Pallas kernels for 14%

profile of v4, /device:TPU:0, one launch (start us, length us, event | category | flops | bytes accessed | tf_op | source)
XLA Modules:
  0.0 46.6 jit_solution(4576752637246396106)
XLA Ops:
  0.6 1.3 %shard_map.104 = (bf16[128,768]{1,0:T(8,128)(2,1)S(1)}, bf16[128,768]{1,0:T(8,128)(2,1)S(1)}, bf16[128,640]{1,0:T(8,128)(2,1)S(1)}, bf16[128,640]{1,0:T(8,128)(2,1)S(1)}) custom-call(bf16[128,2048]{1,0:T(8,128)(2,1)} %bitcast.44, bf16[128,512]{1,0:T(8,128)(2,1)} %bitcast.46, bf16[128,128]{1,0:T(8,128)(2,1)} %bitcast.47), custom_call_target="tpu_custom_call" | custom-call | tf_op jit(solution)/shard_map/pallas_call | solution.py:57
  2.5 2.6 %collective-permute-start.1 = (bf16[128,640]{1,0:T(8,128)(2,1)S(1)}, bf16[128,640]{1,0:T(8,128)(2,1)S(1)}, u32[]{:S(2)}, u32[]{:S(2)}) collective-permute-start(bf16[128,640]{1,0:T(8,128)(2,1)S(1)} %get-tuple-element.27), channel_id=1, source_target_pairs={{0,2},{1,3},{2,0},{3,1},{4,6},{5,7},{6,4},{7,5},{8,10},{9,11},{10,... | collective-permute-start | bytes 491528 | tf_op jit(solution)/shard_map/ppermute | solution.py:169
  5.1 1.5 %shard_map.106 = (bf16[128,1024]{1,0:T(8,128)(2,1)S(1)}, bf16[128,1024]{1,0:T(8,128)(2,1)S(1)}, bf16[128,1024]{1,0:T(8,128)(2,1)S(1)}, bf16[128,1024]{1,0:T(8,128)(2,1)S(1)}) custom-call(bf16[128,4096]{1,0:T(8,128)(2,1)} %bitcast.43), custom_call_target="tpu_custom_call" | custom-call | tf_op jit(solution)/shard_map/pallas_call | solution.py:57
  6.6 1.8 %collective-permute-start.11 = (bf16[128,1024]{1,0:T(8,128)(2,1)S(1)}, bf16[128,1024]{1,0:T(8,128)(2,1)S(1)}, u32[]{:S(2)}, u32[]{:S(2)}) collective-permute-start(bf16[128,1024]{1,0:T(8,128)(2,1)S(1)} %get-tuple-element.40), channel_id=1, source_target_pairs={{0,4},{4,0},{8,12},{12,8},{16,20},{20,16},{24,28},{28,24},{1,5},{5... | collective-permute-start | bytes 786440 | tf_op jit(solution)/shard_map/ppermute | solution.py:169
  8.4 1.6 %collective-permute-start.12 = (bf16[128,1024]{1,0:T(8,128)(2,1)S(1)}, bf16[128,1024]{1,0:T(8,128)(2,1)S(1)}, u32[]{:S(2)}, u32[]{:S(2)}) collective-permute-start(bf16[128,1024]{1,0:T(8,128)(2,1)S(1)} %get-tuple-element.41), channel_id=1, source_target_pairs={{0,8},{4,12},{8,0},{12,4},{16,24},{20,28},{24,16},{28,20},{1,9},{5... | collective-permute-start | bytes 786440 | tf_op jit(solution)/shard_map/ppermute | solution.py:169
  10.6 1.6 %shard_map.105 = (bf16[4,512,512]{2,1,0:T(8,128)(2,1)S(1)}, bf16[64,512]{1,0:T(8,128)(2,1)S(1)}, bf16[64,128]{1,0:T(8,128)(2,1)S(1)}, s32[16,1536]{1,0:T(8,128)S(1)}, s32[16,384]{1,0:T(8,128)S(1)}) custom-call(bf16[4,512,512]{2,1,0:T(8,128)(2,1)} %bitcast.40, bf16[64,2560]{1,0:T(8,128)(2,1)} %bitcast.45, s32[16,1536]{1,0:T(8,128)} %constant.4.clone.refs_2_, ...), custom_call_target="tpu_custom_call" | custom-call | tf_op jit(solution)/shard_map/pallas_call | solution.py:57
  12.3 0.9 %collective-permute-start.13 = (bf16[128,1024]{1,0:T(8,128)(2,1)S(1)}, bf16[128,1024]{1,0:T(8,128)(2,1)S(1)}, u32[]{:S(2)}, u32[]{:S(2)}) collective-permute-start(bf16[128,1024]{1,0:T(8,128)(2,1)S(1)} %get-tuple-element.42), channel_id=1, source_target_pairs={{0,12},{4,8},{8,4},{12,0},{16,28},{20,24},{24,20},{28,16},{1,13},{... | collective-permute-start | bytes 786440 | tf_op jit(solution)/shard_map/ppermute | solution.py:169
  13.2 2.6 %attend.1 = (f32[2,128,128]{2,1,0:T(8,128)S(1)}, f32[2,128,128]{2,1,0:T(8,128)S(1)}, bf16[512,512]{1,0:T(8,128)(2,1)S(1)}, bf16[128,512]{1,0:T(8,128)(2,1)S(1)}) custom-call(s32[1]{0:T(128)S(6)} %copy.23.lengths, bf16[128,768]{1,0:T(8,128)(2,1)S(1)} %get-tuple-element.25.refs_0_, bf16[128,768]{1,0:T(8,128)(2,1)S(1)} %collective-permute-done.refs_1_, ...), custom_call_target="tpu_custom_call" | custom-call | tf_op jit(solution)/shard_map/attend/pallas_call | solution.py:251
  16.1 1.8 %collective-permute-start.8 = (bf16[2,128,128]{2,1,0:T(8,128)(2,1)S(1)}, bf16[2,128,128]{2,1,0:T(8,128)(2,1)S(1)}, u32[]{:S(2)}, u32[]{:S(2)}) collective-permute-start(bf16[2,128,128]{2,1,0:T(8,128)(2,1)S(1)} %pad_maximum_fusion.1), channel_id=1, source_target_pairs={{0,2},{1,3},{2,0},{3,1},{4,6},{5,7},{6,4},{7,5},{8,10},{9,11},{10,... | collective-permute-start | bytes 196616 | tf_op jit(solution)/shard_map/ppermute | solution.py:169
  18.0 1.0 %collective-permute-start.4 = (bf16[1,128,128]{2,1,0:T(8,128)(2,1)S(1)}, bf16[1,128,128]{2,1,0:T(8,128)(2,1)S(1)}, u32[]{:S(2)}, u32[]{:S(2)}) collective-permute-start(bf16[1,128,128]{2,1,0:T(8,128)(2,1)S(1)} %fusion.7), channel_id=1, source_target_pairs={{0,2},{1,3},{2,0},{3,1},{4,6},{5,7},{6,4},{7,5},{8,10},{9,11},{10,... | collective-permute-start | bytes 98312 | tf_op jit(solution)/shard_map/ppermute | solution.py:169
  19.0 1.6 %collective-permute-done.8 = bf16[2,128,128]{2,1,0:T(8,128)(2,1)S(1)} collective-permute-done((bf16[2,128,128]{2,1,0:T(8,128)(2,1)S(1)}, bf16[2,128,128]{2,1,0:T(8,128)(2,1)S(1)}, u32[]{:S(2)}, u32[]{:S(2)}) %collective-permute-start.8) | collective-permute-done | bytes 65568 | tf_op jit(solution)/shard_map/ppermute | solution.py:169
  20.6 0.7 %upgrad.1 = (f32[2,64,384]{2,1,0:T(8,128)S(1)}, bf16[2,64,384]{2,1,0:T(8,128)(2,1)S(1)}) custom-call(bf16[4,128,128]{2,1,0:T(8,128)(2,1)S(1)} %pad_maximum_fusion.refs_0_, bf16[512,512]{1,0:T(8,128)(2,1)S(1)} %get-tuple-element.34.refs_1_, bf16[128,512]{1,0:T(8,128)(2,1)S(1)} %get-tuple-element.35.refs_2_, s32[16,1536]{1,0:T(8,128)S(1)} %get-tuple-element.36.refs_3_), custom_call_target="tpu_custom_call" | custom-call | tf_op jit(solution)/shard_map/upgrad/pallas_call | solution.py:276
  21.3 2.1 %collective-permute-start.9 = (bf16[2,64,384]{2,1,0:T(8,128)(2,1)S(1)}, bf16[2,64,384]{2,1,0:T(8,128)(2,1)S(1)}, u32[]{:S(2)}, u32[]{:S(2)}) collective-permute-start(bf16[2,64,384]{2,1,0:T(8,128)(2,1)S(1)} %get-tuple-element.38), channel_id=1, source_target_pairs={{0,8},{4,12},{8,0},{12,4},{16,24},{20,28},{24,16},{28,20},{1,9},{5... | collective-permute-start | bytes 294920 | tf_op jit(solution)/shard_map/ppermute | solution.py:169
  23.4 1.6 %collective-permute-start.5 = (bf16[1,128,128]{2,1,0:T(8,128)(2,1)S(1)}, bf16[1,128,128]{2,1,0:T(8,128)(2,1)S(1)}, u32[]{:S(2)}, u32[]{:S(2)}) collective-permute-start(bf16[1,128,128]{2,1,0:T(8,128)(2,1)S(1)} %fusion.4.l0), channel_id=1, source_target_pairs={{0,4},{4,0},{8,12},{12,8},{16,20},{20,16},{24,28},{28,24},{1,5},{5... | collective-permute-start | bytes 98312 | tf_op jit(solution)/shard_map/ppermute | solution.py:169
  25.0 1.0 %collective-permute-done.9 = bf16[2,64,384]{2,1,0:T(8,128)(2,1)S(1)} collective-permute-done((bf16[2,64,384]{2,1,0:T(8,128)(2,1)S(1)}, bf16[2,64,384]{2,1,0:T(8,128)(2,1)S(1)}, u32[]{:S(2)}, u32[]{:S(2)}) %collective-permute-start.9) | collective-permute-done | bytes 98336 | tf_op jit(solution)/shard_map/ppermute | solution.py:169
  26.0 2.0 %collective-permute-start.6 = (bf16[1,128,128]{2,1,0:T(8,128)(2,1)S(1)}, bf16[1,128,128]{2,1,0:T(8,128)(2,1)S(1)}, u32[]{:S(2)}, u32[]{:S(2)}) collective-permute-start(bf16[1,128,128]{2,1,0:T(8,128)(2,1)S(1)} %fusion.4.l0), channel_id=1, source_target_pairs={{0,8},{4,12},{8,0},{12,4},{16,24},{20,28},{24,16},{28,20},{1,9},{5... | collective-permute-start | bytes 98312 | tf_op jit(solution)/shard_map/ppermute | solution.py:169
  28.1 1.5 %collective-permute-start.7 = (bf16[1,128,128]{2,1,0:T(8,128)(2,1)S(1)}, bf16[1,128,128]{2,1,0:T(8,128)(2,1)S(1)}, u32[]{:S(2)}, u32[]{:S(2)}) collective-permute-start(bf16[1,128,128]{2,1,0:T(8,128)(2,1)S(1)} %fusion.4.l0), channel_id=1, source_target_pairs={{0,12},{4,8},{8,4},{12,0},{16,28},{20,24},{24,20},{28,16},{1,13},{... | collective-permute-start | bytes 98312 | tf_op jit(solution)/shard_map/ppermute | solution.py:169
  29.9 3.0 %collective-permute-done.7.l3 = bf16[1,128,128]{2,1,0:T(8,128)(2,1)S(1)} collective-permute-done((bf16[1,128,128]{2,1,0:T(8,128)(2,1)S(1)}, bf16[1,128,128]{2,1,0:T(8,128)(2,1)S(1)}, u32[]{:S(2)}, u32[]{:S(2)}) %collective-permute-start.7) | collective-permute-done | bytes 32800 | tf_op jit(solution)/shard_map/ppermute | solution.py:169
  34.4 1.4 %collective-permute-done.14 = bf16[4,192,128]{2,1,0:T(8,128)(2,1)S(1)} collective-permute-done((bf16[4,192,128]{2,1,0:T(8,128)(2,1)S(1)}, bf16[4,192,128]{2,1,0:T(8,128)(2,1)S(1)}, u32[]{:S(2)}, u32[]{:S(2)}) %collective-permute-start.14) | collective-permute-done | bytes 196640 | tf_op jit(solution)/shard_map/ppermute | solution.py:169
  35.9 1.6 %collective-permute-start.15 = (bf16[2,192,128]{2,1,0:T(8,128)(2,1)S(1)}, bf16[2,192,128]{2,1,0:T(8,128)(2,1)S(1)}, u32[]{:S(2)}, u32[]{:S(2)}) collective-permute-start(bf16[2,192,128]{2,1,0:T(8,128)(2,1)S(1)} %fusion.2), channel_id=1, source_target_pairs={{0,2},{1,3},{2,0},{3,1},{4,6},{5,7},{6,4},{7,5},{8,10},{9,11},{10,... | collective-permute-start | bytes 294920 | tf_op jit(solution)/shard_map/ppermute | solution.py:169
  37.4 3.3 %collective-permute-done.15 = bf16[2,192,128]{2,1,0:T(8,128)(2,1)S(1)} collective-permute-done((bf16[2,192,128]{2,1,0:T(8,128)(2,1)S(1)}, bf16[2,192,128]{2,1,0:T(8,128)(2,1)S(1)}, u32[]{:S(2)}, u32[]{:S(2)}) %collective-permute-start.15) | collective-permute-done | bytes 98336 | tf_op jit(solution)/shard_map/ppermute | solution.py:169
  40.8 2.7 %collective-permute-start.16 = (bf16[1,192,128]{2,1,0:T(8,128)(2,1)S(1)}, bf16[1,192,128]{2,1,0:T(8,128)(2,1)S(1)}, u32[]{:S(2)}, u32[]{:S(2)}) collective-permute-start(bf16[1,192,128]{2,1,0:T(8,128)(2,1)S(1)} %fusion.6), channel_id=1, source_target_pairs={{0,16},{4,20},{8,24},{12,28},{16,0},{20,4},{24,8},{28,12},{1,17},{... | collective-permute-start | bytes 147464 | tf_op jit(solution)/shard_map/ppermute | solution.py:169
  43.5 2.4 %collective-permute-done.16.got = bf16[1,192,128]{2,1,0:T(8,128)(2,1)S(1)} collective-permute-done((bf16[1,192,128]{2,1,0:T(8,128)(2,1)S(1)}, bf16[1,192,128]{2,1,0:T(8,128)(2,1)S(1)}, u32[]{:S(2)}, u32[]{:S(2)}) %collective-permute-start.16) | collective-permute-done | bytes 49184 | tf_op jit(solution)/shard_map/ppermute | solution.py:169
  45.9 0.7 %final.1 = (f32[128,128]{1,0:T(8,128)}, f32[64,80]{1,0:T(8,128)}) custom-call(f32[1,192,128]{2,1,0:T(8,128)S(1)} %slice_bitcast_fusion.kept, bf16[1,192,128]{2,1,0:T(8,128)(2,1)S(1)} %collective-permute-done.16.got), custom_call_target="tpu_custom_call" | custom-call | tf_op jit(solution)/shard_map/final/pallas_call | solution.py:306
  (32 shorter events, 2.9 us)
Async XLA Ops:
  1.9 11.2 %collective-permute-start = (bf16[128,768]{1,0:T(8,128)(2,1)S(1)}, bf16[128,768]{1,0:T(8,128)(2,1)S(1)}, u32[]{:S(2)}, u32[]{:S(2)}) collective-permute-start(bf16[128,768]{1,0:T(8,128)(2,1)S(1)} %get-tuple-element.26), channel_id=1, source_target_pairs={{0,1},{1,0},{2,3},{3,2},{4,5},{5,4},{6,7},{7,6},{8,9},{9,8},{10,11... | collective-permute-start | bytes 589832 | tf_op jit(solution)/shard_map/ppermute | solution.py:169
  2.5 9.8 %collective-permute-start.1 = (bf16[128,640]{1,0:T(8,128)(2,1)S(1)}, bf16[128,640]{1,0:T(8,128)(2,1)S(1)}, u32[]{:S(2)}, u32[]{:S(2)}) collective-permute-start(bf16[128,640]{1,0:T(8,128)(2,1)S(1)} %get-tuple-element.27), channel_id=1, source_target_pairs={{0,2},{1,3},{2,0},{3,1},{4,6},{5,7},{6,4},{7,5},{8,10},{9,11},{10,... | collective-permute-start | bytes 491528 | tf_op jit(solution)/shard_map/ppermute | solution.py:169
  5.0 8.1 %collective-permute-start.2 = (bf16[128,640]{1,0:T(8,128)(2,1)S(1)}, bf16[128,640]{1,0:T(8,128)(2,1)S(1)}, u32[]{:S(2)}, u32[]{:S(2)}) collective-permute-start(bf16[128,640]{1,0:T(8,128)(2,1)S(1)} %get-tuple-element.28), channel_id=1, source_target_pairs={{0,3},{1,2},{2,1},{3,0},{4,7},{5,6},{6,5},{7,4},{8,11},{9,10},{10,... | collective-permute-start | bytes 491528 | tf_op jit(solution)/shard_map/ppermute | solution.py:169
  6.6 21.5 %collective-permute-start.11 = (bf16[128,1024]{1,0:T(8,128)(2,1)S(1)}, bf16[128,1024]{1,0:T(8,128)(2,1)S(1)}, u32[]{:S(2)}, u32[]{:S(2)}) collective-permute-start(bf16[128,1024]{1,0:T(8,128)(2,1)S(1)} %get-tuple-element.40), channel_id=1, source_target_pairs={{0,4},{4,0},{8,12},{12,8},{16,20},{20,16},{24,28},{28,24},{1,5},{5... | collective-permute-start | bytes 786440 | tf_op jit(solution)/shard_map/ppermute | solution.py:169
  8.4 21.2 %collective-permute-start.12 = (bf16[128,1024]{1,0:T(8,128)(2,1)S(1)}, bf16[128,1024]{1,0:T(8,128)(2,1)S(1)}, u32[]{:S(2)}, u32[]{:S(2)}) collective-permute-start(bf16[128,1024]{1,0:T(8,128)(2,1)S(1)} %get-tuple-element.41), channel_id=1, source_target_pairs={{0,8},{4,12},{8,0},{12,4},{16,24},{20,28},{24,16},{28,20},{1,9},{5... | collective-permute-start | bytes 786440 | tf_op jit(solution)/shard_map/ppermute | solution.py:169
  12.3 17.5 %collective-permute-start.13 = (bf16[128,1024]{1,0:T(8,128)(2,1)S(1)}, bf16[128,1024]{1,0:T(8,128)(2,1)S(1)}, u32[]{:S(2)}, u32[]{:S(2)}) collective-permute-start(bf16[128,1024]{1,0:T(8,128)(2,1)S(1)} %get-tuple-element.42), channel_id=1, source_target_pairs={{0,12},{4,8},{8,4},{12,0},{16,28},{20,24},{24,20},{28,16},{1,13},{... | collective-permute-start | bytes 786440 | tf_op jit(solution)/shard_map/ppermute | solution.py:169
  15.8 2.2 %collective-permute-start.3 = (f32[2,128,128]{2,1,0:T(8,128)S(1)}, f32[2,128,128]{2,1,0:T(8,128)S(1)}, u32[]{:S(2)}, u32[]{:S(2)}) collective-permute-start(f32[2,128,128]{2,1,0:T(8,128)S(1)} %get-tuple-element.33), channel_id=1, source_target_pairs={{0,1},{1,0},{2,3},{3,2},{4,5},{5,4},{6,7},{7,6},{8,9},{9,8},{10,11... | collective-permute-start | bytes 393224 | tf_op jit(solution)/shard_map/ppermute | solution.py:169
  16.1 4.4 %collective-permute-start.8 = (bf16[2,128,128]{2,1,0:T(8,128)(2,1)S(1)}, bf16[2,128,128]{2,1,0:T(8,128)(2,1)S(1)}, u32[]{:S(2)}, u32[]{:S(2)}) collective-permute-start(bf16[2,128,128]{2,1,0:T(8,128)(2,1)S(1)} %pad_maximum_fusion.1), channel_id=1, source_target_pairs={{0,2},{1,3},{2,0},{3,1},{4,6},{5,7},{6,4},{7,5},{8,10},{9,11},{10,... | collective-permute-start | bytes 196616 | tf_op jit(solution)/shard_map/ppermute | solution.py:169
  18.0 5.4 %collective-permute-start.4 = (bf16[1,128,128]{2,1,0:T(8,128)(2,1)S(1)}, bf16[1,128,128]{2,1,0:T(8,128)(2,1)S(1)}, u32[]{:S(2)}, u32[]{:S(2)}) collective-permute-start(bf16[1,128,128]{2,1,0:T(8,128)(2,1)S(1)} %fusion.7), channel_id=1, source_target_pairs={{0,2},{1,3},{2,0},{3,1},{4,6},{5,7},{6,4},{7,5},{8,10},{9,11},{10,... | collective-permute-start | bytes 98312 | tf_op jit(solution)/shard_map/ppermute | solution.py:169
  21.3 4.7 %collective-permute-start.9 = (bf16[2,64,384]{2,1,0:T(8,128)(2,1)S(1)}, bf16[2,64,384]{2,1,0:T(8,128)(2,1)S(1)}, u32[]{:S(2)}, u32[]{:S(2)}) collective-permute-start(bf16[2,64,384]{2,1,0:T(8,128)(2,1)S(1)} %get-tuple-element.38), channel_id=1, source_target_pairs={{0,8},{4,12},{8,0},{12,4},{16,24},{20,28},{24,16},{28,20},{1,9},{5... | collective-permute-start | bytes 294920 | tf_op jit(solution)/shard_map/ppermute | solution.py:169
  23.4 6.3 %collective-permute-start.5 = (bf16[1,128,128]{2,1,0:T(8,128)(2,1)S(1)}, bf16[1,128,128]{2,1,0:T(8,128)(2,1)S(1)}, u32[]{:S(2)}, u32[]{:S(2)}) collective-permute-start(bf16[1,128,128]{2,1,0:T(8,128)(2,1)S(1)} %fusion.4.l0), channel_id=1, source_target_pairs={{0,4},{4,0},{8,12},{12,8},{16,20},{20,16},{24,28},{28,24},{1,5},{5... | collective-permute-start | bytes 98312 | tf_op jit(solution)/shard_map/ppermute | solution.py:169
  26.0 3.9 %collective-permute-start.6 = (bf16[1,128,128]{2,1,0:T(8,128)(2,1)S(1)}, bf16[1,128,128]{2,1,0:T(8,128)(2,1)S(1)}, u32[]{:S(2)}, u32[]{:S(2)}) collective-permute-start(bf16[1,128,128]{2,1,0:T(8,128)(2,1)S(1)} %fusion.4.l0), channel_id=1, source_target_pairs={{0,8},{4,12},{8,0},{12,4},{16,24},{20,28},{24,16},{28,20},{1,9},{5... | collective-permute-start | bytes 98312 | tf_op jit(solution)/shard_map/ppermute | solution.py:169
  28.1 4.9 %collective-permute-start.7 = (bf16[1,128,128]{2,1,0:T(8,128)(2,1)S(1)}, bf16[1,128,128]{2,1,0:T(8,128)(2,1)S(1)}, u32[]{:S(2)}, u32[]{:S(2)}) collective-permute-start(bf16[1,128,128]{2,1,0:T(8,128)(2,1)S(1)} %fusion.4.l0), channel_id=1, source_target_pairs={{0,12},{4,8},{8,4},{12,0},{16,28},{20,24},{24,20},{28,16},{1,13},{... | collective-permute-start | bytes 98312 | tf_op jit(solution)/shard_map/ppermute | solution.py:169
  29.6 4.1 %collective-permute-start.10 = (bf16[64,384]{1,0:T(8,128)(2,1)S(1)}, bf16[64,384]{1,0:T(8,128)(2,1)S(1)}, u32[]{:S(2)}, u32[]{:S(2)}) collective-permute-start(bf16[64,384]{1,0:T(8,128)(2,1)S(1)} %fusion.5), channel_id=1, source_target_pairs={{0,4},{4,0},{8,12},{12,8},{16,20},{20,16},{24,28},{28,24},{1,5},{5... | collective-permute-start | bytes 147464 | tf_op jit(solution)/shard_map/ppermute | solution.py:169
  34.3 1.5 %collective-permute-start.14 = (bf16[4,192,128]{2,1,0:T(8,128)(2,1)S(1)}, bf16[4,192,128]{2,1,0:T(8,128)(2,1)S(1)}, u32[]{:S(2)}, u32[]{:S(2)}) collective-permute-start(bf16[4,192,128]{2,1,0:T(8,128)(2,1)S(1)} %get-tuple-element.45), channel_id=1, source_target_pairs={{0,1},{1,0},{2,3},{3,2},{4,5},{5,4},{6,7},{7,6},{8,9},{9,8},{10,11... | collective-permute-start | bytes 589832 | tf_op jit(solution)/shard_map/ppermute | solution.py:169
  35.9 4.9 %collective-permute-start.15 = (bf16[2,192,128]{2,1,0:T(8,128)(2,1)S(1)}, bf16[2,192,128]{2,1,0:T(8,128)(2,1)S(1)}, u32[]{:S(2)}, u32[]{:S(2)}) collective-permute-start(bf16[2,192,128]{2,1,0:T(8,128)(2,1)S(1)} %fusion.2), channel_id=1, source_target_pairs={{0,2},{1,3},{2,0},{3,1},{4,6},{5,7},{6,4},{7,5},{8,10},{9,11},{10,... | collective-permute-start | bytes 294920 | tf_op jit(solution)/shard_map/ppermute | solution.py:169
  40.8 5.1 %collective-permute-start.16 = (bf16[1,192,128]{2,1,0:T(8,128)(2,1)S(1)}, bf16[1,192,128]{2,1,0:T(8,128)(2,1)S(1)}, u32[]{:S(2)}, u32[]{:S(2)}) collective-permute-start(bf16[1,192,128]{2,1,0:T(8,128)(2,1)S(1)} %fusion.6), channel_id=1, source_target_pairs={{0,16},{4,20},{8,24},{12,28},{16,0},{20,4},{24,8},{28,12},{1,17},{... | collective-permute-start | bytes 147464 | tf_op jit(solution)/shard_map/ppermute | solution.py:169

commit v5 on v4

--- a/solution.py
+++ b/solution.py
@@ -199,6 +199,18 @@
                 if s < 2:
                     yield 2, 0, s, W + Wk, 2 * R
 
+        E = C * Dp // 4
+
+        def column(me, me_d, n, e):
+            return (jnp.bitwise_xor(me_d, n + e // C * 4) * C + jnp.bitwise_xor(me, e % C)) * rblk
+
+        by_dma = rblk % 128 == 0
+
+        def hidden_plan(me, me_d):
+            for n in range(4):
+                for e in range(E):
+                    yield 0, pl.multiple_of(column(me, me_d, n, e), 128), n, e * rblk, rblk
+
         def second_plan(me, me_d):
             yield 0, None, 0, None, None
             yield 1, pl.multiple_of(me * W, 128), 1, 0, W
@@ -206,28 +218,17 @@
             yield 2, None, 3, None, None
             yield 3, None, 4, None, None
 
-        def hidden_plan(me, me_d):
-            for n in range(4):
-                for e in range(E):
-                    yield 0, pl.multiple_of(column(me, me_d, n, e), 128), n, e * rblk, rblk
-
-        E = C * Dp // 4
-
-        def column(me, me_d, n, e):
-            return (jnp.bitwise_xor(me_d, n + e // C * 4) * C + jnp.bitwise_xor(me, e % C)) * rblk
-
         pack, land, slot, rows_each = owner_tables(C, Dp, W, Wk, DH, q_width, group_cols, rows_total, rblk, tok)
         pack, land = jnp.asarray(pack), jnp.asarray(land)
         shapes = [pltpu.VMEM((tok, W + Wk + (2 * R if s < 2 else 0)), bf) for s in range(C)]
         msgs = list(slices(first_plan, 2 * C + 2, (queries[0], keys[0], adapter[0]), shapes))
         for s in range(1, C):
             msgs[s] = swap(msgs[s], s)
-        if rblk % 128 == 0:
+        if by_dma:
             hids = list(slices(hidden_plan, 4 * E, (hidden[0],), [pltpu.VMEM((tok, E * rblk), bf)] * 4))
         else:
-            blocks = hidden[0].reshape(tok, C * Dp, rblk)
+            blocks, hids = hidden[0].reshape(tok, C * Dp, rblk), []
             me, me_d = lax.axis_index("ctx"), lax.axis_index("dp")
-            hids = []
             for n in range(4):
                 order = jnp.stack([column(me, me_d, n, e) // rblk for e in range(E)])
                 hids.append(jnp.take(blocks, order, axis=1).reshape(tok, E * rblk))
@@ -284,7 +285,9 @@
         )(near(adapters), near(dq), near(dk), near(pack))
         ups = ups + swap(send, 2, "dp").astype(f32)
         low = low.astype(bf)
-        lows = [low] + [swap(low, n, "dp") for n in range(1, 4)]
+        lows = [low]
+        for n in range(1, 4):
+            lows.append(swap(low, n, "dp"))
         got = swap(ups[1].astype(bf), 1, "dp")
         send, keep = pl.pallas_call(
             functools.partial(down_kernel, R, rblk),

time: 46.9 us -> 46.9 us (level)
  no operation moved by 1% of the time
where the time goes in v5:
time: 46.9 us; the launch traced here: 46.6 us
  starting transfers between devices  22.2 us (47%)
  waiting for transfers between devices  13.6 us (29%)
  Pallas kernels  9.09 us (19%)
  between operations  1.44 us (3%)
    ppermute x17, starting transfers between devices, swap(): return lax.ppermute(x, axis, [(i, i ^ s) for i in range(mesh.shape[axis])])  22.2 us
    ppermute x17, waiting for transfers between devices, swap(): return lax.ppermute(x, axis, [(i, i ^ s) for i in range(mesh.shape[axis])])  13.6 us
    pallas_call x3, Pallas kernels, slices(): pl.pallas_call(functools.partial(slice_kernel, plan, len(ins)), out_shape...  4.42 us
    pallas_call x1, Pallas kernels, body(): pl.pallas_call(functools.partial(attend_kernel, C, tok, hq, kh, DH, H, R)...  2.59 us
  transfers between devices with their start and end apart: 17, of which 8 were waited for; matrix products, arithmetic and copies ran while one was open for 0% of the time, Pallas kernels for 14%

profile of v5, /device:TPU:0, one launch (start us, length us, event | category | flops | bytes accessed | tf_op | source)
XLA Modules:
  0.0 46.6 jit_solution(4576752637246396106)
XLA Ops:
  0.6 1.3 %shard_map.104 = (bf16[128,768]{1,0:T(8,128)(2,1)S(1)}, bf16[128,768]{1,0:T(8,128)(2,1)S(1)}, bf16[128,640]{1,0:T(8,128)(2,1)S(1)}, bf16[128,640]{1,0:T(8,128)(2,1)S(1)}) custom-call(bf16[128,2048]{1,0:T(8,128)(2,1)} %bitcast.44, bf16[128,512]{1,0:T(8,128)(2,1)} %bitcast.46, bf16[128,128]{1,0:T(8,128)(2,1)} %bitcast.47), custom_call_target="tpu_custom_call" | custom-call | tf_op jit(solution)/shard_map/pallas_call | solution.py:57
  2.5 2.6 %collective-permute-start.1 = (bf16[128,640]{1,0:T(8,128)(2,1)S(1)}, bf16[128,640]{1,0:T(8,128)(2,1)S(1)}, u32[]{:S(2)}, u32[]{:S(2)}) collective-permute-start(bf16[128,640]{1,0:T(8,128)(2,1)S(1)} %get-tuple-element.27), channel_id=1, source_target_pairs={{0,2},{1,3},{2,0},{3,1},{4,6},{5,7},{6,4},{7,5},{8,10},{9,11},{10,... | collective-permute-start | bytes 491528 | tf_op jit(solution)/shard_map/ppermute | solution.py:169
  5.1 1.5 %shard_map.106 = (bf16[128,1024]{1,0:T(8,128)(2,1)S(1)}, bf16[128,1024]{1,0:T(8,128)(2,1)S(1)}, bf16[128,1024]{1,0:T(8,128)(2,1)S(1)}, bf16[128,1024]{1,0:T(8,128)(2,1)S(1)}) custom-call(bf16[128,4096]{1,0:T(8,128)(2,1)} %bitcast.43), custom_call_target="tpu_custom_call" | custom-call | tf_op jit(solution)/shard_map/pallas_call | solution.py:57
  6.6 1.8 %collective-permute-start.11 = (bf16[128,1024]{1,0:T(8,128)(2,1)S(1)}, bf16[128,1024]{1,0:T(8,128)(2,1)S(1)}, u32[]{:S(2)}, u32[]{:S(2)}) collective-permute-start(bf16[128,1024]{1,0:T(8,128)(2,1)S(1)} %get-tuple-element.40), channel_id=1, source_target_pairs={{0,4},{4,0},{8,12},{12,8},{16,20},{20,16},{24,28},{28,24},{1,5},{5... | collective-permute-start | bytes 786440 | tf_op jit(solution)/shard_map/ppermute | solution.py:169
  8.4 1.6 %collective-permute-start.12 = (bf16[128,1024]{1,0:T(8,128)(2,1)S(1)}, bf16[128,1024]{1,0:T(8,128)(2,1)S(1)}, u32[]{:S(2)}, u32[]{:S(2)}) collective-permute-start(bf16[128,1024]{1,0:T(8,128)(2,1)S(1)} %get-tuple-element.41), channel_id=1, source_target_pairs={{0,8},{4,12},{8,0},{12,4},{16,24},{20,28},{24,16},{28,20},{1,9},{5... | collective-permute-start | bytes 786440 | tf_op jit(solution)/shard_map/ppermute | solution.py:169
  10.6 1.6 %shard_map.105 = (bf16[4,512,512]{2,1,0:T(8,128)(2,1)S(1)}, bf16[64,512]{1,0:T(8,128)(2,1)S(1)}, bf16[64,128]{1,0:T(8,128)(2,1)S(1)}, s32[16,1536]{1,0:T(8,128)S(1)}, s32[16,384]{1,0:T(8,128)S(1)}) custom-call(bf16[4,512,512]{2,1,0:T(8,128)(2,1)} %bitcast.40, bf16[64,2560]{1,0:T(8,128)(2,1)} %bitcast.45, s32[16,1536]{1,0:T(8,128)} %constant.4.clone.refs_2_, ...), custom_call_target="tpu_custom_call" | custom-call | tf_op jit(solution)/shard_map/pallas_call | solution.py:57
  12.3 0.9 %collective-permute-start.13 = (bf16[128,1024]{1,0:T(8,128)(2,1)S(1)}, bf16[128,1024]{1,0:T(8,128)(2,1)S(1)}, u32[]{:S(2)}, u32[]{:S(2)}) collective-permute-start(bf16[128,1024]{1,0:T(8,128)(2,1)S(1)} %get-tuple-element.42), channel_id=1, source_target_pairs={{0,12},{4,8},{8,4},{12,0},{16,28},{20,24},{24,20},{28,16},{1,13},{... | collective-permute-start | bytes 786440 | tf_op jit(solution)/shard_map/ppermute | solution.py:169
  13.2 2.6 %attend.1 = (f32[2,128,128]{2,1,0:T(8,128)S(1)}, f32[2,128,128]{2,1,0:T(8,128)S(1)}, bf16[512,512]{1,0:T(8,128)(2,1)S(1)}, bf16[128,512]{1,0:T(8,128)(2,1)S(1)}) custom-call(s32[1]{0:T(128)S(6)} %copy.23.lengths, bf16[128,768]{1,0:T(8,128)(2,1)S(1)} %get-tuple-element.25.refs_0_, bf16[128,768]{1,0:T(8,128)(2,1)S(1)} %collective-permute-done.refs_1_, ...), custom_call_target="tpu_custom_call" | custom-call | tf_op jit(solution)/shard_map/attend/pallas_call | solution.py:252
  16.1 1.8 %collective-permute-start.8 = (bf16[2,128,128]{2,1,0:T(8,128)(2,1)S(1)}, bf16[2,128,128]{2,1,0:T(8,128)(2,1)S(1)}, u32[]{:S(2)}, u32[]{:S(2)}) collective-permute-start(bf16[2,128,128]{2,1,0:T(8,128)(2,1)S(1)} %pad_maximum_fusion.1), channel_id=1, source_target_pairs={{0,2},{1,3},{2,0},{3,1},{4,6},{5,7},{6,4},{7,5},{8,10},{9,11},{10,... | collective-permute-start | bytes 196616 | tf_op jit(solution)/shard_map/ppermute | solution.py:169
  18.0 1.0 %collective-permute-start.4 = (bf16[1,128,128]{2,1,0:T(8,128)(2,1)S(1)}, bf16[1,128,128]{2,1,0:T(8,128)(2,1)S(1)}, u32[]{:S(2)}, u32[]{:S(2)}) collective-permute-start(bf16[1,128,128]{2,1,0:T(8,128)(2,1)S(1)} %fusion.7), channel_id=1, source_target_pairs={{0,2},{1,3},{2,0},{3,1},{4,6},{5,7},{6,4},{7,5},{8,10},{9,11},{10,... | collective-permute-start | bytes 98312 | tf_op jit(solution)/shard_map/ppermute | solution.py:169
  19.0 1.6 %collective-permute-done.8 = bf16[2,128,128]{2,1,0:T(8,128)(2,1)S(1)} collective-permute-done((bf16[2,128,128]{2,1,0:T(8,128)(2,1)S(1)}, bf16[2,128,128]{2,1,0:T(8,128)(2,1)S(1)}, u32[]{:S(2)}, u32[]{:S(2)}) %collective-permute-start.8) | collective-permute-done | bytes 65568 | tf_op jit(solution)/shard_map/ppermute | solution.py:169
  20.6 0.7 %upgrad.1 = (f32[2,64,384]{2,1,0:T(8,128)S(1)}, bf16[2,64,384]{2,1,0:T(8,128)(2,1)S(1)}) custom-call(bf16[4,128,128]{2,1,0:T(8,128)(2,1)S(1)} %pad_maximum_fusion.refs_0_, bf16[512,512]{1,0:T(8,128)(2,1)S(1)} %get-tuple-element.34.refs_1_, bf16[128,512]{1,0:T(8,128)(2,1)S(1)} %get-tuple-element.35.refs_2_, s32[16,1536]{1,0:T(8,128)S(1)} %get-tuple-element.36.refs_3_), custom_call_target="tpu_custom_call" | custom-call | tf_op jit(solution)/shard_map/upgrad/pallas_call | solution.py:277
  21.3 2.1 %collective-permute-start.9 = (bf16[2,64,384]{2,1,0:T(8,128)(2,1)S(1)}, bf16[2,64,384]{2,1,0:T(8,128)(2,1)S(1)}, u32[]{:S(2)}, u32[]{:S(2)}) collective-permute-start(bf16[2,64,384]{2,1,0:T(8,128)(2,1)S(1)} %get-tuple-element.38), channel_id=1, source_target_pairs={{0,8},{4,12},{8,0},{12,4},{16,24},{20,28},{24,16},{28,20},{1,9},{5... | collective-permute-start | bytes 294920 | tf_op jit(solution)/shard_map/ppermute | solution.py:169
  23.4 1.6 %collective-permute-start.5 = (bf16[1,128,128]{2,1,0:T(8,128)(2,1)S(1)}, bf16[1,128,128]{2,1,0:T(8,128)(2,1)S(1)}, u32[]{:S(2)}, u32[]{:S(2)}) collective-permute-start(bf16[1,128,128]{2,1,0:T(8,128)(2,1)S(1)} %fusion.4.l0), channel_id=1, source_target_pairs={{0,4},{4,0},{8,12},{12,8},{16,20},{20,16},{24,28},{28,24},{1,5},{5... | collective-permute-start | bytes 98312 | tf_op jit(solution)/shard_map/ppermute | solution.py:169
  25.0 1.0 %collective-permute-done.9 = bf16[2,64,384]{2,1,0:T(8,128)(2,1)S(1)} collective-permute-done((bf16[2,64,384]{2,1,0:T(8,128)(2,1)S(1)}, bf16[2,64,384]{2,1,0:T(8,128)(2,1)S(1)}, u32[]{:S(2)}, u32[]{:S(2)}) %collective-permute-start.9) | collective-permute-done | bytes 98336 | tf_op jit(solution)/shard_map/ppermute | solution.py:169
  26.0 2.0 %collective-permute-start.6 = (bf16[1,128,128]{2,1,0:T(8,128)(2,1)S(1)}, bf16[1,128,128]{2,1,0:T(8,128)(2,1)S(1)}, u32[]{:S(2)}, u32[]{:S(2)}) collective-permute-start(bf16[1,128,128]{2,1,0:T(8,128)(2,1)S(1)} %fusion.4.l0), channel_id=1, source_target_pairs={{0,8},{4,12},{8,0},{12,4},{16,24},{20,28},{24,16},{28,20},{1,9},{5... | collective-permute-start | bytes 98312 | tf_op jit(solution)/shard_map/ppermute | solution.py:169
  28.1 1.5 %collective-permute-start.7 = (bf16[1,128,128]{2,1,0:T(8,128)(2,1)S(1)}, bf16[1,128,128]{2,1,0:T(8,128)(2,1)S(1)}, u32[]{:S(2)}, u32[]{:S(2)}) collective-permute-start(bf16[1,128,128]{2,1,0:T(8,128)(2,1)S(1)} %fusion.4.l0), channel_id=1, source_target_pairs={{0,12},{4,8},{8,4},{12,0},{16,28},{20,24},{24,20},{28,16},{1,13},{... | collective-permute-start | bytes 98312 | tf_op jit(solution)/shard_map/ppermute | solution.py:169
  29.9 3.0 %collective-permute-done.7.l3 = bf16[1,128,128]{2,1,0:T(8,128)(2,1)S(1)} collective-permute-done((bf16[1,128,128]{2,1,0:T(8,128)(2,1)S(1)}, bf16[1,128,128]{2,1,0:T(8,128)(2,1)S(1)}, u32[]{:S(2)}, u32[]{:S(2)}) %collective-permute-start.7) | collective-permute-done | bytes 32800 | tf_op jit(solution)/shard_map/ppermute | solution.py:169
  34.4 1.4 %collective-permute-done.14 = bf16[4,192,128]{2,1,0:T(8,128)(2,1)S(1)} collective-permute-done((bf16[4,192,128]{2,1,0:T(8,128)(2,1)S(1)}, bf16[4,192,128]{2,1,0:T(8,128)(2,1)S(1)}, u32[]{:S(2)}, u32[]{:S(2)}) %collective-permute-start.14) | collective-permute-done | bytes 196640 | tf_op jit(solution)/shard_map/ppermute | solution.py:169
  35.9 1.6 %collective-permute-start.15 = (bf16[2,192,128]{2,1,0:T(8,128)(2,1)S(1)}, bf16[2,192,128]{2,1,0:T(8,128)(2,1)S(1)}, u32[]{:S(2)}, u32[]{:S(2)}) collective-permute-start(bf16[2,192,128]{2,1,0:T(8,128)(2,1)S(1)} %fusion.2), channel_id=1, source_target_pairs={{0,2},{1,3},{2,0},{3,1},{4,6},{5,7},{6,4},{7,5},{8,10},{9,11},{10,... | collective-permute-start | bytes 294920 | tf_op jit(solution)/shard_map/ppermute | solution.py:169
  37.4 3.3 %collective-permute-done.15 = bf16[2,192,128]{2,1,0:T(8,128)(2,1)S(1)} collective-permute-done((bf16[2,192,128]{2,1,0:T(8,128)(2,1)S(1)}, bf16[2,192,128]{2,1,0:T(8,128)(2,1)S(1)}, u32[]{:S(2)}, u32[]{:S(2)}) %collective-permute-start.15) | collective-permute-done | bytes 98336 | tf_op jit(solution)/shard_map/ppermute | solution.py:169
  40.8 2.7 %collective-permute-start.16 = (bf16[1,192,128]{2,1,0:T(8,128)(2,1)S(1)}, bf16[1,192,128]{2,1,0:T(8,128)(2,1)S(1)}, u32[]{:S(2)}, u32[]{:S(2)}) collective-permute-start(bf16[1,192,128]{2,1,0:T(8,128)(2,1)S(1)} %fusion.6), channel_id=1, source_target_pairs={{0,16},{4,20},{8,24},{12,28},{16,0},{20,4},{24,8},{28,12},{1,17},{... | collective-permute-start | bytes 147464 | tf_op jit(solution)/shard_map/ppermute | solution.py:169
  43.5 2.4 %collective-permute-done.16.got = bf16[1,192,128]{2,1,0:T(8,128)(2,1)S(1)} collective-permute-done((bf16[1,192,128]{2,1,0:T(8,128)(2,1)S(1)}, bf16[1,192,128]{2,1,0:T(8,128)(2,1)S(1)}, u32[]{:S(2)}, u32[]{:S(2)}) %collective-permute-start.16) | collective-permute-done | bytes 49184 | tf_op jit(solution)/shard_map/ppermute | solution.py:169
  45.9 0.7 %final.1 = (f32[128,128]{1,0:T(8,128)}, f32[64,80]{1,0:T(8,128)}) custom-call(f32[1,192,128]{2,1,0:T(8,128)S(1)} %slice_bitcast_fusion.kept, bf16[1,192,128]{2,1,0:T(8,128)(2,1)S(1)} %collective-permute-done.16.got), custom_call_target="tpu_custom_call" | custom-call | tf_op jit(solution)/shard_map/final/pallas_call | solution.py:309
  (32 shorter events, 2.9 us)
Async XLA Ops:
  1.9 11.2 %collective-permute-start = (bf16[128,768]{1,0:T(8,128)(2,1)S(1)}, bf16[128,768]{1,0:T(8,128)(2,1)S(1)}, u32[]{:S(2)}, u32[]{:S(2)}) collective-permute-start(bf16[128,768]{1,0:T(8,128)(2,1)S(1)} %get-tuple-element.26), channel_id=1, source_target_pairs={{0,1},{1,0},{2,3},{3,2},{4,5},{5,4},{6,7},{7,6},{8,9},{9,8},{10,11... | collective-permute-start | bytes 589832 | tf_op jit(solution)/shard_map/ppermute | solution.py:169
  2.5 9.8 %collective-permute-start.1 = (bf16[128,640]{1,0:T(8,128)(2,1)S(1)}, bf16[128,640]{1,0:T(8,128)(2,1)S(1)}, u32[]{:S(2)}, u32[]{:S(2)}) collective-permute-start(bf16[128,640]{1,0:T(8,128)(2,1)S(1)} %get-tuple-element.27), channel_id=1, source_target_pairs={{0,2},{1,3},{2,0},{3,1},{4,6},{5,7},{6,4},{7,5},{8,10},{9,11},{10,... | collective-permute-start | bytes 491528 | tf_op jit(solution)/shard_map/ppermute | solution.py:169
  5.0 8.1 %collective-permute-start.2 = (bf16[128,640]{1,0:T(8,128)(2,1)S(1)}, bf16[128,640]{1,0:T(8,128)(2,1)S(1)}, u32[]{:S(2)}, u32[]{:S(2)}) collective-permute-start(bf16[128,640]{1,0:T(8,128)(2,1)S(1)} %get-tuple-element.28), channel_id=1, source_target_pairs={{0,3},{1,2},{2,1},{3,0},{4,7},{5,6},{6,5},{7,4},{8,11},{9,10},{10,... | collective-permute-start | bytes 491528 | tf_op jit(solution)/shard_map/ppermute | solution.py:169
  6.6 21.5 %collective-permute-start.11 = (bf16[128,1024]{1,0:T(8,128)(2,1)S(1)}, bf16[128,1024]{1,0:T(8,128)(2,1)S(1)}, u32[]{:S(2)}, u32[]{:S(2)}) collective-permute-start(bf16[128,1024]{1,0:T(8,128)(2,1)S(1)} %get-tuple-element.40), channel_id=1, source_target_pairs={{0,4},{4,0},{8,12},{12,8},{16,20},{20,16},{24,28},{28,24},{1,5},{5... | collective-permute-start | bytes 786440 | tf_op jit(solution)/shard_map/ppermute | solution.py:169
  8.4 21.2 %collective-permute-start.12 = (bf16[128,1024]{1,0:T(8,128)(2,1)S(1)}, bf16[128,1024]{1,0:T(8,128)(2,1)S(1)}, u32[]{:S(2)}, u32[]{:S(2)}) collective-permute-start(bf16[128,1024]{1,0:T(8,128)(2,1)S(1)} %get-tuple-element.41), channel_id=1, source_target_pairs={{0,8},{4,12},{8,0},{12,4},{16,24},{20,28},{24,16},{28,20},{1,9},{5... | collective-permute-start | bytes 786440 | tf_op jit(solution)/shard_map/ppermute | solution.py:169
  12.3 17.5 %collective-permute-start.13 = (bf16[128,1024]{1,0:T(8,128)(2,1)S(1)}, bf16[128,1024]{1,0:T(8,128)(2,1)S(1)}, u32[]{:S(2)}, u32[]{:S(2)}) collective-permute-start(bf16[128,1024]{1,0:T(8,128)(2,1)S(1)} %get-tuple-element.42), channel_id=1, source_target_pairs={{0,12},{4,8},{8,4},{12,0},{16,28},{20,24},{24,20},{28,16},{1,13},{... | collective-permute-start | bytes 786440 | tf_op jit(solution)/shard_map/ppermute | solution.py:169
  15.8 2.2 %collective-permute-start.3 = (f32[2,128,128]{2,1,0:T(8,128)S(1)}, f32[2,128,128]{2,1,0:T(8,128)S(1)}, u32[]{:S(2)}, u32[]{:S(2)}) collective-permute-start(f32[2,128,128]{2,1,0:T(8,128)S(1)} %get-tuple-element.33), channel_id=1, source_target_pairs={{0,1},{1,0},{2,3},{3,2},{4,5},{5,4},{6,7},{7,6},{8,9},{9,8},{10,11... | collective-permute-start | bytes 393224 | tf_op jit(solution)/shard_map/ppermute | solution.py:169
  16.1 4.4 %collective-permute-start.8 = (bf16[2,128,128]{2,1,0:T(8,128)(2,1)S(1)}, bf16[2,128,128]{2,1,0:T(8,128)(2,1)S(1)}, u32[]{:S(2)}, u32[]{:S(2)}) collective-permute-start(bf16[2,128,128]{2,1,0:T(8,128)(2,1)S(1)} %pad_maximum_fusion.1), channel_id=1, source_target_pairs={{0,2},{1,3},{2,0},{3,1},{4,6},{5,7},{6,4},{7,5},{8,10},{9,11},{10,... | collective-permute-start | bytes 196616 | tf_op jit(solution)/shard_map/ppermute | solution.py:169
  18.0 5.4 %collective-permute-start.4 = (bf16[1,128,128]{2,1,0:T(8,128)(2,1)S(1)}, bf16[1,128,128]{2,1,0:T(8,128)(2,1)S(1)}, u32[]{:S(2)}, u32[]{:S(2)}) collective-permute-start(bf16[1,128,128]{2,1,0:T(8,128)(2,1)S(1)} %fusion.7), channel_id=1, source_target_pairs={{0,2},{1,3},{2,0},{3,1},{4,6},{5,7},{6,4},{7,5},{8,10},{9,11},{10,... | collective-permute-start | bytes 98312 | tf_op jit(solution)/shard_map/ppermute | solution.py:169
  21.3 4.7 %collective-permute-start.9 = (bf16[2,64,384]{2,1,0:T(8,128)(2,1)S(1)}, bf16[2,64,384]{2,1,0:T(8,128)(2,1)S(1)}, u32[]{:S(2)}, u32[]{:S(2)}) collective-permute-start(bf16[2,64,384]{2,1,0:T(8,128)(2,1)S(1)} %get-tuple-element.38), channel_id=1, source_target_pairs={{0,8},{4,12},{8,0},{12,4},{16,24},{20,28},{24,16},{28,20},{1,9},{5... | collective-permute-start | bytes 294920 | tf_op jit(solution)/shard_map/ppermute | solution.py:169
  23.4 6.3 %collective-permute-start.5 = (bf16[1,128,128]{2,1,0:T(8,128)(2,1)S(1)}, bf16[1,128,128]{2,1,0:T(8,128)(2,1)S(1)}, u32[]{:S(2)}, u32[]{:S(2)}) collective-permute-start(bf16[1,128,128]{2,1,0:T(8,128)(2,1)S(1)} %fusion.4.l0), channel_id=1, source_target_pairs={{0,4},{4,0},{8,12},{12,8},{16,20},{20,16},{24,28},{28,24},{1,5},{5... | collective-permute-start | bytes 98312 | tf_op jit(solution)/shard_map/ppermute | solution.py:169
  26.0 3.9 %collective-permute-start.6 = (bf16[1,128,128]{2,1,0:T(8,128)(2,1)S(1)}, bf16[1,128,128]{2,1,0:T(8,128)(2,1)S(1)}, u32[]{:S(2)}, u32[]{:S(2)}) collective-permute-start(bf16[1,128,128]{2,1,0:T(8,128)(2,1)S(1)} %fusion.4.l0), channel_id=1, source_target_pairs={{0,8},{4,12},{8,0},{12,4},{16,24},{20,28},{24,16},{28,20},{1,9},{5... | collective-permute-start | bytes 98312 | tf_op jit(solution)/shard_map/ppermute | solution.py:169
  28.1 4.9 %collective-permute-start.7 = (bf16[1,128,128]{2,1,0:T(8,128)(2,1)S(1)}, bf16[1,128,128]{2,1,0:T(8,128)(2,1)S(1)}, u32[]{:S(2)}, u32[]{:S(2)}) collective-permute-start(bf16[1,128,128]{2,1,0:T(8,128)(2,1)S(1)} %fusion.4.l0), channel_id=1, source_target_pairs={{0,12},{4,8},{8,4},{12,0},{16,28},{20,24},{24,20},{28,16},{1,13},{... | collective-permute-start | bytes 98312 | tf_op jit(solution)/shard_map/ppermute | solution.py:169
  29.6 4.1 %collective-permute-start.10 = (bf16[64,384]{1,0:T(8,128)(2,1)S(1)}, bf16[64,384]{1,0:T(8,128)(2,1)S(1)}, u32[]{:S(2)}, u32[]{:S(2)}) collective-permute-start(bf16[64,384]{1,0:T(8,128)(2,1)S(1)} %fusion.5), channel_id=1, source_target_pairs={{0,4},{4,0},{8,12},{12,8},{16,20},{20,16},{24,28},{28,24},{1,5},{5... | collective-permute-start | bytes 147464 | tf_op jit(solution)/shard_map/ppermute | solution.py:169
  34.3 1.5 %collective-permute-start.14 = (bf16[4,192,128]{2,1,0:T(8,128)(2,1)S(1)}, bf16[4,192,128]{2,1,0:T(8,128)(2,1)S(1)}, u32[]{:S(2)}, u32[]{:S(2)}) collective-permute-start(bf16[4,192,128]{2,1,0:T(8,128)(2,1)S(1)} %get-tuple-element.45), channel_id=1, source_target_pairs={{0,1},{1,0},{2,3},{3,2},{4,5},{5,4},{6,7},{7,6},{8,9},{9,8},{10,11... | collective-permute-start | bytes 589832 | tf_op jit(solution)/shard_map/ppermute | solution.py:169
  35.9 4.9 %collective-permute-start.15 = (bf16[2,192,128]{2,1,0:T(8,128)(2,1)S(1)}, bf16[2,192,128]{2,1,0:T(8,128)(2,1)S(1)}, u32[]{:S(2)}, u32[]{:S(2)}) collective-permute-start(bf16[2,192,128]{2,1,0:T(8,128)(2,1)S(1)} %fusion.2), channel_id=1, source_target_pairs={{0,2},{1,3},{2,0},{3,1},{4,6},{5,7},{6,4},{7,5},{8,10},{9,11},{10,... | collective-permute-start | bytes 294920 | tf_op jit(solution)/shard_map/ppermute | solution.py:169
  40.8 5.1 %collective-permute-start.16 = (bf16[1,192,128]{2,1,0:T(8,128)(2,1)S(1)}, bf16[1,192,128]{2,1,0:T(8,128)(2,1)S(1)}, u32[]{:S(2)}, u32[]{:S(2)}) collective-permute-start(bf16[1,192,128]{2,1,0:T(8,128)(2,1)S(1)} %fusion.6), channel_id=1, source_target_pairs={{0,16},{4,20},{8,24},{12,28},{16,0},{20,4},{24,8},{28,12},{1,17},{... | collective-permute-start | bytes 147464 | tf_op jit(solution)/shard_map/ppermute | solution.py:169

commit v6 on v5

--- a/solution.py
+++ b/solution.py
@@ -81,34 +81,53 @@
     dk_buf[...] = jnp.zeros_like(dk_buf)
     row_in = lax.broadcasted_iota(jnp.int32, (tok, 1), 0)
     col_in = lax.broadcasted_iota(jnp.int32, (tok, tok), 1)
-    for p in range(C):
+
+    def scores_of(p, g):
+        start, ext = p * tok, (p + 1) * tok
+        q_all = q_buf[g * per_key : (g + 1) * per_key, start:ext, :].reshape(per_key * tok, DH)
+        return q_all, dot32(q_all, k_buf[:ext, g * DH : (g + 1) * DH], NT)
+
+    def grads_of(p, g, scores):
         start, ext = p * tok, (p + 1) * tok
         row_pos = row_in + start
         visible = (col_in + start) <= jnp.minimum(row_pos, length - 1)
         weight = jnp.where(row_pos < length, 1.0 / H, 0.0)
-        for g in range(kh):
-            keys = k_buf[:ext, g * DH : (g + 1) * DH]
-            heads = range(g * per_key, (g + 1) * per_key)
-            q_all = q_buf[g * per_key : (g + 1) * per_key, start:ext, :].reshape(per_key * tok, DH)
-            scores = dot32(q_all, keys, NT)
-            grads = []
-            for n, h in enumerate(heads):
-                sc = scores[n * tok : (n + 1) * tok]
-                diag = jnp.where(visible, sc[:, start:], -1e30)
-                sc = diag if p == 0 else jnp.concatenate([sc[:, :start], diag], axis=1)
-                te_d = jnp.where(visible, teacher[h, start:ext, start:ext].astype(jnp.float32), 0.0)
-                te = te_d if p == 0 else jnp.concatenate(
-                    [teacher[h, start:ext, :start].astype(jnp.float32), te_d], axis=1
-                )
-                ex = jnp.exp2((sc - jnp.max(sc, axis=1, keepdims=True)) * exp_scale)
-                w_s = weight / jnp.sum(ex, axis=1, keepdims=True)
-                w_t = weight / jnp.sum(te, axis=1, keepdims=True)
-                grads.append((ex * w_s - te * w_t).astype(jnp.bfloat16))
-            grad = grads[0] if per_key == 1 else jnp.concatenate(grads, axis=0)
-            dq = (dot32(grad, keys) * scale).astype(jnp.bfloat16)
-            for n, h in enumerate(heads):
-                dq_buf[start:ext, h * DH : (h + 1) * DH] = dq[n * tok : (n + 1) * tok]
-            dk_buf[g * DH : (g + 1) * DH, :ext] += dot32(q_all, grad, TN)
+        grads = []
+        for n in range(per_key):
+            h = g * per_key + n
+            sc = scores[n * tok : (n + 1) * tok]
+            diag = jnp.where(visible, sc[:, start:], -1e30)
+            sc = diag if p == 0 else jnp.concatenate([sc[:, :start], diag], axis=1)
+            te_d = jnp.where(visible, teacher[h, start:ext, start:ext].astype(jnp.float32), 0.0)
+            te = te_d if p == 0 else jnp.concatenate(
+                [teacher[h, start:ext, :start].astype(jnp.float32), te_d], axis=1
+            )
+            ex = jnp.exp2((sc - jnp.max(sc, axis=1, keepdims=True)) * exp_scale)
+            w_s = weight / jnp.sum(ex, axis=1, keepdims=True)
+            w_t = weight / jnp.sum(te, axis=1, keepdims=True)
+            grads.append((ex * w_s - te * w_t).astype(jnp.bfloat16))
+        return grads[0] if per_key == 1 else jnp.concatenate(grads, axis=0)
+
+    def products_of(p, g, q_all, grad):
+        start, ext = p * tok, (p + 1) * tok
+        dq = (dot32(grad, k_buf[:ext, g * DH : (g + 1) * DH]) * scale).astype(jnp.bfloat16)
+        for n in range(per_key):
+            h = g * per_key + n
+            dq_buf[start:ext, h * DH : (h + 1) * DH] = dq[n * tok : (n + 1) * tok]
+        dk_buf[g * DH : (g + 1) * DH, :ext] += dot32(q_all, grad, TN)
+
+    steps = [(p, g) for p in reversed(range(C)) for g in range(kh)]
+    lag, ready, done = 1, {}, {}
+    for i in range(len(steps) + 2 * lag):
+        if i < len(steps):
+            ready[i] = scores_of(*steps[i])
+        j = i - lag
+        if 0 <= j < len(steps):
+            q_all, scores = ready.pop(j)
+            done[j] = q_all, grads_of(*steps[j], scores)
+        j = i - 2 * lag
+        if 0 <= j < len(steps):
+            products_of(*steps[j], *done.pop(j))
     dq = dq_buf[...]
     dk = (dk_buf[...] * scale).astype(jnp.bfloat16)
     dk_out[...] = dk

time: 46.9 us -> 46.4 us (0.989)
  transfers between devices with their start and end apart: 17 -> 17, of which waited for: 8 -> 8; matrix products, arithmetic and copies ran while one was open for 0% -> 0% of each run, Pallas kernels for 14% -> 13%
where the time goes in v6:
time: 46.4 us; the launch traced here: 46.2 us
  starting transfers between devices  22.2 us (48%)
  waiting for transfers between devices  13.7 us (30%)
  Pallas kernels  8.65 us (19%)
  between operations  1.44 us (3%)
    ppermute x17, starting transfers between devices, swap(): return lax.ppermute(x, axis, [(i, i ^ s) for i in range(mesh.shape[axis])])  22.2 us
    ppermute x17, waiting for transfers between devices, swap(): return lax.ppermute(x, axis, [(i, i ^ s) for i in range(mesh.shape[axis])])  13.7 us
    pallas_call x3, Pallas kernels, slices(): pl.pallas_call(functools.partial(slice_kernel, plan, len(ins)), out_shape...  4.42 us
    pallas_call x1, Pallas kernels, body(): pl.pallas_call(functools.partial(attend_kernel, C, tok, hq, kh, DH, H, R)...  2.15 us
  transfers between devices with their start and end apart: 17, of which 8 were waited for; matrix products, arithmetic and copies ran while one was open for 0% of the time, Pallas kernels for 13%

profile of v6, /device:TPU:0, one launch (start us, length us, event | category | flops | bytes accessed | tf_op | source)
XLA Modules:
  0.0 46.2 jit_solution(2131095960433626627)
XLA Ops:
  0.6 1.3 %shard_map.104 = (bf16[128,768]{1,0:T(8,128)(2,1)S(1)}, bf16[128,768]{1,0:T(8,128)(2,1)S(1)}, bf16[128,640]{1,0:T(8,128)(2,1)S(1)}, bf16[128,640]{1,0:T(8,128)(2,1)S(1)}) custom-call(bf16[128,2048]{1,0:T(8,128)(2,1)} %bitcast.44, bf16[128,512]{1,0:T(8,128)(2,1)} %bitcast.46, bf16[128,128]{1,0:T(8,128)(2,1)} %bitcast.47), custom_call_target="tpu_custom_call" | custom-call | tf_op jit(solution)/shard_map/pallas_call | solution.py:57
  2.5 2.6 %collective-permute-start.1 = (bf16[128,640]{1,0:T(8,128)(2,1)S(1)}, bf16[128,640]{1,0:T(8,128)(2,1)S(1)}, u32[]{:S(2)}, u32[]{:S(2)}) collective-permute-start(bf16[128,640]{1,0:T(8,128)(2,1)S(1)} %get-tuple-element.27), channel_id=1, source_target_pairs={{0,2},{1,3},{2,0},{3,1},{4,6},{5,7},{6,4},{7,5},{8,10},{9,11},{10,... | collective-permute-start | bytes 491528 | tf_op jit(solution)/shard_map/ppermute | solution.py:188
  5.1 1.5 %shard_map.106 = (bf16[128,1024]{1,0:T(8,128)(2,1)S(1)}, bf16[128,1024]{1,0:T(8,128)(2,1)S(1)}, bf16[128,1024]{1,0:T(8,128)(2,1)S(1)}, bf16[128,1024]{1,0:T(8,128)(2,1)S(1)}) custom-call(bf16[128,4096]{1,0:T(8,128)(2,1)} %bitcast.43), custom_call_target="tpu_custom_call" | custom-call | tf_op jit(solution)/shard_map/pallas_call | solution.py:57
  6.6 1.8 %collective-permute-start.11 = (bf16[128,1024]{1,0:T(8,128)(2,1)S(1)}, bf16[128,1024]{1,0:T(8,128)(2,1)S(1)}, u32[]{:S(2)}, u32[]{:S(2)}) collective-permute-start(bf16[128,1024]{1,0:T(8,128)(2,1)S(1)} %get-tuple-element.40), channel_id=1, source_target_pairs={{0,4},{4,0},{8,12},{12,8},{16,20},{20,16},{24,28},{28,24},{1,5},{5... | collective-permute-start | bytes 786440 | tf_op jit(solution)/shard_map/ppermute | solution.py:188
  8.4 1.6 %collective-permute-start.12 = (bf16[128,1024]{1,0:T(8,128)(2,1)S(1)}, bf16[128,1024]{1,0:T(8,128)(2,1)S(1)}, u32[]{:S(2)}, u32[]{:S(2)}) collective-permute-start(bf16[128,1024]{1,0:T(8,128)(2,1)S(1)} %get-tuple-element.41), channel_id=1, source_target_pairs={{0,8},{4,12},{8,0},{12,4},{16,24},{20,28},{24,16},{28,20},{1,9},{5... | collective-permute-start | bytes 786440 | tf_op jit(solution)/shard_map/ppermute | solution.py:188
  10.6 1.6 %shard_map.105 = (bf16[4,512,512]{2,1,0:T(8,128)(2,1)S(1)}, bf16[64,512]{1,0:T(8,128)(2,1)S(1)}, bf16[64,128]{1,0:T(8,128)(2,1)S(1)}, s32[16,1536]{1,0:T(8,128)S(1)}, s32[16,384]{1,0:T(8,128)S(1)}) custom-call(bf16[4,512,512]{2,1,0:T(8,128)(2,1)} %bitcast.40, bf16[64,2560]{1,0:T(8,128)(2,1)} %bitcast.45, s32[16,1536]{1,0:T(8,128)} %constant.4.clone.refs_2_, ...), custom_call_target="tpu_custom_call" | custom-call | tf_op jit(solution)/shard_map/pallas_call | solution.py:57
  12.3 0.9 %collective-permute-start.13 = (bf16[128,1024]{1,0:T(8,128)(2,1)S(1)}, bf16[128,1024]{1,0:T(8,128)(2,1)S(1)}, u32[]{:S(2)}, u32[]{:S(2)}) collective-permute-start(bf16[128,1024]{1,0:T(8,128)(2,1)S(1)} %get-tuple-element.42), channel_id=1, source_target_pairs={{0,12},{4,8},{8,4},{12,0},{16,28},{20,24},{24,20},{28,16},{1,13},{... | collective-permute-start | bytes 786440 | tf_op jit(solution)/shard_map/ppermute | solution.py:188
  13.2 2.1 %attend.1 = (f32[2,128,128]{2,1,0:T(8,128)S(1)}, f32[2,128,128]{2,1,0:T(8,128)S(1)}, bf16[512,512]{1,0:T(8,128)(2,1)S(1)}, bf16[128,512]{1,0:T(8,128)(2,1)S(1)}) custom-call(s32[1]{0:T(128)S(6)} %copy.23.lengths, bf16[128,768]{1,0:T(8,128)(2,1)S(1)} %get-tuple-element.25.refs_0_, bf16[128,768]{1,0:T(8,128)(2,1)S(1)} %collective-permute-done.refs_1_, ...), custom_call_target="tpu_custom_call" | custom-call | tf_op jit(solution)/shard_map/attend/pallas_call | solution.py:271
  15.7 1.8 %collective-permute-start.8 = (bf16[2,128,128]{2,1,0:T(8,128)(2,1)S(1)}, bf16[2,128,128]{2,1,0:T(8,128)(2,1)S(1)}, u32[]{:S(2)}, u32[]{:S(2)}) collective-permute-start(bf16[2,128,128]{2,1,0:T(8,128)(2,1)S(1)} %pad_maximum_fusion.1), channel_id=1, source_target_pairs={{0,2},{1,3},{2,0},{3,1},{4,6},{5,7},{6,4},{7,5},{8,10},{9,11},{10,... | collective-permute-start | bytes 196616 | tf_op jit(solution)/shard_map/ppermute | solution.py:188
  17.5 1.0 %collective-permute-start.4 = (bf16[1,128,128]{2,1,0:T(8,128)(2,1)S(1)}, bf16[1,128,128]{2,1,0:T(8,128)(2,1)S(1)}, u32[]{:S(2)}, u32[]{:S(2)}) collective-permute-start(bf16[1,128,128]{2,1,0:T(8,128)(2,1)S(1)} %fusion.7), channel_id=1, source_target_pairs={{0,2},{1,3},{2,0},{3,1},{4,6},{5,7},{6,4},{7,5},{8,10},{9,11},{10,... | collective-permute-start | bytes 98312 | tf_op jit(solution)/shard_map/ppermute | solution.py:188
  18.5 1.6 %collective-permute-done.8 = bf16[2,128,128]{2,1,0:T(8,128)(2,1)S(1)} collective-permute-done((bf16[2,128,128]{2,1,0:T(8,128)(2,1)S(1)}, bf16[2,128,128]{2,1,0:T(8,128)(2,1)S(1)}, u32[]{:S(2)}, u32[]{:S(2)}) %collective-permute-start.8) | collective-permute-done | bytes 65568 | tf_op jit(solution)/shard_map/ppermute | solution.py:188
  20.1 0.7 %upgrad.1 = (f32[2,64,384]{2,1,0:T(8,128)S(1)}, bf16[2,64,384]{2,1,0:T(8,128)(2,1)S(1)}) custom-call(bf16[4,128,128]{2,1,0:T(8,128)(2,1)S(1)} %pad_maximum_fusion.refs_0_, bf16[512,512]{1,0:T(8,128)(2,1)S(1)} %get-tuple-element.34.refs_1_, bf16[128,512]{1,0:T(8,128)(2,1)S(1)} %get-tuple-element.35.refs_2_, s32[16,1536]{1,0:T(8,128)S(1)} %get-tuple-element.36.refs_3_), custom_call_target="tpu_custom_call" | custom-call | tf_op jit(solution)/shard_map/upgrad/pallas_call | solution.py:296
  20.9 2.1 %collective-permute-start.9 = (bf16[2,64,384]{2,1,0:T(8,128)(2,1)S(1)}, bf16[2,64,384]{2,1,0:T(8,128)(2,1)S(1)}, u32[]{:S(2)}, u32[]{:S(2)}) collective-permute-start(bf16[2,64,384]{2,1,0:T(8,128)(2,1)S(1)} %get-tuple-element.38), channel_id=1, source_target_pairs={{0,8},{4,12},{8,0},{12,4},{16,24},{20,28},{24,16},{28,20},{1,9},{5... | collective-permute-start | bytes 294920 | tf_op jit(solution)/shard_map/ppermute | solution.py:188
  23.0 1.6 %collective-permute-start.5 = (bf16[1,128,128]{2,1,0:T(8,128)(2,1)S(1)}, bf16[1,128,128]{2,1,0:T(8,128)(2,1)S(1)}, u32[]{:S(2)}, u32[]{:S(2)}) collective-permute-start(bf16[1,128,128]{2,1,0:T(8,128)(2,1)S(1)} %fusion.4.l0), channel_id=1, source_target_pairs={{0,4},{4,0},{8,12},{12,8},{16,20},{20,16},{24,28},{28,24},{1,5},{5... | collective-permute-start | bytes 98312 | tf_op jit(solution)/shard_map/ppermute | solution.py:188
  24.6 1.0 %collective-permute-done.9 = bf16[2,64,384]{2,1,0:T(8,128)(2,1)S(1)} collective-permute-done((bf16[2,64,384]{2,1,0:T(8,128)(2,1)S(1)}, bf16[2,64,384]{2,1,0:T(8,128)(2,1)S(1)}, u32[]{:S(2)}, u32[]{:S(2)}) %collective-permute-start.9) | collective-permute-done | bytes 98336 | tf_op jit(solution)/shard_map/ppermute | solution.py:188
  25.6 2.0 %collective-permute-start.6 = (bf16[1,128,128]{2,1,0:T(8,128)(2,1)S(1)}, bf16[1,128,128]{2,1,0:T(8,128)(2,1)S(1)}, u32[]{:S(2)}, u32[]{:S(2)}) collective-permute-start(bf16[1,128,128]{2,1,0:T(8,128)(2,1)S(1)} %fusion.4.l0), channel_id=1, source_target_pairs={{0,8},{4,12},{8,0},{12,4},{16,24},{20,28},{24,16},{28,20},{1,9},{5... | collective-permute-start | bytes 98312 | tf_op jit(solution)/shard_map/ppermute | solution.py:188
  27.7 1.5 %collective-permute-start.7 = (bf16[1,128,128]{2,1,0:T(8,128)(2,1)S(1)}, bf16[1,128,128]{2,1,0:T(8,128)(2,1)S(1)}, u32[]{:S(2)}, u32[]{:S(2)}) collective-permute-start(bf16[1,128,128]{2,1,0:T(8,128)(2,1)S(1)} %fusion.4.l0), channel_id=1, source_target_pairs={{0,12},{4,8},{8,4},{12,0},{16,28},{20,24},{24,20},{28,16},{1,13},{... | collective-permute-start | bytes 98312 | tf_op jit(solution)/shard_map/ppermute | solution.py:188
  29.5 3.0 %collective-permute-done.7.l3 = bf16[1,128,128]{2,1,0:T(8,128)(2,1)S(1)} collective-permute-done((bf16[1,128,128]{2,1,0:T(8,128)(2,1)S(1)}, bf16[1,128,128]{2,1,0:T(8,128)(2,1)S(1)}, u32[]{:S(2)}, u32[]{:S(2)}) %collective-permute-start.7) | collective-permute-done | bytes 32800 | tf_op jit(solution)/shard_map/ppermute | solution.py:188
  33.9 1.4 %collective-permute-done.14 = bf16[4,192,128]{2,1,0:T(8,128)(2,1)S(1)} collective-permute-done((bf16[4,192,128]{2,1,0:T(8,128)(2,1)S(1)}, bf16[4,192,128]{2,1,0:T(8,128)(2,1)S(1)}, u32[]{:S(2)}, u32[]{:S(2)}) %collective-permute-start.14) | collective-permute-done | bytes 196640 | tf_op jit(solution)/shard_map/ppermute | solution.py:188
  35.4 1.5 %collective-permute-start.15 = (bf16[2,192,128]{2,1,0:T(8,128)(2,1)S(1)}, bf16[2,192,128]{2,1,0:T(8,128)(2,1)S(1)}, u32[]{:S(2)}, u32[]{:S(2)}) collective-permute-start(bf16[2,192,128]{2,1,0:T(8,128)(2,1)S(1)} %fusion.2), channel_id=1, source_target_pairs={{0,2},{1,3},{2,0},{3,1},{4,6},{5,7},{6,4},{7,5},{8,10},{9,11},{10,... | collective-permute-start | bytes 294920 | tf_op jit(solution)/shard_map/ppermute | solution.py:188
  37.0 3.4 %collective-permute-done.15 = bf16[2,192,128]{2,1,0:T(8,128)(2,1)S(1)} collective-permute-done((bf16[2,192,128]{2,1,0:T(8,128)(2,1)S(1)}, bf16[2,192,128]{2,1,0:T(8,128)(2,1)S(1)}, u32[]{:S(2)}, u32[]{:S(2)}) %collective-permute-start.15) | collective-permute-done | bytes 98336 | tf_op jit(solution)/shard_map/ppermute | solution.py:188
  40.4 2.7 %collective-permute-start.16 = (bf16[1,192,128]{2,1,0:T(8,128)(2,1)S(1)}, bf16[1,192,128]{2,1,0:T(8,128)(2,1)S(1)}, u32[]{:S(2)}, u32[]{:S(2)}) collective-permute-start(bf16[1,192,128]{2,1,0:T(8,128)(2,1)S(1)} %fusion.6), channel_id=1, source_target_pairs={{0,16},{4,20},{8,24},{12,28},{16,0},{20,4},{24,8},{28,12},{1,17},{... | collective-permute-start | bytes 147464 | tf_op jit(solution)/shard_map/ppermute | solution.py:188
  43.0 2.4 %collective-permute-done.16.got = bf16[1,192,128]{2,1,0:T(8,128)(2,1)S(1)} collective-permute-done((bf16[1,192,128]{2,1,0:T(8,128)(2,1)S(1)}, bf16[1,192,128]{2,1,0:T(8,128)(2,1)S(1)}, u32[]{:S(2)}, u32[]{:S(2)}) %collective-permute-start.16) | collective-permute-done | bytes 49184 | tf_op jit(solution)/shard_map/ppermute | solution.py:188
  45.4 0.7 %final.1 = (f32[128,128]{1,0:T(8,128)}, f32[64,80]{1,0:T(8,128)}) custom-call(f32[1,192,128]{2,1,0:T(8,128)S(1)} %slice_bitcast_fusion.kept, bf16[1,192,128]{2,1,0:T(8,128)(2,1)S(1)} %collective-permute-done.16.got), custom_call_target="tpu_custom_call" | custom-call | tf_op jit(solution)/shard_map/final/pallas_call | solution.py:328
  (32 shorter events, 2.9 us)
Async XLA Ops:
  1.9 11.2 %collective-permute-start = (bf16[128,768]{1,0:T(8,128)(2,1)S(1)}, bf16[128,768]{1,0:T(8,128)(2,1)S(1)}, u32[]{:S(2)}, u32[]{:S(2)}) collective-permute-start(bf16[128,768]{1,0:T(8,128)(2,1)S(1)} %get-tuple-element.26), channel_id=1, source_target_pairs={{0,1},{1,0},{2,3},{3,2},{4,5},{5,4},{6,7},{7,6},{8,9},{9,8},{10,11... | collective-permute-start | bytes 589832 | tf_op jit(solution)/shard_map/ppermute | solution.py:188
  2.5 9.8 %collective-permute-start.1 = (bf16[128,640]{1,0:T(8,128)(2,1)S(1)}, bf16[128,640]{1,0:T(8,128)(2,1)S(1)}, u32[]{:S(2)}, u32[]{:S(2)}) collective-permute-start(bf16[128,640]{1,0:T(8,128)(2,1)S(1)} %get-tuple-element.27), channel_id=1, source_target_pairs={{0,2},{1,3},{2,0},{3,1},{4,6},{5,7},{6,4},{7,5},{8,10},{9,11},{10,... | collective-permute-start | bytes 491528 | tf_op jit(solution)/shard_map/ppermute | solution.py:188
  5.0 8.1 %collective-permute-start.2 = (bf16[128,640]{1,0:T(8,128)(2,1)S(1)}, bf16[128,640]{1,0:T(8,128)(2,1)S(1)}, u32[]{:S(2)}, u32[]{:S(2)}) collective-permute-start(bf16[128,640]{1,0:T(8,128)(2,1)S(1)} %get-tuple-element.28), channel_id=1, source_target_pairs={{0,3},{1,2},{2,1},{3,0},{4,7},{5,6},{6,5},{7,4},{8,11},{9,10},{10,... | collective-permute-start | bytes 491528 | tf_op jit(solution)/shard_map/ppermute | solution.py:188
  6.6 21.1 %collective-permute-start.11 = (bf16[128,1024]{1,0:T(8,128)(2,1)S(1)}, bf16[128,1024]{1,0:T(8,128)(2,1)S(1)}, u32[]{:S(2)}, u32[]{:S(2)}) collective-permute-start(bf16[128,1024]{1,0:T(8,128)(2,1)S(1)} %get-tuple-element.40), channel_id=1, source_target_pairs={{0,4},{4,0},{8,12},{12,8},{16,20},{20,16},{24,28},{28,24},{1,5},{5... | collective-permute-start | bytes 786440 | tf_op jit(solution)/shard_map/ppermute | solution.py:188
  8.4 20.7 %collective-permute-start.12 = (bf16[128,1024]{1,0:T(8,128)(2,1)S(1)}, bf16[128,1024]{1,0:T(8,128)(2,1)S(1)}, u32[]{:S(2)}, u32[]{:S(2)}) collective-permute-start(bf16[128,1024]{1,0:T(8,128)(2,1)S(1)} %get-tuple-element.41), channel_id=1, source_target_pairs={{0,8},{4,12},{8,0},{12,4},{16,24},{20,28},{24,16},{28,20},{1,9},{5... | collective-permute-start | bytes 786440 | tf_op jit(solution)/shard_map/ppermute | solution.py:188
  12.3 17.0 %collective-permute-start.13 = (bf16[128,1024]{1,0:T(8,128)(2,1)S(1)}, bf16[128,1024]{1,0:T(8,128)(2,1)S(1)}, u32[]{:S(2)}, u32[]{:S(2)}) collective-permute-start(bf16[128,1024]{1,0:T(8,128)(2,1)S(1)} %get-tuple-element.42), channel_id=1, source_target_pairs={{0,12},{4,8},{8,4},{12,0},{16,28},{20,24},{24,20},{28,16},{1,13},{... | collective-permute-start | bytes 786440 | tf_op jit(solution)/shard_map/ppermute | solution.py:188
  15.3 2.2 %collective-permute-start.3 = (f32[2,128,128]{2,1,0:T(8,128)S(1)}, f32[2,128,128]{2,1,0:T(8,128)S(1)}, u32[]{:S(2)}, u32[]{:S(2)}) collective-permute-start(f32[2,128,128]{2,1,0:T(8,128)S(1)} %get-tuple-element.33), channel_id=1, source_target_pairs={{0,1},{1,0},{2,3},{3,2},{4,5},{5,4},{6,7},{7,6},{8,9},{9,8},{10,11... | collective-permute-start | bytes 393224 | tf_op jit(solution)/shard_map/ppermute | solution.py:188
  15.7 4.4 %collective-permute-start.8 = (bf16[2,128,128]{2,1,0:T(8,128)(2,1)S(1)}, bf16[2,128,128]{2,1,0:T(8,128)(2,1)S(1)}, u32[]{:S(2)}, u32[]{:S(2)}) collective-permute-start(bf16[2,128,128]{2,1,0:T(8,128)(2,1)S(1)} %pad_maximum_fusion.1), channel_id=1, source_target_pairs={{0,2},{1,3},{2,0},{3,1},{4,6},{5,7},{6,4},{7,5},{8,10},{9,11},{10,... | collective-permute-start | bytes 196616 | tf_op jit(solution)/shard_map/ppermute | solution.py:188
  17.5 5.5 %collective-permute-start.4 = (bf16[1,128,128]{2,1,0:T(8,128)(2,1)S(1)}, bf16[1,128,128]{2,1,0:T(8,128)(2,1)S(1)}, u32[]{:S(2)}, u32[]{:S(2)}) collective-permute-start(bf16[1,128,128]{2,1,0:T(8,128)(2,1)S(1)} %fusion.7), channel_id=1, source_target_pairs={{0,2},{1,3},{2,0},{3,1},{4,6},{5,7},{6,4},{7,5},{8,10},{9,11},{10,... | collective-permute-start | bytes 98312 | tf_op jit(solution)/shard_map/ppermute | solution.py:188
  20.9 4.7 %collective-permute-start.9 = (bf16[2,64,384]{2,1,0:T(8,128)(2,1)S(1)}, bf16[2,64,384]{2,1,0:T(8,128)(2,1)S(1)}, u32[]{:S(2)}, u32[]{:S(2)}) collective-permute-start(bf16[2,64,384]{2,1,0:T(8,128)(2,1)S(1)} %get-tuple-element.38), channel_id=1, source_target_pairs={{0,8},{4,12},{8,0},{12,4},{16,24},{20,28},{24,16},{28,20},{1,9},{5... | collective-permute-start | bytes 294920 | tf_op jit(solution)/shard_map/ppermute | solution.py:188
  23.0 6.3 %collective-permute-start.5 = (bf16[1,128,128]{2,1,0:T(8,128)(2,1)S(1)}, bf16[1,128,128]{2,1,0:T(8,128)(2,1)S(1)}, u32[]{:S(2)}, u32[]{:S(2)}) collective-permute-start(bf16[1,128,128]{2,1,0:T(8,128)(2,1)S(1)} %fusion.4.l0), channel_id=1, source_target_pairs={{0,4},{4,0},{8,12},{12,8},{16,20},{20,16},{24,28},{28,24},{1,5},{5... | collective-permute-start | bytes 98312 | tf_op jit(solution)/shard_map/ppermute | solution.py:188
  25.6 3.9 %collective-permute-start.6 = (bf16[1,128,128]{2,1,0:T(8,128)(2,1)S(1)}, bf16[1,128,128]{2,1,0:T(8,128)(2,1)S(1)}, u32[]{:S(2)}, u32[]{:S(2)}) collective-permute-start(bf16[1,128,128]{2,1,0:T(8,128)(2,1)S(1)} %fusion.4.l0), channel_id=1, source_target_pairs={{0,8},{4,12},{8,0},{12,4},{16,24},{20,28},{24,16},{28,20},{1,9},{5... | collective-permute-start | bytes 98312 | tf_op jit(solution)/shard_map/ppermute | solution.py:188
  27.7 4.9 %collective-permute-start.7 = (bf16[1,128,128]{2,1,0:T(8,128)(2,1)S(1)}, bf16[1,128,128]{2,1,0:T(8,128)(2,1)S(1)}, u32[]{:S(2)}, u32[]{:S(2)}) collective-permute-start(bf16[1,128,128]{2,1,0:T(8,128)(2,1)S(1)} %fusion.4.l0), channel_id=1, source_target_pairs={{0,12},{4,8},{8,4},{12,0},{16,28},{20,24},{24,20},{28,16},{1,13},{... | collective-permute-start | bytes 98312 | tf_op jit(solution)/shard_map/ppermute | solution.py:188
  29.1 4.1 %collective-permute-start.10 = (bf16[64,384]{1,0:T(8,128)(2,1)S(1)}, bf16[64,384]{1,0:T(8,128)(2,1)S(1)}, u32[]{:S(2)}, u32[]{:S(2)}) collective-permute-start(bf16[64,384]{1,0:T(8,128)(2,1)S(1)} %fusion.5), channel_id=1, source_target_pairs={{0,4},{4,0},{8,12},{12,8},{16,20},{20,16},{24,28},{28,24},{1,5},{5... | collective-permute-start | bytes 147464 | tf_op jit(solution)/shard_map/ppermute | solution.py:188
  33.9 1.5 %collective-permute-start.14 = (bf16[4,192,128]{2,1,0:T(8,128)(2,1)S(1)}, bf16[4,192,128]{2,1,0:T(8,128)(2,1)S(1)}, u32[]{:S(2)}, u32[]{:S(2)}) collective-permute-start(bf16[4,192,128]{2,1,0:T(8,128)(2,1)S(1)} %get-tuple-element.45), channel_id=1, source_target_pairs={{0,1},{1,0},{2,3},{3,2},{4,5},{5,4},{6,7},{7,6},{8,9},{9,8},{10,11... | collective-permute-start | bytes 589832 | tf_op jit(solution)/shard_map/ppermute | solution.py:188
  35.4 4.9 %collective-permute-start.15 = (bf16[2,192,128]{2,1,0:T(8,128)(2,1)S(1)}, bf16[2,192,128]{2,1,0:T(8,128)(2,1)S(1)}, u32[]{:S(2)}, u32[]{:S(2)}) collective-permute-start(bf16[2,192,128]{2,1,0:T(8,128)(2,1)S(1)} %fusion.2), channel_id=1, source_target_pairs={{0,2},{1,3},{2,0},{3,1},{4,6},{5,7},{6,4},{7,5},{8,10},{9,11},{10,... | collective-permute-start | bytes 294920 | tf_op jit(solution)/shard_map/ppermute | solution.py:188
  40.4 5.1 %collective-permute-start.16 = (bf16[1,192,128]{2,1,0:T(8,128)(2,1)S(1)}, bf16[1,192,128]{2,1,0:T(8,128)(2,1)S(1)}, u32[]{:S(2)}, u32[]{:S(2)}) collective-permute-start(bf16[1,192,128]{2,1,0:T(8,128)(2,1)S(1)} %fusion.6), channel_id=1, source_target_pairs={{0,16},{4,20},{8,24},{12,28},{16,0},{20,4},{24,8},{28,12},{1,17},{... | collective-permute-start | bytes 147464 | tf_op jit(solution)/shard_map/ppermute | solution.py:188

commit v7 on v6

--- a/solution.py
+++ b/solution.py
@@ -157,22 +157,27 @@
         dst[n % 2] = rows[:, n * slot : (n + 1) * slot].astype(dst.dtype)
 
 
-def down_kernel(R, rblk, l0, l1, l2, l3, ups_a, ups_b, h0, h1, h2, h3, land, send, keep):
+def down_kernel(rblk, l0, l1, l2, l3, h0, h1, h2, h3, send, keep):
     acc = None
     for low, hid in zip((l0, l1, l2, l3), (h0, h1, h2, h3)):
         term = dot32(low[0], hid[...])
         acc = term if acc is None else acc + term
+    for e in range(h0.shape[1] // rblk):
+        dst = send if e % 2 else keep
+        dst[e // 2] = acc[:, e * rblk : (e + 1) * rblk].astype(dst.dtype)
+
+
+def place_kernel(rblk, ups_a, ups_b, land, send, keep):
     rows = (ups_a[...] + ups_b[...].astype(jnp.float32)).astype(jnp.bfloat16)
-    me, me_d, width = lax.axis_index("ctx"), lax.axis_index("dp"), h0.shape[1]
+    me, me_d, blocks = lax.axis_index("ctx"), lax.axis_index("dp"), 2 * keep.shape[0]
     here = jnp.right_shift(me_d, 2) * lax.axis_size("ctx") + me
     where_to = jnp.bitwise_xor(land[pl.ds(me * 4 + jnp.bitwise_and(me_d, 3), 1), :], here * rblk)
-    place = lax.broadcasted_iota(jnp.int32, (width, rows.shape[1]), 0) == where_to
+    place = lax.broadcasted_iota(jnp.int32, (blocks * rblk, rows.shape[1]), 0) == where_to
     place = jnp.where(place, 1.0, 0.0).astype(jnp.bfloat16)
     ups = dot32(rows, place, NT)
-    for e in range(width // rblk):
+    for e in range(blocks):
         dst = send if e % 2 else keep
-        dst[e // 2, : 2 * R, :] = acc[:, e * rblk : (e + 1) * rblk].astype(dst.dtype)
-        dst[e // 2, 2 * R :, :] = ups[:, e * rblk : (e + 1) * rblk].astype(dst.dtype)
+        dst[e // 2] = ups[:, e * rblk : (e + 1) * rblk].astype(dst.dtype)
 
 
 def final_kernel(R, rows_each, kept, got, down, up):
@@ -309,22 +314,34 @@
             lows.append(swap(low, n, "dp"))
         got = swap(ups[1].astype(bf), 1, "dp")
         send, keep = pl.pallas_call(
-            functools.partial(down_kernel, R, rblk),
-            out_shape=(pltpu.VMEM((E // 2, 3 * R, rblk), bf), pltpu.VMEM((E // 2, 3 * R, rblk), f32)),
-            in_specs=[vmem] * 11,
+            functools.partial(down_kernel, rblk),
+            out_shape=(pltpu.VMEM((E // 2, 2 * R, rblk), bf), pltpu.VMEM((E // 2, 2 * R, rblk), f32)),
+            in_specs=[vmem] * 8,
             out_specs=(vmem, vmem),
             compiler_params=params,
             name="down",
-        )(*[near(x) for x in (*lows, ups[0], got, *hids, land)])
+        )(*[near(x) for x in (*lows, *hids)])
+        up_send, up_keep = pl.pallas_call(
+            functools.partial(place_kernel, rblk),
+            out_shape=(pltpu.VMEM((E // 2, R, rblk), bf), pltpu.VMEM((E // 2, R, rblk), f32)),
+            in_specs=[vmem] * 3,
+            out_specs=(vmem, vmem),
+            compiler_params=params,
+            name="place",
+        )(near(ups[0]), near(got), near(land))
+
+        def halves(x):
+            both = x.reshape((-1, 2) + x.shape[1:])
+            return both[:, 0], both[:, 1].astype(bf)
+
         rounds = [("ctx", 1 << i) for i in range(C.bit_length() - 1)]
         rounds += [("dp", 4 << i) for i in range(Dp.bit_length() - 3)]
-        for n, (axis, bit) in enumerate(rounds):
-            if n:
-                both = keep.reshape((-1, 2) + keep.shape[1:])
-                keep, send = both[:, 0], both[:, 1].astype(bf)
-            got = swap(send, bit, axis)
-            if n < len(rounds) - 1:
-                keep = keep + got.astype(f32)
+        for axis, bit in rounds[:-1]:
+            keep, send = halves(keep + swap(send, bit, axis).astype(f32))
+            up_keep, up_send = halves(up_keep + swap(up_send, bit, axis).astype(f32))
+        axis, bit = rounds[-1]
+        keep = jnp.concatenate([keep, up_keep], axis=1)
+        got = swap(jnp.concatenate([send, up_send], axis=1), bit, axis)
         down, up = pl.pallas_call(
             functools.partial(final_kernel, R, rows_each),
             out_shape=(jax.ShapeDtypeStruct((rblk, 2 * R), f32), jax.ShapeDtypeStruct((R, rows_each), f32)),

time: 46.4 us -> 59.9 us (1.29)
  waiting for transfers between devices: 13.7 us -> 27.3 us
    ppermute x17 -> x19, waiting for transfers between devices: 13.7 us -> 27.3 us  [swap(): return lax.ppermute(x, axis, [(i, i ^ s) for i in range(mesh.shape[axis])])]
    ppermute x17 -> x19, starting transfers between devices: 22.2 us -> 21.8 us  [swap(): return lax.ppermute(x, axis, [(i, i ^ s) for i in range(mesh.shape[axis])])]
  transfers between devices with their start and end apart: 17 -> 19, of which waited for: 8 -> 9; matrix products, arithmetic and copies ran while one was open for 0% -> 0% of each run, Pallas kernels for 13% -> 11%
where the time goes in v7:
time: 59.9 us; the launch traced here: 59.6 us
  waiting for transfers between devices  27.3 us (46%)
  starting transfers between devices  21.8 us (36%)
  Pallas kernels  8.82 us (15%)
  between operations  1.5 us (3%)
    ppermute x19, waiting for transfers between devices, swap(): return lax.ppermute(x, axis, [(i, i ^ s) for i in range(mesh.shape[axis])])  27.3 us
    ppermute x19, starting transfers between devices, swap(): return lax.ppermute(x, axis, [(i, i ^ s) for i in range(mesh.shape[axis])])  21.8 us
    pallas_call x3, Pallas kernels, slices(): pl.pallas_call(functools.partial(slice_kernel, plan, len(ins)), out_shape...  4.41 us
    pallas_call x1, Pallas kernels, body(): pl.pallas_call(functools.partial(attend_kernel, C, tok, hq, kh, DH, H, R)...  2.15 us
  transfers between devices with their start and end apart: 19, of which 9 were waited for; matrix products, arithmetic and copies ran while one was open for 0% of the time, Pallas kernels for 11%

profile of v7, /device:TPU:0, one launch (start us, length us, event | category | flops | bytes accessed | tf_op | source)
XLA Modules:
  0.0 59.6 jit_solution(6377181432287794391)
XLA Ops:
  0.6 1.3 %shard_map.104 = (bf16[128,768]{1,0:T(8,128)(2,1)S(1)}, bf16[128,768]{1,0:T(8,128)(2,1)S(1)}, bf16[128,640]{1,0:T(8,128)(2,1)S(1)}, bf16[128,640]{1,0:T(8,128)(2,1)S(1)}) custom-call(bf16[128,2048]{1,0:T(8,128)(2,1)} %bitcast.59, bf16[128,512]{1,0:T(8,128)(2,1)} %bitcast.63, bf16[128,128]{1,0:T(8,128)(2,1)} %bitcast.64), custom_call_target="tpu_custom_call" | custom-call | tf_op jit(solution)/shard_map/pallas_call | solution.py:57
  2.5 2.6 %collective-permute-start.1 = (bf16[128,640]{1,0:T(8,128)(2,1)S(1)}, bf16[128,640]{1,0:T(8,128)(2,1)S(1)}, u32[]{:S(2)}, u32[]{:S(2)}) collective-permute-start(bf16[128,640]{1,0:T(8,128)(2,1)S(1)} %get-tuple-element.29), channel_id=1, source_target_pairs={{0,2},{1,3},{2,0},{3,1},{4,6},{5,7},{6,4},{7,5},{8,10},{9,11},{10,... | collective-permute-start | bytes 491528 | tf_op jit(solution)/shard_map/ppermute | solution.py:193
  5.1 1.8 %collective-permute-start.13 = (bf16[2,128,128]{2,1,0:T(8,128)(2,1)S(1)}, bf16[2,128,128]{2,1,0:T(8,128)(2,1)S(1)}, u32[]{:S(2)}, u32[]{:S(2)}) collective-permute-start(bf16[2,128,128]{2,1,0:T(8,128)(2,1)S(1)} %pad_maximum_fusion.2), channel_id=1, source_target_pairs={{0,2},{1,3},{2,0},{3,1},{4,6},{5,7},{6,4},{7,5},{8,10},{9,11},{10,... | collective-permute-start | bytes 196616 | tf_op jit(solution)/shard_map/ppermute | solution.py:193
  7.6 1.6 %shard_map.105 = (bf16[4,512,512]{2,1,0:T(8,128)(2,1)S(1)}, bf16[64,512]{1,0:T(8,128)(2,1)S(1)}, bf16[64,128]{1,0:T(8,128)(2,1)S(1)}, s32[16,1536]{1,0:T(8,128)S(1)}, s32[16,384]{1,0:T(8,128)S(1)}) custom-call(bf16[4,512,512]{2,1,0:T(8,128)(2,1)} %bitcast.55, bf16[64,2560]{1,0:T(8,128)(2,1)} %bitcast.62, s32[16,1536]{1,0:T(8,128)} %constant.4.clone.refs_2_, ...), custom_call_target="tpu_custom_call" | custom-call | tf_op jit(solution)/shard_map/pallas_call | solution.py:57
  9.2 0.9 %collective-permute-done.1.refs_2_ = bf16[128,640]{1,0:T(8,128)(2,1)S(1)} collective-permute-done((bf16[128,640]{1,0:T(8,128)(2,1)S(1)}, bf16[128,640]{1,0:T(8,128)(2,1)S(1)}, u32[]{:S(2)}, u32[]{:S(2)}) %collective-permute-start.1) | collective-permute-done | bytes 163872 | tf_op jit(solution)/shard_map/ppermute | solution.py:193
  10.1 3.1 %collective-permute-done.2.refs_3_ = bf16[128,640]{1,0:T(8,128)(2,1)S(1)} collective-permute-done((bf16[128,640]{1,0:T(8,128)(2,1)S(1)}, bf16[128,640]{1,0:T(8,128)(2,1)S(1)}, u32[]{:S(2)}, u32[]{:S(2)}) %collective-permute-start.2) | collective-permute-done | bytes 163872 | tf_op jit(solution)/shard_map/ppermute | solution.py:193
  13.1 2.2 %attend.1 = (f32[2,128,128]{2,1,0:T(8,128)S(1)}, f32[2,128,128]{2,1,0:T(8,128)S(1)}, bf16[512,512]{1,0:T(8,128)(2,1)S(1)}, bf16[128,512]{1,0:T(8,128)(2,1)S(1)}) custom-call(s32[1]{0:T(128)S(6)} %copy.35.lengths, bf16[128,768]{1,0:T(8,128)(2,1)S(1)} %get-tuple-element.27.refs_0_, bf16[128,768]{1,0:T(8,128)(2,1)S(1)} %collective-permute-done.refs_1_, ...), custom_call_target="tpu_custom_call" | custom-call | tf_op jit(solution)/shard_map/attend/pallas_call | solution.py:276
  15.7 1.5 %shard_map.106 = (bf16[128,1024]{1,0:T(8,128)(2,1)S(1)}, bf16[128,1024]{1,0:T(8,128)(2,1)S(1)}, bf16[128,1024]{1,0:T(8,128)(2,1)S(1)}, bf16[128,1024]{1,0:T(8,128)(2,1)S(1)}) custom-call(bf16[128,4096]{1,0:T(8,128)(2,1)} %bitcast.56), custom_call_target="tpu_custom_call" | custom-call | tf_op jit(solution)/shard_map/pallas_call | solution.py:57
  17.1 3.1 %collective-permute-start.10 = (bf16[128,1024]{1,0:T(8,128)(2,1)S(1)}, bf16[128,1024]{1,0:T(8,128)(2,1)S(1)}, u32[]{:S(2)}, u32[]{:S(2)}) collective-permute-start(bf16[128,1024]{1,0:T(8,128)(2,1)S(1)} %get-tuple-element.39), channel_id=1, source_target_pairs={{0,12},{4,8},{8,4},{12,0},{16,28},{20,24},{24,20},{28,16},{1,13},{... | collective-permute-start | bytes 786440 | tf_op jit(solution)/shard_map/ppermute | solution.py:193
  21.6 1.9 %collective-permute-start.14 = (bf16[2,64,384]{2,1,0:T(8,128)(2,1)S(1)}, bf16[2,64,384]{2,1,0:T(8,128)(2,1)S(1)}, u32[]{:S(2)}, u32[]{:S(2)}) collective-permute-start(bf16[2,64,384]{2,1,0:T(8,128)(2,1)S(1)} %get-tuple-element.46), channel_id=1, source_target_pairs={{0,8},{4,12},{8,0},{12,4},{16,24},{20,28},{24,16},{28,20},{1,9},{5... | collective-permute-start | bytes 294920 | tf_op jit(solution)/shard_map/ppermute | solution.py:193
  23.6 1.5 %collective-permute-start.4 = (bf16[1,128,128]{2,1,0:T(8,128)(2,1)S(1)}, bf16[1,128,128]{2,1,0:T(8,128)(2,1)S(1)}, u32[]{:S(2)}, u32[]{:S(2)}) collective-permute-start(bf16[1,128,128]{2,1,0:T(8,128)(2,1)S(1)} %fusion.8), channel_id=1, source_target_pairs={{0,2},{1,3},{2,0},{3,1},{4,6},{5,7},{6,4},{7,5},{8,10},{9,11},{10,... | collective-permute-start | bytes 98312 | tf_op jit(solution)/shard_map/ppermute | solution.py:193
  25.2 9.5 %collective-permute-done.14 = bf16[2,64,384]{2,1,0:T(8,128)(2,1)S(1)} collective-permute-done((bf16[2,64,384]{2,1,0:T(8,128)(2,1)S(1)}, bf16[2,64,384]{2,1,0:T(8,128)(2,1)S(1)}, u32[]{:S(2)}, u32[]{:S(2)}) %collective-permute-start.14) | collective-permute-done | bytes 98336 | tf_op jit(solution)/shard_map/ppermute | solution.py:193
  35.2 3.7 %collective-permute-done.15.ups_b = bf16[64,384]{1,0:T(8,128)(2,1)S(1)} collective-permute-done((bf16[64,384]{1,0:T(8,128)(2,1)S(1)}, bf16[64,384]{1,0:T(8,128)(2,1)S(1)}, u32[]{:S(2)}, u32[]{:S(2)}) %collective-permute-start.15) | collective-permute-done | bytes 49184 | tf_op jit(solution)/shard_map/ppermute | solution.py:193
  39.9 0.7 %collective-permute-done.16 = bf16[4,64,128]{2,1,0:T(8,128)(2,1)S(1)} collective-permute-done((bf16[4,64,128]{2,1,0:T(8,128)(2,1)S(1)}, bf16[4,64,128]{2,1,0:T(8,128)(2,1)S(1)}, u32[]{:S(2)}, u32[]{:S(2)}) %collective-permute-start.16) | collective-permute-done | bytes 65568 | tf_op jit(solution)/shard_map/ppermute | solution.py:193
  40.6 1.6 %collective-permute-start.6 = (bf16[1,128,128]{2,1,0:T(8,128)(2,1)S(1)}, bf16[1,128,128]{2,1,0:T(8,128)(2,1)S(1)}, u32[]{:S(2)}, u32[]{:S(2)}) collective-permute-start(bf16[1,128,128]{2,1,0:T(8,128)(2,1)S(1)} %fusion.6.l0), channel_id=1, source_target_pairs={{0,8},{4,12},{8,0},{12,4},{16,24},{20,28},{24,16},{28,20},{1,9},{5... | collective-permute-start | bytes 98312 | tf_op jit(solution)/shard_map/ppermute | solution.py:193
  42.2 0.8 %collective-permute-start.7 = (bf16[1,128,128]{2,1,0:T(8,128)(2,1)S(1)}, bf16[1,128,128]{2,1,0:T(8,128)(2,1)S(1)}, u32[]{:S(2)}, u32[]{:S(2)}) collective-permute-start(bf16[1,128,128]{2,1,0:T(8,128)(2,1)S(1)} %fusion.6.l0), channel_id=1, source_target_pairs={{0,12},{4,8},{8,4},{12,0},{16,28},{20,24},{24,20},{28,16},{1,13},{... | collective-permute-start | bytes 98312 | tf_op jit(solution)/shard_map/ppermute | solution.py:193
  43.1 1.5 %collective-permute-start.17 = (bf16[2,64,128]{2,1,0:T(8,128)(2,1)S(1)}, bf16[2,64,128]{2,1,0:T(8,128)(2,1)S(1)}, u32[]{:S(2)}, u32[]{:S(2)}) collective-permute-start(bf16[2,64,128]{2,1,0:T(8,128)(2,1)S(1)} %fusion.10), channel_id=1, source_target_pairs={{0,2},{1,3},{2,0},{3,1},{4,6},{5,7},{6,4},{7,5},{8,10},{9,11},{10,... | collective-permute-start | bytes 98312 | tf_op jit(solution)/shard_map/ppermute | solution.py:193
  44.6 2.5 %collective-permute-done.7.l3 = bf16[1,128,128]{2,1,0:T(8,128)(2,1)S(1)} collective-permute-done((bf16[1,128,128]{2,1,0:T(8,128)(2,1)S(1)}, bf16[1,128,128]{2,1,0:T(8,128)(2,1)S(1)}, u32[]{:S(2)}, u32[]{:S(2)}) %collective-permute-start.7) | collective-permute-done | bytes 32800 | tf_op jit(solution)/shard_map/ppermute | solution.py:193
  47.6 1.3 %collective-permute-done.11 = bf16[4,128,128]{2,1,0:T(8,128)(2,1)S(1)} collective-permute-done((bf16[4,128,128]{2,1,0:T(8,128)(2,1)S(1)}, bf16[4,128,128]{2,1,0:T(8,128)(2,1)S(1)}, u32[]{:S(2)}, u32[]{:S(2)}) %collective-permute-start.11) | collective-permute-done | bytes 131104 | tf_op jit(solution)/shard_map/ppermute | solution.py:193
  49.0 1.5 %collective-permute-start.12 = (bf16[2,128,128]{2,1,0:T(8,128)(2,1)S(1)}, bf16[2,128,128]{2,1,0:T(8,128)(2,1)S(1)}, u32[]{:S(2)}, u32[]{:S(2)}) collective-permute-start(bf16[2,128,128]{2,1,0:T(8,128)(2,1)S(1)} %fusion.2), channel_id=1, source_target_pairs={{0,2},{1,3},{2,0},{3,1},{4,6},{5,7},{6,4},{7,5},{8,10},{9,11},{10,... | collective-permute-start | bytes 196616 | tf_op jit(solution)/shard_map/ppermute | solution.py:193
  50.5 2.8 %collective-permute-done.12 = bf16[2,128,128]{2,1,0:T(8,128)(2,1)S(1)} collective-permute-done((bf16[2,128,128]{2,1,0:T(8,128)(2,1)S(1)}, bf16[2,128,128]{2,1,0:T(8,128)(2,1)S(1)}, u32[]{:S(2)}, u32[]{:S(2)}) %collective-permute-start.12) | collective-permute-done | bytes 65568 | tf_op jit(solution)/shard_map/ppermute | solution.py:193
  53.4 2.6 %collective-permute-start.18 = (bf16[1,192,128]{2,1,0:T(8,128)(2,1)S(1)}, bf16[1,192,128]{2,1,0:T(8,128)(2,1)S(1)}, u32[]{:S(2)}, u32[]{:S(2)}) collective-permute-start(bf16[1,192,128]{2,1,0:T(8,128)(2,1)S(1)} %pad_maximum_fusion.3), channel_id=1, source_target_pairs={{0,16},{4,20},{8,24},{12,28},{16,0},{20,4},{24,8},{28,12},{1,17},{... | collective-permute-start | bytes 147464 | tf_op jit(solution)/shard_map/ppermute | solution.py:193
  56.0 2.8 %collective-permute-done.18.got = bf16[1,192,128]{2,1,0:T(8,128)(2,1)S(1)} collective-permute-done((bf16[1,192,128]{2,1,0:T(8,128)(2,1)S(1)}, bf16[1,192,128]{2,1,0:T(8,128)(2,1)S(1)}, u32[]{:S(2)}, u32[]{:S(2)}) %collective-permute-start.18) | collective-permute-done | bytes 49184 | tf_op jit(solution)/shard_map/ppermute | solution.py:193
  58.8 0.7 %final.1 = (f32[128,128]{1,0:T(8,128)}, f32[64,80]{1,0:T(8,128)}) custom-call(f32[1,192,128]{2,1,0:T(8,128)S(1)} %pad_maximum_fusion.1.kept, bf16[1,192,128]{2,1,0:T(8,128)(2,1)S(1)} %collective-permute-done.18.got), custom_call_target="tpu_custom_call" | custom-call | tf_op jit(solution)/shard_map/final/pallas_call | solution.py:345
  (44 shorter events, 4.4 us)
Async XLA Ops:
  1.9 3.2 %collective-permute-start = (bf16[128,768]{1,0:T(8,128)(2,1)S(1)}, bf16[128,768]{1,0:T(8,128)(2,1)S(1)}, u32[]{:S(2)}, u32[]{:S(2)}) collective-permute-start(bf16[128,768]{1,0:T(8,128)(2,1)S(1)} %get-tuple-element.28), channel_id=1, source_target_pairs={{0,1},{1,0},{2,3},{3,2},{4,5},{5,4},{6,7},{7,6},{8,9},{9,8},{10,11... | collective-permute-start | bytes 589832 | tf_op jit(solution)/shard_map/ppermute | solution.py:193
  2.5 7.6 %collective-permute-start.1 = (bf16[128,640]{1,0:T(8,128)(2,1)S(1)}, bf16[128,640]{1,0:T(8,128)(2,1)S(1)}, u32[]{:S(2)}, u32[]{:S(2)}) collective-permute-start(bf16[128,640]{1,0:T(8,128)(2,1)S(1)} %get-tuple-element.29), channel_id=1, source_target_pairs={{0,2},{1,3},{2,0},{3,1},{4,6},{5,7},{6,4},{7,5},{8,10},{9,11},{10,... | collective-permute-start | bytes 491528 | tf_op jit(solution)/shard_map/ppermute | solution.py:193
  5.0 8.1 %collective-permute-start.2 = (bf16[128,640]{1,0:T(8,128)(2,1)S(1)}, bf16[128,640]{1,0:T(8,128)(2,1)S(1)}, u32[]{:S(2)}, u32[]{:S(2)}) collective-permute-start(bf16[128,640]{1,0:T(8,128)(2,1)S(1)} %get-tuple-element.30), channel_id=1, source_target_pairs={{0,3},{1,2},{2,1},{3,0},{4,7},{5,6},{6,5},{7,4},{8,11},{9,10},{10,... | collective-permute-start | bytes 491528 | tf_op jit(solution)/shard_map/ppermute | solution.py:193
  5.1 15.8 %collective-permute-start.13 = (bf16[2,128,128]{2,1,0:T(8,128)(2,1)S(1)}, bf16[2,128,128]{2,1,0:T(8,128)(2,1)S(1)}, u32[]{:S(2)}, u32[]{:S(2)}) collective-permute-start(bf16[2,128,128]{2,1,0:T(8,128)(2,1)S(1)} %pad_maximum_fusion.2), channel_id=1, source_target_pairs={{0,2},{1,3},{2,0},{3,1},{4,6},{5,7},{6,4},{7,5},{8,10},{9,11},{10,... | collective-permute-start | bytes 196616 | tf_op jit(solution)/shard_map/ppermute | solution.py:193
  15.3 8.3 %collective-permute-start.3 = (f32[2,128,128]{2,1,0:T(8,128)S(1)}, f32[2,128,128]{2,1,0:T(8,128)S(1)}, u32[]{:S(2)}, u32[]{:S(2)}) collective-permute-start(f32[2,128,128]{2,1,0:T(8,128)S(1)} %get-tuple-element.35), channel_id=1, source_target_pairs={{0,1},{1,0},{2,3},{3,2},{4,5},{5,4},{6,7},{7,6},{8,9},{9,8},{10,11... | collective-permute-start | bytes 393224 | tf_op jit(solution)/shard_map/ppermute | solution.py:193
  17.1 25.1 %collective-permute-start.10 = (bf16[128,1024]{1,0:T(8,128)(2,1)S(1)}, bf16[128,1024]{1,0:T(8,128)(2,1)S(1)}, u32[]{:S(2)}, u32[]{:S(2)}) collective-permute-start(bf16[128,1024]{1,0:T(8,128)(2,1)S(1)} %get-tuple-element.39), channel_id=1, source_target_pairs={{0,12},{4,8},{8,4},{12,0},{16,28},{20,24},{24,20},{28,16},{1,13},{... | collective-permute-start | bytes 786440 | tf_op jit(solution)/shard_map/ppermute | solution.py:193
  20.3 22.8 %collective-permute-start.8 = (bf16[128,1024]{1,0:T(8,128)(2,1)S(1)}, bf16[128,1024]{1,0:T(8,128)(2,1)S(1)}, u32[]{:S(2)}, u32[]{:S(2)}) collective-permute-start(bf16[128,1024]{1,0:T(8,128)(2,1)S(1)} %get-tuple-element.37), channel_id=1, source_target_pairs={{0,4},{4,0},{8,12},{12,8},{16,20},{20,16},{24,28},{28,24},{1,5},{5... | collective-permute-start | bytes 786440 | tf_op jit(solution)/shard_map/ppermute | solution.py:193
  20.8 23.8 %collective-permute-start.9 = (bf16[128,1024]{1,0:T(8,128)(2,1)S(1)}, bf16[128,1024]{1,0:T(8,128)(2,1)S(1)}, u32[]{:S(2)}, u32[]{:S(2)}) collective-permute-start(bf16[128,1024]{1,0:T(8,128)(2,1)S(1)} %get-tuple-element.38), channel_id=1, source_target_pairs={{0,8},{4,12},{8,0},{12,4},{16,24},{20,28},{24,16},{28,20},{1,9},{5... | collective-permute-start | bytes 786440 | tf_op jit(solution)/shard_map/ppermute | solution.py:193
  21.6 13.0 %collective-permute-start.14 = (bf16[2,64,384]{2,1,0:T(8,128)(2,1)S(1)}, bf16[2,64,384]{2,1,0:T(8,128)(2,1)S(1)}, u32[]{:S(2)}, u32[]{:S(2)}) collective-permute-start(bf16[2,64,384]{2,1,0:T(8,128)(2,1)S(1)} %get-tuple-element.46), channel_id=1, source_target_pairs={{0,8},{4,12},{8,0},{12,4},{16,24},{20,28},{24,16},{28,20},{1,9},{5... | collective-permute-start | bytes 294920 | tf_op jit(solution)/shard_map/ppermute | solution.py:193
  23.6 15.7 %collective-permute-start.4 = (bf16[1,128,128]{2,1,0:T(8,128)(2,1)S(1)}, bf16[1,128,128]{2,1,0:T(8,128)(2,1)S(1)}, u32[]{:S(2)}, u32[]{:S(2)}) collective-permute-start(bf16[1,128,128]{2,1,0:T(8,128)(2,1)S(1)} %fusion.8), channel_id=1, source_target_pairs={{0,2},{1,3},{2,0},{3,1},{4,6},{5,7},{6,4},{7,5},{8,10},{9,11},{10,... | collective-permute-start | bytes 98312 | tf_op jit(solution)/shard_map/ppermute | solution.py:193
  34.7 4.2 %collective-permute-start.15 = (bf16[64,384]{1,0:T(8,128)(2,1)S(1)}, bf16[64,384]{1,0:T(8,128)(2,1)S(1)}, u32[]{:S(2)}, u32[]{:S(2)}) collective-permute-start(bf16[64,384]{1,0:T(8,128)(2,1)S(1)} %fusion.7), channel_id=1, source_target_pairs={{0,4},{4,0},{8,12},{12,8},{16,20},{20,16},{24,28},{28,24},{1,5},{5... | collective-permute-start | bytes 147464 | tf_op jit(solution)/shard_map/ppermute | solution.py:193
  39.3 1.3 %collective-permute-start.16 = (bf16[4,64,128]{2,1,0:T(8,128)(2,1)S(1)}, bf16[4,64,128]{2,1,0:T(8,128)(2,1)S(1)}, u32[]{:S(2)}, u32[]{:S(2)}) collective-permute-start(bf16[4,64,128]{2,1,0:T(8,128)(2,1)S(1)} %get-tuple-element.49), channel_id=1, source_target_pairs={{0,1},{1,0},{2,3},{3,2},{4,5},{5,4},{6,7},{7,6},{8,9},{9,8},{10,11... | collective-permute-start | bytes 196616 | tf_op jit(solution)/shard_map/ppermute | solution.py:193
  39.4 5.2 %collective-permute-start.5 = (bf16[1,128,128]{2,1,0:T(8,128)(2,1)S(1)}, bf16[1,128,128]{2,1,0:T(8,128)(2,1)S(1)}, u32[]{:S(2)}, u32[]{:S(2)}) collective-permute-start(bf16[1,128,128]{2,1,0:T(8,128)(2,1)S(1)} %fusion.6.l0), channel_id=1, source_target_pairs={{0,4},{4,0},{8,12},{12,8},{16,20},{20,16},{24,28},{28,24},{1,5},{5... | collective-permute-start | bytes 98312 | tf_op jit(solution)/shard_map/ppermute | solution.py:193
  40.6 4.0 %collective-permute-start.6 = (bf16[1,128,128]{2,1,0:T(8,128)(2,1)S(1)}, bf16[1,128,128]{2,1,0:T(8,128)(2,1)S(1)}, u32[]{:S(2)}, u32[]{:S(2)}) collective-permute-start(bf16[1,128,128]{2,1,0:T(8,128)(2,1)S(1)} %fusion.6.l0), channel_id=1, source_target_pairs={{0,8},{4,12},{8,0},{12,4},{16,24},{20,28},{24,16},{28,20},{1,9},{5... | collective-permute-start | bytes 98312 | tf_op jit(solution)/shard_map/ppermute | solution.py:193
  42.2 4.9 %collective-permute-start.7 = (bf16[1,128,128]{2,1,0:T(8,128)(2,1)S(1)}, bf16[1,128,128]{2,1,0:T(8,128)(2,1)S(1)}, u32[]{:S(2)}, u32[]{:S(2)}) collective-permute-start(bf16[1,128,128]{2,1,0:T(8,128)(2,1)S(1)} %fusion.6.l0), channel_id=1, source_target_pairs={{0,12},{4,8},{8,4},{12,0},{16,28},{20,24},{24,20},{28,16},{1,13},{... | collective-permute-start | bytes 98312 | tf_op jit(solution)/shard_map/ppermute | solution.py:193
  43.1 4.5 %collective-permute-start.17 = (bf16[2,64,128]{2,1,0:T(8,128)(2,1)S(1)}, bf16[2,64,128]{2,1,0:T(8,128)(2,1)S(1)}, u32[]{:S(2)}, u32[]{:S(2)}) collective-permute-start(bf16[2,64,128]{2,1,0:T(8,128)(2,1)S(1)} %fusion.10), channel_id=1, source_target_pairs={{0,2},{1,3},{2,0},{3,1},{4,6},{5,7},{6,4},{7,5},{8,10},{9,11},{10,... | collective-permute-start | bytes 98312 | tf_op jit(solution)/shard_map/ppermute | solution.py:193
  47.5 1.4 %collective-permute-start.11 = (bf16[4,128,128]{2,1,0:T(8,128)(2,1)S(1)}, bf16[4,128,128]{2,1,0:T(8,128)(2,1)S(1)}, u32[]{:S(2)}, u32[]{:S(2)}) collective-permute-start(bf16[4,128,128]{2,1,0:T(8,128)(2,1)S(1)} %get-tuple-element.41), channel_id=1, source_target_pairs={{0,1},{1,0},{2,3},{3,2},{4,5},{5,4},{6,7},{7,6},{8,9},{9,8},{10,11... | collective-permute-start | bytes 393224 | tf_op jit(solution)/shard_map/ppermute | solution.py:193
  49.0 4.3 %collective-permute-start.12 = (bf16[2,128,128]{2,1,0:T(8,128)(2,1)S(1)}, bf16[2,128,128]{2,1,0:T(8,128)(2,1)S(1)}, u32[]{:S(2)}, u32[]{:S(2)}) collective-permute-start(bf16[2,128,128]{2,1,0:T(8,128)(2,1)S(1)} %fusion.2), channel_id=1, source_target_pairs={{0,2},{1,3},{2,0},{3,1},{4,6},{5,7},{6,4},{7,5},{8,10},{9,11},{10,... | collective-permute-start | bytes 196616 | tf_op jit(solution)/shard_map/ppermute | solution.py:193
  53.4 5.5 %collective-permute-start.18 = (bf16[1,192,128]{2,1,0:T(8,128)(2,1)S(1)}, bf16[1,192,128]{2,1,0:T(8,128)(2,1)S(1)}, u32[]{:S(2)}, u32[]{:S(2)}) collective-permute-start(bf16[1,192,128]{2,1,0:T(8,128)(2,1)S(1)} %pad_maximum_fusion.3), channel_id=1, source_target_pairs={{0,16},{4,20},{8,24},{12,28},{16,0},{20,4},{24,8},{28,12},{1,17},{... | collective-permute-start | bytes 147464 | tf_op jit(solution)/shard_map/ppermute | solution.py:193

commit v8 on v7

--- a/solution.py
+++ b/solution.py
@@ -138,8 +138,8 @@
         (send_out if s % 2 else keep_out)[s // 2] = low_buf[:, pl.ds(pos, tok)]
 
 
-def up_kernel(C, tok, R, *refs):
-    adapters, dq, dk, pack, keep, send, a_buf = refs
+def up_kernel(C, tok, R, rblk, *refs):
+    adapters, dq, dk, pack, land, keep, send, place, a_buf = refs
     me, me_d = lax.axis_index("ctx"), lax.axis_index("dp")
     for s in range(C):
         a_buf[pl.ds(pl.multiple_of(jnp.bitwise_xor(me, s) * tok, tok), tok), :] = adapters[s][...]
@@ -155,6 +155,9 @@
     for n in range(4):
         dst = send if n // 2 else keep
         dst[n % 2] = rows[:, n * slot : (n + 1) * slot].astype(dst.dtype)
+    here = jnp.right_shift(me_d, 2) * lax.axis_size("ctx") + me
+    lands = jnp.bitwise_xor(land[pl.ds(me * 4 + jnp.bitwise_and(me_d, 3), 1), :], here * rblk)
+    place[...] = jnp.where(lax.broadcasted_iota(jnp.int32, place.shape, 0) == lands, 1.0, 0.0).astype(place.dtype)
 
 
 def down_kernel(rblk, l0, l1, l2, l3, h0, h1, h2, h3, send, keep):
@@ -167,15 +170,10 @@
         dst[e // 2] = acc[:, e * rblk : (e + 1) * rblk].astype(dst.dtype)
 
 
-def place_kernel(rblk, ups_a, ups_b, land, send, keep):
+def place_kernel(rblk, ups_a, ups_b, place, send, keep):
     rows = (ups_a[...] + ups_b[...].astype(jnp.float32)).astype(jnp.bfloat16)
-    me, me_d, blocks = lax.axis_index("ctx"), lax.axis_index("dp"), 2 * keep.shape[0]
-    here = jnp.right_shift(me_d, 2) * lax.axis_size("ctx") + me
-    where_to = jnp.bitwise_xor(land[pl.ds(me * 4 + jnp.bitwise_and(me_d, 3), 1), :], here * rblk)
-    place = lax.broadcasted_iota(jnp.int32, (blocks * rblk, rows.shape[1]), 0) == where_to
-    place = jnp.where(place, 1.0, 0.0).astype(jnp.bfloat16)
-    ups = dot32(rows, place, NT)
-    for e in range(blocks):
+    ups = dot32(rows, place[...], NT)
+    for e in range(2 * keep.shape[0]):
         dst = send if e % 2 else keep
         dst[e // 2] = ups[:, e * rblk : (e + 1) * rblk].astype(dst.dtype)
 
@@ -298,15 +296,15 @@
             both = low.reshape((-1, 2) + low.shape[1:])
             low = both[:, 0] + swap(both[:, 1].astype(bf), bit).astype(f32)
             bit *= 2
-        ups, send = pl.pallas_call(
-            functools.partial(up_kernel, C, tok, R),
-            out_shape=(pltpu.VMEM((2, R, slot), f32), pltpu.VMEM((2, R, slot), bf)),
-            in_specs=[vmem] * 4,
-            out_specs=(vmem, vmem),
+        ups, send, place = pl.pallas_call(
+            functools.partial(up_kernel, C, tok, R, rblk),
+            out_shape=(pltpu.VMEM((2, R, slot), f32), pltpu.VMEM((2, R, slot), bf), pltpu.VMEM((E * rblk, slot), bf)),
+            in_specs=[vmem] * 5,
+            out_specs=(vmem, vmem, vmem),
             scratch_shapes=[pltpu.VMEM((S, 2 * R), bf)],
             compiler_params=params,
             name="upgrad",
-        )(near(adapters), near(dq), near(dk), near(pack))
+        )(near(adapters), near(dq), near(dk), near(pack), near(land))
         ups = ups + swap(send, 2, "dp").astype(f32)
         low = low.astype(bf)
         lows = [low]
@@ -328,7 +326,7 @@
             out_specs=(vmem, vmem),
             compiler_params=params,
             name="place",
-        )(near(ups[0]), near(got), near(land))
+        )(near(ups[0]), near(got), near(place))
 
         def halves(x):
             both = x.reshape((-1, 2) + x.shape[1:])

time: 59.9 us -> 59.8 us (level)
  transfers between devices with their start and end apart: 19 -> 19, of which waited for: 9 -> 9; matrix products, arithmetic and copies ran while one was open for 0% -> 0% of each run, Pallas kernels for 11% -> 12%
where the time goes in v8:
time: 59.8 us; the launch traced here: 59.6 us
  waiting for transfers between devices  27.1 us (45%)
  starting transfers between devices  21.8 us (36%)
  Pallas kernels  8.9 us (15%)
  between operations  1.5 us (3%)
    ppermute x19, waiting for transfers between devices, swap(): return lax.ppermute(x, axis, [(i, i ^ s) for i in range(mesh.shape[axis])])  27.1 us
    ppermute x19, starting transfers between devices, swap(): return lax.ppermute(x, axis, [(i, i ^ s) for i in range(mesh.shape[axis])])  21.8 us
    pallas_call x3, Pallas kernels, slices(): pl.pallas_call(functools.partial(slice_kernel, plan, len(ins)), out_shape...  4.41 us
    pallas_call x1, Pallas kernels, body(): pl.pallas_call(functools.partial(attend_kernel, C, tok, hq, kh, DH, H, R)...  2.15 us
  transfers between devices with their start and end apart: 19, of which 9 were waited for; matrix products, arithmetic and copies ran while one was open for 0% of the time, Pallas kernels for 12%

profile of v8, /device:TPU:0, one launch (start us, length us, event | category | flops | bytes accessed | tf_op | source)
XLA Modules:
  0.0 59.6 jit_solution(1429903427801779936)
XLA Ops:
  0.6 1.3 %shard_map.104 = (bf16[128,768]{1,0:T(8,128)(2,1)S(1)}, bf16[128,768]{1,0:T(8,128)(2,1)S(1)}, bf16[128,640]{1,0:T(8,128)(2,1)S(1)}, bf16[128,640]{1,0:T(8,128)(2,1)S(1)}) custom-call(bf16[128,2048]{1,0:T(8,128)(2,1)} %bitcast.59, bf16[128,512]{1,0:T(8,128)(2,1)} %bitcast.63, bf16[128,128]{1,0:T(8,128)(2,1)} %bitcast.64), custom_call_target="tpu_custom_call" | custom-call | tf_op jit(solution)/shard_map/pallas_call | solution.py:57
  2.5 2.6 %collective-permute-start.1 = (bf16[128,640]{1,0:T(8,128)(2,1)S(1)}, bf16[128,640]{1,0:T(8,128)(2,1)S(1)}, u32[]{:S(2)}, u32[]{:S(2)}) collective-permute-start(bf16[128,640]{1,0:T(8,128)(2,1)S(1)} %get-tuple-element.30), channel_id=1, source_target_pairs={{0,2},{1,3},{2,0},{3,1},{4,6},{5,7},{6,4},{7,5},{8,10},{9,11},{10,... | collective-permute-start | bytes 491528 | tf_op jit(solution)/shard_map/ppermute | solution.py:191
  5.1 1.8 %collective-permute-start.13 = (bf16[2,128,128]{2,1,0:T(8,128)(2,1)S(1)}, bf16[2,128,128]{2,1,0:T(8,128)(2,1)S(1)}, u32[]{:S(2)}, u32[]{:S(2)}) collective-permute-start(bf16[2,128,128]{2,1,0:T(8,128)(2,1)S(1)} %pad_maximum_fusion.2), channel_id=1, source_target_pairs={{0,2},{1,3},{2,0},{3,1},{4,6},{5,7},{6,4},{7,5},{8,10},{9,11},{10,... | collective-permute-start | bytes 196616 | tf_op jit(solution)/shard_map/ppermute | solution.py:191
  7.6 1.6 %shard_map.105 = (bf16[4,512,512]{2,1,0:T(8,128)(2,1)S(1)}, bf16[64,512]{1,0:T(8,128)(2,1)S(1)}, bf16[64,128]{1,0:T(8,128)(2,1)S(1)}, s32[16,1536]{1,0:T(8,128)S(1)}, s32[16,384]{1,0:T(8,128)S(1)}) custom-call(bf16[4,512,512]{2,1,0:T(8,128)(2,1)} %bitcast.55, bf16[64,2560]{1,0:T(8,128)(2,1)} %bitcast.62, s32[16,1536]{1,0:T(8,128)} %constant.4.clone.refs_2_, ...), custom_call_target="tpu_custom_call" | custom-call | tf_op jit(solution)/shard_map/pallas_call | solution.py:57
  9.2 0.9 %collective-permute-done.1.refs_2_ = bf16[128,640]{1,0:T(8,128)(2,1)S(1)} collective-permute-done((bf16[128,640]{1,0:T(8,128)(2,1)S(1)}, bf16[128,640]{1,0:T(8,128)(2,1)S(1)}, u32[]{:S(2)}, u32[]{:S(2)}) %collective-permute-start.1) | collective-permute-done | bytes 163872 | tf_op jit(solution)/shard_map/ppermute | solution.py:191
  10.1 3.1 %collective-permute-done.2.refs_3_ = bf16[128,640]{1,0:T(8,128)(2,1)S(1)} collective-permute-done((bf16[128,640]{1,0:T(8,128)(2,1)S(1)}, bf16[128,640]{1,0:T(8,128)(2,1)S(1)}, u32[]{:S(2)}, u32[]{:S(2)}) %collective-permute-start.2) | collective-permute-done | bytes 163872 | tf_op jit(solution)/shard_map/ppermute | solution.py:191
  13.1 2.2 %attend.1 = (f32[2,128,128]{2,1,0:T(8,128)S(1)}, f32[2,128,128]{2,1,0:T(8,128)S(1)}, bf16[512,512]{1,0:T(8,128)(2,1)S(1)}, bf16[128,512]{1,0:T(8,128)(2,1)S(1)}) custom-call(s32[1]{0:T(128)S(6)} %copy.35.lengths, bf16[128,768]{1,0:T(8,128)(2,1)S(1)} %get-tuple-element.28.refs_0_, bf16[128,768]{1,0:T(8,128)(2,1)S(1)} %collective-permute-done.refs_1_, ...), custom_call_target="tpu_custom_call" | custom-call | tf_op jit(solution)/shard_map/attend/pallas_call | solution.py:274
  15.7 1.5 %shard_map.106 = (bf16[128,1024]{1,0:T(8,128)(2,1)S(1)}, bf16[128,1024]{1,0:T(8,128)(2,1)S(1)}, bf16[128,1024]{1,0:T(8,128)(2,1)S(1)}, bf16[128,1024]{1,0:T(8,128)(2,1)S(1)}) custom-call(bf16[128,4096]{1,0:T(8,128)(2,1)} %bitcast.56), custom_call_target="tpu_custom_call" | custom-call | tf_op jit(solution)/shard_map/pallas_call | solution.py:57
  17.1 3.1 %collective-permute-start.10 = (bf16[128,1024]{1,0:T(8,128)(2,1)S(1)}, bf16[128,1024]{1,0:T(8,128)(2,1)S(1)}, u32[]{:S(2)}, u32[]{:S(2)}) collective-permute-start(bf16[128,1024]{1,0:T(8,128)(2,1)S(1)} %get-tuple-element.40), channel_id=1, source_target_pairs={{0,12},{4,8},{8,4},{12,0},{16,28},{20,24},{24,20},{28,16},{1,13},{... | collective-permute-start | bytes 786440 | tf_op jit(solution)/shard_map/ppermute | solution.py:191
  20.9 0.8 %upgrad.1 = (f32[2,64,384]{2,1,0:T(8,128)S(1)}, bf16[2,64,384]{2,1,0:T(8,128)(2,1)S(1)}, bf16[1024,384]{1,0:T(8,128)(2,1)S(1)}) custom-call(bf16[4,128,128]{2,1,0:T(8,128)(2,1)S(1)} %pad_maximum_fusion.refs_0_, bf16[512,512]{1,0:T(8,128)(2,1)S(1)} %get-tuple-element.43.refs_1_, bf16[128,512]{1,0:T(8,128)(2,1)S(1)} %get-tuple-element.44.refs_2_, ...), custom_call_target="tpu_custom_call" | custom-call | tf_op jit(solution)/shard_map/upgrad/pallas_call | solution.py:299
  21.8 1.9 %collective-permute-start.14 = (bf16[2,64,384]{2,1,0:T(8,128)(2,1)S(1)}, bf16[2,64,384]{2,1,0:T(8,128)(2,1)S(1)}, u32[]{:S(2)}, u32[]{:S(2)}) collective-permute-start(bf16[2,64,384]{2,1,0:T(8,128)(2,1)S(1)} %get-tuple-element.48), channel_id=1, source_target_pairs={{0,8},{4,12},{8,0},{12,4},{16,24},{20,28},{24,16},{28,20},{1,9},{5... | collective-permute-start | bytes 294920 | tf_op jit(solution)/shard_map/ppermute | solution.py:191
  23.7 1.5 %collective-permute-start.4 = (bf16[1,128,128]{2,1,0:T(8,128)(2,1)S(1)}, bf16[1,128,128]{2,1,0:T(8,128)(2,1)S(1)}, u32[]{:S(2)}, u32[]{:S(2)}) collective-permute-start(bf16[1,128,128]{2,1,0:T(8,128)(2,1)S(1)} %fusion.8), channel_id=1, source_target_pairs={{0,2},{1,3},{2,0},{3,1},{4,6},{5,7},{6,4},{7,5},{8,10},{9,11},{10,... | collective-permute-start | bytes 98312 | tf_op jit(solution)/shard_map/ppermute | solution.py:191
  25.3 9.4 %collective-permute-done.14 = bf16[2,64,384]{2,1,0:T(8,128)(2,1)S(1)} collective-permute-done((bf16[2,64,384]{2,1,0:T(8,128)(2,1)S(1)}, bf16[2,64,384]{2,1,0:T(8,128)(2,1)S(1)}, u32[]{:S(2)}, u32[]{:S(2)}) %collective-permute-start.14) | collective-permute-done | bytes 98336 | tf_op jit(solution)/shard_map/ppermute | solution.py:191
  35.2 3.7 %collective-permute-done.15.ups_b = bf16[64,384]{1,0:T(8,128)(2,1)S(1)} collective-permute-done((bf16[64,384]{1,0:T(8,128)(2,1)S(1)}, bf16[64,384]{1,0:T(8,128)(2,1)S(1)}, u32[]{:S(2)}, u32[]{:S(2)}) %collective-permute-start.15) | collective-permute-done | bytes 49184 | tf_op jit(solution)/shard_map/ppermute | solution.py:191
  39.8 0.7 %collective-permute-done.16 = bf16[4,64,128]{2,1,0:T(8,128)(2,1)S(1)} collective-permute-done((bf16[4,64,128]{2,1,0:T(8,128)(2,1)S(1)}, bf16[4,64,128]{2,1,0:T(8,128)(2,1)S(1)}, u32[]{:S(2)}, u32[]{:S(2)}) %collective-permute-start.16) | collective-permute-done | bytes 65568 | tf_op jit(solution)/shard_map/ppermute | solution.py:191
  40.6 1.6 %collective-permute-start.6 = (bf16[1,128,128]{2,1,0:T(8,128)(2,1)S(1)}, bf16[1,128,128]{2,1,0:T(8,128)(2,1)S(1)}, u32[]{:S(2)}, u32[]{:S(2)}) collective-permute-start(bf16[1,128,128]{2,1,0:T(8,128)(2,1)S(1)} %fusion.6.l0), channel_id=1, source_target_pairs={{0,8},{4,12},{8,0},{12,4},{16,24},{20,28},{24,16},{28,20},{1,9},{5... | collective-permute-start | bytes 98312 | tf_op jit(solution)/shard_map/ppermute | solution.py:191
  42.2 0.8 %collective-permute-start.7 = (bf16[1,128,128]{2,1,0:T(8,128)(2,1)S(1)}, bf16[1,128,128]{2,1,0:T(8,128)(2,1)S(1)}, u32[]{:S(2)}, u32[]{:S(2)}) collective-permute-start(bf16[1,128,128]{2,1,0:T(8,128)(2,1)S(1)} %fusion.6.l0), channel_id=1, source_target_pairs={{0,12},{4,8},{8,4},{12,0},{16,28},{20,24},{24,20},{28,16},{1,13},{... | collective-permute-start | bytes 98312 | tf_op jit(solution)/shard_map/ppermute | solution.py:191
  43.0 1.5 %collective-permute-start.17 = (bf16[2,64,128]{2,1,0:T(8,128)(2,1)S(1)}, bf16[2,64,128]{2,1,0:T(8,128)(2,1)S(1)}, u32[]{:S(2)}, u32[]{:S(2)}) collective-permute-start(bf16[2,64,128]{2,1,0:T(8,128)(2,1)S(1)} %fusion.10), channel_id=1, source_target_pairs={{0,2},{1,3},{2,0},{3,1},{4,6},{5,7},{6,4},{7,5},{8,10},{9,11},{10,... | collective-permute-start | bytes 98312 | tf_op jit(solution)/shard_map/ppermute | solution.py:191
  44.6 2.5 %collective-permute-done.7.l3 = bf16[1,128,128]{2,1,0:T(8,128)(2,1)S(1)} collective-permute-done((bf16[1,128,128]{2,1,0:T(8,128)(2,1)S(1)}, bf16[1,128,128]{2,1,0:T(8,128)(2,1)S(1)}, u32[]{:S(2)}, u32[]{:S(2)}) %collective-permute-start.7) | collective-permute-done | bytes 32800 | tf_op jit(solution)/shard_map/ppermute | solution.py:191
  47.6 1.3 %collective-permute-done.11 = bf16[4,128,128]{2,1,0:T(8,128)(2,1)S(1)} collective-permute-done((bf16[4,128,128]{2,1,0:T(8,128)(2,1)S(1)}, bf16[4,128,128]{2,1,0:T(8,128)(2,1)S(1)}, u32[]{:S(2)}, u32[]{:S(2)}) %collective-permute-start.11) | collective-permute-done | bytes 131104 | tf_op jit(solution)/shard_map/ppermute | solution.py:191
  49.0 1.5 %collective-permute-start.12 = (bf16[2,128,128]{2,1,0:T(8,128)(2,1)S(1)}, bf16[2,128,128]{2,1,0:T(8,128)(2,1)S(1)}, u32[]{:S(2)}, u32[]{:S(2)}) collective-permute-start(bf16[2,128,128]{2,1,0:T(8,128)(2,1)S(1)} %fusion.2), channel_id=1, source_target_pairs={{0,2},{1,3},{2,0},{3,1},{4,6},{5,7},{6,4},{7,5},{8,10},{9,11},{10,... | collective-permute-start | bytes 196616 | tf_op jit(solution)/shard_map/ppermute | solution.py:191
  50.5 2.8 %collective-permute-done.12 = bf16[2,128,128]{2,1,0:T(8,128)(2,1)S(1)} collective-permute-done((bf16[2,128,128]{2,1,0:T(8,128)(2,1)S(1)}, bf16[2,128,128]{2,1,0:T(8,128)(2,1)S(1)}, u32[]{:S(2)}, u32[]{:S(2)}) %collective-permute-start.12) | collective-permute-done | bytes 65568 | tf_op jit(solution)/shard_map/ppermute | solution.py:191
  53.4 2.6 %collective-permute-start.18 = (bf16[1,192,128]{2,1,0:T(8,128)(2,1)S(1)}, bf16[1,192,128]{2,1,0:T(8,128)(2,1)S(1)}, u32[]{:S(2)}, u32[]{:S(2)}) collective-permute-start(bf16[1,192,128]{2,1,0:T(8,128)(2,1)S(1)} %pad_maximum_fusion.3), channel_id=1, source_target_pairs={{0,16},{4,20},{8,24},{12,28},{16,0},{20,4},{24,8},{28,12},{1,17},{... | collective-permute-start | bytes 147464 | tf_op jit(solution)/shard_map/ppermute | solution.py:191
  56.0 2.8 %collective-permute-done.18.got = bf16[1,192,128]{2,1,0:T(8,128)(2,1)S(1)} collective-permute-done((bf16[1,192,128]{2,1,0:T(8,128)(2,1)S(1)}, bf16[1,192,128]{2,1,0:T(8,128)(2,1)S(1)}, u32[]{:S(2)}, u32[]{:S(2)}) %collective-permute-start.18) | collective-permute-done | bytes 49184 | tf_op jit(solution)/shard_map/ppermute | solution.py:191
  (44 shorter events, 4.4 us)
Async XLA Ops:
  1.9 3.2 %collective-permute-start = (bf16[128,768]{1,0:T(8,128)(2,1)S(1)}, bf16[128,768]{1,0:T(8,128)(2,1)S(1)}, u32[]{:S(2)}, u32[]{:S(2)}) collective-permute-start(bf16[128,768]{1,0:T(8,128)(2,1)S(1)} %get-tuple-element.29), channel_id=1, source_target_pairs={{0,1},{1,0},{2,3},{3,2},{4,5},{5,4},{6,7},{7,6},{8,9},{9,8},{10,11... | collective-permute-start | bytes 589832 | tf_op jit(solution)/shard_map/ppermute | solution.py:191
  2.5 7.6 %collective-permute-start.1 = (bf16[128,640]{1,0:T(8,128)(2,1)S(1)}, bf16[128,640]{1,0:T(8,128)(2,1)S(1)}, u32[]{:S(2)}, u32[]{:S(2)}) collective-permute-start(bf16[128,640]{1,0:T(8,128)(2,1)S(1)} %get-tuple-element.30), channel_id=1, source_target_pairs={{0,2},{1,3},{2,0},{3,1},{4,6},{5,7},{6,4},{7,5},{8,10},{9,11},{10,... | collective-permute-start | bytes 491528 | tf_op jit(solution)/shard_map/ppermute | solution.py:191
  5.0 8.1 %collective-permute-start.2 = (bf16[128,640]{1,0:T(8,128)(2,1)S(1)}, bf16[128,640]{1,0:T(8,128)(2,1)S(1)}, u32[]{:S(2)}, u32[]{:S(2)}) collective-permute-start(bf16[128,640]{1,0:T(8,128)(2,1)S(1)} %get-tuple-element.31), channel_id=1, source_target_pairs={{0,3},{1,2},{2,1},{3,0},{4,7},{5,6},{6,5},{7,4},{8,11},{9,10},{10,... | collective-permute-start | bytes 491528 | tf_op jit(solution)/shard_map/ppermute | solution.py:191
  5.1 15.8 %collective-permute-start.13 = (bf16[2,128,128]{2,1,0:T(8,128)(2,1)S(1)}, bf16[2,128,128]{2,1,0:T(8,128)(2,1)S(1)}, u32[]{:S(2)}, u32[]{:S(2)}) collective-permute-start(bf16[2,128,128]{2,1,0:T(8,128)(2,1)S(1)} %pad_maximum_fusion.2), channel_id=1, source_target_pairs={{0,2},{1,3},{2,0},{3,1},{4,6},{5,7},{6,4},{7,5},{8,10},{9,11},{10,... | collective-permute-start | bytes 196616 | tf_op jit(solution)/shard_map/ppermute | solution.py:191
  15.3 8.4 %collective-permute-start.3 = (f32[2,128,128]{2,1,0:T(8,128)S(1)}, f32[2,128,128]{2,1,0:T(8,128)S(1)}, u32[]{:S(2)}, u32[]{:S(2)}) collective-permute-start(f32[2,128,128]{2,1,0:T(8,128)S(1)} %get-tuple-element.36), channel_id=1, source_target_pairs={{0,1},{1,0},{2,3},{3,2},{4,5},{5,4},{6,7},{7,6},{8,9},{9,8},{10,11... | collective-permute-start | bytes 393224 | tf_op jit(solution)/shard_map/ppermute | solution.py:191
  17.1 25.1 %collective-permute-start.10 = (bf16[128,1024]{1,0:T(8,128)(2,1)S(1)}, bf16[128,1024]{1,0:T(8,128)(2,1)S(1)}, u32[]{:S(2)}, u32[]{:S(2)}) collective-permute-start(bf16[128,1024]{1,0:T(8,128)(2,1)S(1)} %get-tuple-element.40), channel_id=1, source_target_pairs={{0,12},{4,8},{8,4},{12,0},{16,28},{20,24},{24,20},{28,16},{1,13},{... | collective-permute-start | bytes 786440 | tf_op jit(solution)/shard_map/ppermute | solution.py:191
  20.3 22.8 %collective-permute-start.8 = (bf16[128,1024]{1,0:T(8,128)(2,1)S(1)}, bf16[128,1024]{1,0:T(8,128)(2,1)S(1)}, u32[]{:S(2)}, u32[]{:S(2)}) collective-permute-start(bf16[128,1024]{1,0:T(8,128)(2,1)S(1)} %get-tuple-element.38), channel_id=1, source_target_pairs={{0,4},{4,0},{8,12},{12,8},{16,20},{20,16},{24,28},{28,24},{1,5},{5... | collective-permute-start | bytes 786440 | tf_op jit(solution)/shard_map/ppermute | solution.py:191
  20.8 23.8 %collective-permute-start.9 = (bf16[128,1024]{1,0:T(8,128)(2,1)S(1)}, bf16[128,1024]{1,0:T(8,128)(2,1)S(1)}, u32[]{:S(2)}, u32[]{:S(2)}) collective-permute-start(bf16[128,1024]{1,0:T(8,128)(2,1)S(1)} %get-tuple-element.39), channel_id=1, source_target_pairs={{0,8},{4,12},{8,0},{12,4},{16,24},{20,28},{24,16},{28,20},{1,9},{5... | collective-permute-start | bytes 786440 | tf_op jit(solution)/shard_map/ppermute | solution.py:191
  21.8 12.9 %collective-permute-start.14 = (bf16[2,64,384]{2,1,0:T(8,128)(2,1)S(1)}, bf16[2,64,384]{2,1,0:T(8,128)(2,1)S(1)}, u32[]{:S(2)}, u32[]{:S(2)}) collective-permute-start(bf16[2,64,384]{2,1,0:T(8,128)(2,1)S(1)} %get-tuple-element.48), channel_id=1, source_target_pairs={{0,8},{4,12},{8,0},{12,4},{16,24},{20,28},{24,16},{28,20},{1,9},{5... | collective-permute-start | bytes 294920 | tf_op jit(solution)/shard_map/ppermute | solution.py:191
  23.7 15.6 %collective-permute-start.4 = (bf16[1,128,128]{2,1,0:T(8,128)(2,1)S(1)}, bf16[1,128,128]{2,1,0:T(8,128)(2,1)S(1)}, u32[]{:S(2)}, u32[]{:S(2)}) collective-permute-start(bf16[1,128,128]{2,1,0:T(8,128)(2,1)S(1)} %fusion.8), channel_id=1, source_target_pairs={{0,2},{1,3},{2,0},{3,1},{4,6},{5,7},{6,4},{7,5},{8,10},{9,11},{10,... | collective-permute-start | bytes 98312 | tf_op jit(solution)/shard_map/ppermute | solution.py:191
  34.7 4.2 %collective-permute-start.15 = (bf16[64,384]{1,0:T(8,128)(2,1)S(1)}, bf16[64,384]{1,0:T(8,128)(2,1)S(1)}, u32[]{:S(2)}, u32[]{:S(2)}) collective-permute-start(bf16[64,384]{1,0:T(8,128)(2,1)S(1)} %fusion.7), channel_id=1, source_target_pairs={{0,4},{4,0},{8,12},{12,8},{16,20},{20,16},{24,28},{28,24},{1,5},{5... | collective-permute-start | bytes 147464 | tf_op jit(solution)/shard_map/ppermute | solution.py:191
  39.3 1.3 %collective-permute-start.16 = (bf16[4,64,128]{2,1,0:T(8,128)(2,1)S(1)}, bf16[4,64,128]{2,1,0:T(8,128)(2,1)S(1)}, u32[]{:S(2)}, u32[]{:S(2)}) collective-permute-start(bf16[4,64,128]{2,1,0:T(8,128)(2,1)S(1)} %get-tuple-element.51), channel_id=1, source_target_pairs={{0,1},{1,0},{2,3},{3,2},{4,5},{5,4},{6,7},{7,6},{8,9},{9,8},{10,11... | collective-permute-start | bytes 196616 | tf_op jit(solution)/shard_map/ppermute | solution.py:191
  39.4 5.2 %collective-permute-start.5 = (bf16[1,128,128]{2,1,0:T(8,128)(2,1)S(1)}, bf16[1,128,128]{2,1,0:T(8,128)(2,1)S(1)}, u32[]{:S(2)}, u32[]{:S(2)}) collective-permute-start(bf16[1,128,128]{2,1,0:T(8,128)(2,1)S(1)} %fusion.6.l0), channel_id=1, source_target_pairs={{0,4},{4,0},{8,12},{12,8},{16,20},{20,16},{24,28},{28,24},{1,5},{5... | collective-permute-start | bytes 98312 | tf_op jit(solution)/shard_map/ppermute | solution.py:191
  40.6 4.0 %collective-permute-start.6 = (bf16[1,128,128]{2,1,0:T(8,128)(2,1)S(1)}, bf16[1,128,128]{2,1,0:T(8,128)(2,1)S(1)}, u32[]{:S(2)}, u32[]{:S(2)}) collective-permute-start(bf16[1,128,128]{2,1,0:T(8,128)(2,1)S(1)} %fusion.6.l0), channel_id=1, source_target_pairs={{0,8},{4,12},{8,0},{12,4},{16,24},{20,28},{24,16},{28,20},{1,9},{5... | collective-permute-start | bytes 98312 | tf_op jit(solution)/shard_map/ppermute | solution.py:191
  42.2 4.9 %collective-permute-start.7 = (bf16[1,128,128]{2,1,0:T(8,128)(2,1)S(1)}, bf16[1,128,128]{2,1,0:T(8,128)(2,1)S(1)}, u32[]{:S(2)}, u32[]{:S(2)}) collective-permute-start(bf16[1,128,128]{2,1,0:T(8,128)(2,1)S(1)} %fusion.6.l0), channel_id=1, source_target_pairs={{0,12},{4,8},{8,4},{12,0},{16,28},{20,24},{24,20},{28,16},{1,13},{... | collective-permute-start | bytes 98312 | tf_op jit(solution)/shard_map/ppermute | solution.py:191
  43.0 4.5 %collective-permute-start.17 = (bf16[2,64,128]{2,1,0:T(8,128)(2,1)S(1)}, bf16[2,64,128]{2,1,0:T(8,128)(2,1)S(1)}, u32[]{:S(2)}, u32[]{:S(2)}) collective-permute-start(bf16[2,64,128]{2,1,0:T(8,128)(2,1)S(1)} %fusion.10), channel_id=1, source_target_pairs={{0,2},{1,3},{2,0},{3,1},{4,6},{5,7},{6,4},{7,5},{8,10},{9,11},{10,... | collective-permute-start | bytes 98312 | tf_op jit(solution)/shard_map/ppermute | solution.py:191
  47.5 1.4 %collective-permute-start.11 = (bf16[4,128,128]{2,1,0:T(8,128)(2,1)S(1)}, bf16[4,128,128]{2,1,0:T(8,128)(2,1)S(1)}, u32[]{:S(2)}, u32[]{:S(2)}) collective-permute-start(bf16[4,128,128]{2,1,0:T(8,128)(2,1)S(1)} %get-tuple-element.42), channel_id=1, source_target_pairs={{0,1},{1,0},{2,3},{3,2},{4,5},{5,4},{6,7},{7,6},{8,9},{9,8},{10,11... | collective-permute-start | bytes 393224 | tf_op jit(solution)/shard_map/ppermute | solution.py:191
  49.0 4.3 %collective-permute-start.12 = (bf16[2,128,128]{2,1,0:T(8,128)(2,1)S(1)}, bf16[2,128,128]{2,1,0:T(8,128)(2,1)S(1)}, u32[]{:S(2)}, u32[]{:S(2)}) collective-permute-start(bf16[2,128,128]{2,1,0:T(8,128)(2,1)S(1)} %fusion.2), channel_id=1, source_target_pairs={{0,2},{1,3},{2,0},{3,1},{4,6},{5,7},{6,4},{7,5},{8,10},{9,11},{10,... | collective-permute-start | bytes 196616 | tf_op jit(solution)/shard_map/ppermute | solution.py:191
  53.4 5.5 %collective-permute-start.18 = (bf16[1,192,128]{2,1,0:T(8,128)(2,1)S(1)}, bf16[1,192,128]{2,1,0:T(8,128)(2,1)S(1)}, u32[]{:S(2)}, u32[]{:S(2)}) collective-permute-start(bf16[1,192,128]{2,1,0:T(8,128)(2,1)S(1)} %pad_maximum_fusion.3), channel_id=1, source_target_pairs={{0,16},{4,20},{8,24},{12,28},{16,0},{20,4},{24,8},{28,12},{1,17},{... | collective-permute-start | bytes 147464 | tf_op jit(solution)/shard_map/ppermute | solution.py:191
